TPU v7x, 512 devices: a whole 4x8x8 slice. The times are simulated.
512 devices in a mesh: hyp: 8 (over x, core), rows: 64 (over z, y).
Axes of the slice: x: 4, y: 8, z: 8, core: 2. Of those that a mesh axis runs over, the one named last changes fastest.
Arguments:
- offsets: float32 [2, 262144], P(None, 'rows'), may hold values from 0 to 1
- tile_cell: int32 [2048], P('rows'), may hold values from 0 to 31, as said below
- probes: int32 [8, 262144], P(None, 'rows'), may hold values from 0 to 1
- target: float32 [262144], P('rows'), may hold values from -6 to 6
- lengthscale: float32 [8], P('hyp'), parts along dimension 0, may hold values from 0.5 to 1
- amplitude: float32 [8], P('hyp'), parts along dimension 0, may hold values from 0.02 to 0.08
- noise: float32 [8], P('hyp'), parts along dimension 0, may hold values from 0.1 to 0.4
Outputs:
- solutions: float32 [72, 262144], P('hyp', 'rows'), parts along dimension 0
- quadratic: float32 [72], P('hyp'), parts along dimension 0
There are 8 independent parts, one for each index of `hyp`. A program takes and returns all parts, laid end to end along the dimension named above; an argument that names none is the same for every part. Nothing has to cross between parts.
Inputs may be any that keep to these rules, and one draw needn't show every extreme that they name: `tile_cell`: each aligned block of 32 entries (one device's tiles) is a permutation of 0 to 31.
All inputs are finite; a program needn't handle non-finite values.
Results may differ from a plain program's by a relative error of at most 0.0003.
Values sent between devices are 32-bit elements; how exact they have to be, the bound alone decides.
No kernel may reach another device: no remote copies, remote signals or barrier semaphores. Data moves between devices by JAX's collectives and lax.ppermute only.
A program may use at most 64 MiB of HBM per device.

v0:
```python
import jax
import jax.numpy as jnp
from jax import lax
from jax.experimental import pallas as pl
from jax.experimental.pallas import tpu as pltpu
from jax.sharding import PartitionSpec as P

TILE = 128
GX = 16
RHS = 9
ROWS = 16
WIDE = GX * TILE
FEATURES = 32
PAD = GX + 2
BAND = 3 * 2 * TILE
F32 = jnp.float32
BF16 = jnp.bfloat16
TINY = 1e-30

VMEM = pl.BlockSpec(memory_space=pltpu.VMEM)
SMEM = pl.BlockSpec(memory_space=pltpu.SMEM)


def call(kernel, name, out_shape, in_specs, scratch=(), flops=0, limit=12):
    return pl.pallas_call(
        kernel,
        name=name,
        out_shape=out_shape,
        in_specs=in_specs,
        out_specs=jax.tree.map(lambda _: VMEM, out_shape),
        scratch_shapes=list(scratch),
        cost_estimate=pl.CostEstimate(flops=flops, bytes_accessed=1 << 20, transcendentals=0),
        compiler_params=pltpu.CompilerParams(vmem_limit_bytes=limit << 20),
    )


def grid_row(dtype=F32):
    return jax.ShapeDtypeStruct((ROWS, WIDE), dtype)


def lanes(tile, width=TILE):
    return pl.ds(pl.multiple_of(tile * width, width), width)


def pack_kernel(cell_ref, offsets_ref, probes_ref, target_ref, first_ref, second_ref):
    filler = jnp.zeros((ROWS - RHS - 2, TILE), F32)
    for s in range(cell_ref.shape[0]):
        here = slice(s * TILE, (s + 1) * TILE)
        signs = 2.0 * probes_ref[:, here].astype(F32) - 1.0
        rest = jnp.concatenate([target_ref[:, here], offsets_ref[:, here], filler], axis=0)
        cell = cell_ref[s]

        def put(ref, column, signs=signs, rest=rest):
            ref[0:8, lanes(column)] = signs
            ref[8:16, lanes(column)] = rest

        @pl.when(cell < GX)
        def _():
            put(first_ref, cell)

        @pl.when(cell >= GX)
        def _():
            put(second_ref, cell - GX)


def constants(scale_ref, amp_ref):
    amp = jnp.full((1, TILE), amp_ref[0], F32)
    reach = jnp.exp(0.2 * jnp.log(4.0 * amp))
    square = reach * reach
    top = 5.0 * amp / (square * square)
    factor = reach / jnp.full((1, TILE), scale_ref[0], F32)
    return reach, top, factor


def split_rows(values, level):
    first = values.astype(BF16).astype(F32)
    rest = values - first
    second = rest.astype(BF16).astype(F32)
    third = rest - second
    return jnp.where(level == 0, first, jnp.where(level == 1, second, third))


def feature_rows():
    row = lax.broadcasted_iota(jnp.int32, (FEATURES, TILE), 0)

    def level(order):
        out = jnp.zeros_like(row)
        for k, v in enumerate(order):
            if v:
                out = jnp.where(row == k, v, out)
        return out

    source = level([0, 0, 1, 1, 0, 2] * 2 + [0, 1, 2] + [0, 0, 0])
    target = level([0, 1, 0, 1, 2, 0] * 2 + [0, 0, 0] + [0, 1, 2])
    kind = jnp.where(row < 6, 0, jnp.where(row < 12, 1, jnp.where(row < 15, 2, jnp.where(row < 18, 3, 4))))
    return kind, source, target


def choose(kind, a, b, c, d):
    return jnp.where(
        kind == 0, a, jnp.where(kind == 1, b, jnp.where(kind == 2, c, jnp.where(kind == 3, d, 0.0)))
    )


def source_features(row_ref, factor, rows, out_ref, slot):
    kind, source, _ = rows
    zero = jnp.zeros((TILE, FEATURES), BF16)
    out_ref[slot, 0] = zero
    out_ref[slot, PAD - 1] = zero

    def one(tile, carry):
        a = factor * (row_ref[9:10, lanes(tile)] - 0.5)
        b = factor * (row_ref[10:11, lanes(tile)] - 0.5)
        values = choose(kind, a, b, a * a + b * b, 1.0)
        out_ref[slot, tile + 1] = split_rows(values, source).T.astype(BF16)
        return carry

    lax.fori_loop(0, GX, one, 0, unroll=2)


def target_features(row_ref, tile, row_shift, col_shift, factor, rows):
    kind, _, target = rows
    a = factor * ((row_shift + 0.5) - row_ref[9:10, lanes(tile)])
    b = factor * ((col_shift + 0.5) - row_ref[10:11, lanes(tile)])
    values = choose(kind, 2.0 * a, 2.0 * b, 1.0, a * a + b * b)
    return split_rows(values, target).astype(BF16)


def fill_weights(target_ref, row_shift, feats_ref, slot, weights_ref, combo, consts, rows):
    reach, top, factor = consts
    reach = jnp.broadcast_to(reach, (16, TILE))
    top = jnp.broadcast_to(top, (16, TILE))

    def one(tile, carry):
        for k in range(3):
            wanted = target_features(target_ref, tile, float(row_shift), float(k - 1), factor, rows)
            square = lax.dot_general(
                feats_ref[slot, tile + k],
                wanted,
                (((1,), (0,)), ((), ())),
                preferred_element_type=F32,
            )
            for part in range(TILE // 16):
                here = jnp.maximum(square[part * 16 : (part + 1) * 16, :], 1e-12)
                close = jnp.maximum(reach - here * lax.rsqrt(here), 0.0)
                second = close * close
                weight = (second * second) * (top - close)
                high = weight.astype(BF16)
                low = (weight - high.astype(F32)).astype(BF16)
                base = k * 2 * TILE + part * 16
                weights_ref[combo, tile, base : base + 16, :] = high
                weights_ref[combo, tile, base + TILE : base + TILE + 16, :] = low
        return carry

    lax.fori_loop(0, GX, one, 0, unroll=2)


def spread(row_ref, out_ref, slot):
    empty = jnp.zeros((2 * ROWS, 2 * TILE), BF16)
    out_ref[slot, :, 0 : 2 * TILE] = empty
    out_ref[slot, :, (PAD - 1) * 2 * TILE :] = empty
    for tile in range(GX):
        values = row_ref[:, tile * TILE : (tile + 1) * TILE]
        high = values.astype(BF16)
        low = (values - high.astype(F32)).astype(BF16)
        both = jnp.concatenate([high, low], axis=0)
        at = (tile + 1) * 2 * TILE
        out_ref[slot, :, at : at + TILE] = both
        out_ref[slot, :, at + TILE : at + 2 * TILE] = both


def banded(spread_ref, slot, weights_ref, combo, tile):
    at = pl.multiple_of(tile * 2 * TILE, 2 * TILE)
    both = jnp.dot(
        spread_ref[slot, :, pl.ds(at, BAND)],
        weights_ref[combo, tile],
        preferred_element_type=F32,
    )
    return both[0:ROWS] + both[ROWS:]


GROUP = 4


def apply_rows(first_ref, second_ref, spread_ref, inner_ref, outer_ref, noise, out_refs):
    def group(g, carry):
        for j in range(GROUP):
            tile = g * GROUP + j
            here = lanes(tile)
            out_refs[0][:, here] = (
                noise * first_ref[:, here]
                + banded(spread_ref, 0, outer_ref, 0, tile)
                + banded(spread_ref, 1, inner_ref, 0, tile)
                + banded(spread_ref, 2, inner_ref, 1, tile)
            )
            out_refs[1][:, here] = (
                noise * second_ref[:, here]
                + banded(spread_ref, 1, inner_ref, 2, tile)
                + banded(spread_ref, 2, inner_ref, 3, tile)
                + banded(spread_ref, 3, outer_ref, 1, tile)
            )
        return carry

    lax.fori_loop(0, GX // GROUP, group, 0)


def two_sum(a, b):
    total = a + b
    part = total - a
    return total, (a - (total - part)) + (b - part)


def quick_sum(a, b):
    total = a + b
    return total, b - (total - a)


def halves(a):
    scaled = 4097.0 * a
    high = scaled - (scaled - a)
    return high, a - high


def two_product(a, b, a_halves=None, b_halves=None):
    a1, a2 = halves(a) if a_halves is None else a_halves
    b1, b2 = halves(b) if b_halves is None else b_halves
    product = a * b
    return product, ((a1 * b1 - product) + a1 * b2 + a2 * b1) + a2 * b2


class Pair:
    def __init__(self, high, low):
        self.high, self.low = high, low

    def __add__(self, other):
        total, error = two_sum(self.high, other.high)
        return Pair(*quick_sum(total, error + (self.low + other.low)))

    def __neg__(self):
        return Pair(-self.high, -self.low)

    def __sub__(self, other):
        return self + (-other)

    def __mul__(self, other):
        if not isinstance(other, Pair):
            return Pair(self.high * other, self.low * other)
        product, error = two_product(self.high, other.high)
        return Pair(*quick_sum(product, error + (self.high * other.low + self.low * other.high)))

    def __truediv__(self, other):
        first = self.high / other.high
        rest = self - other * Pair(first, jnp.zeros_like(first))
        return Pair(*quick_sum(first, rest.high / other.high))

    def where(self, keep, other):
        return Pair(jnp.where(keep, self.high, other.high), jnp.where(keep, self.low, other.low))


def grid_mask(k):
    lane = lax.broadcasted_iota(jnp.int32, (ROWS, TILE), 1)
    row = lax.broadcasted_iota(jnp.int32, (ROWS, TILE), 0)
    return lane == row + ROWS * k


def add_product(sums, a, b, a_halves, b_halves):
    product, error = two_product(a, b, a_halves, b_halves)
    total, left = two_sum(sums[0], product)
    return total, sums[1] + (left + error)


def lines(sums, first):
    placed = [jnp.zeros((ROWS, TILE), F32), jnp.zeros((ROWS, TILE), F32)]
    for k, (high, low) in enumerate(sums):
        for shift in (64, 32, 16, 8, 4, 2, 1):
            high, left = two_sum(high, pltpu.roll(high, shift, 1))
            low = (low + pltpu.roll(low, shift, 1)) + left
        high, low = quick_sum(high, low)
        mask = grid_mask(first + k)
        placed = [jnp.where(mask, high, placed[0]), jnp.where(mask, low, placed[1])]
    return [jnp.sum(p, axis=0, keepdims=True) for p in placed]


def inner_kernel(scale_ref, amp_ref, first_ref, second_ref, inner_ref, feats_ref):
    rows = feature_rows()
    consts = constants(scale_ref, amp_ref)
    source_features(first_ref, consts[2], rows, feats_ref, 0)
    source_features(second_ref, consts[2], rows, feats_ref, 1)
    fill_weights(first_ref, 0, feats_ref, 0, inner_ref, 0, consts, rows)
    fill_weights(first_ref, 1, feats_ref, 1, inner_ref, 1, consts, rows)
    fill_weights(second_ref, -1, feats_ref, 0, inner_ref, 2, consts, rows)
    fill_weights(second_ref, 0, feats_ref, 1, inner_ref, 3, consts, rows)


def outer_kernel(
    scale_ref,
    amp_ref,
    noise_ref,
    above_ref,
    first_ref,
    second_ref,
    below_ref,
    inner_ref,
    outer_ref,
    one_ref,
    two_ref,
    feats_ref,
    spread_ref,
):
    rows = feature_rows()
    consts = constants(scale_ref, amp_ref)
    source_features(above_ref, consts[2], rows, feats_ref, 0)
    source_features(below_ref, consts[2], rows, feats_ref, 1)
    fill_weights(first_ref, -1, feats_ref, 0, outer_ref, 0, consts, rows)
    fill_weights(second_ref, 1, feats_ref, 1, outer_ref, 1, consts, rows)
    for slot, ref in enumerate((above_ref, first_ref, second_ref, below_ref)):
        spread(ref, spread_ref, slot)
    apply_rows(
        first_ref, second_ref, spread_ref, inner_ref, outer_ref, noise_ref[0], (one_ref, two_ref)
    )


def product_kernel(
    noise_ref, above_ref, first_ref, second_ref, below_ref, inner_ref, outer_ref, one_ref, two_ref, spread_ref
):
    for slot, ref in enumerate((above_ref, first_ref, second_ref, below_ref)):
        spread(ref, spread_ref, slot)
    apply_rows(
        first_ref, second_ref, spread_ref, inner_ref, outer_ref, noise_ref[0], (one_ref, two_ref)
    )


def gram_kernel(b0_ref, b1_ref, f0_ref, f1_ref, g0_ref, g1_ref, sums_ref):
    zero = jnp.zeros((ROWS, TILE), F32)

    def one(tile, sums):
        sums = list(sums)
        here = lanes(tile)
        for refs in ((b0_ref, f0_ref, g0_ref), (b1_ref, f1_ref, g1_ref)):
            values = [ref[:, here] for ref in refs]
            parts = [halves(v) for v in values]
            for k, (i, j) in enumerate(((0, 0), (0, 1), (0, 2), (1, 1), (1, 2), (2, 2))):
                sums[k] = add_product(sums[k], values[i], values[j], parts[i], parts[j])
        return tuple(sums)

    high, low = lines(lax.fori_loop(0, GX, one, ((zero, zero),) * 6), 0)
    sums_ref[0:1, :] = high
    sums_ref[1:2, :] = low


def moment_kernel(
    noise_ref, sums_ref, g0_ref, g1_ref, below_ref, inner_ref, outer_ref, out_ref, spread_ref
):
    spread(g0_ref, spread_ref, 0)
    spread(g1_ref, spread_ref, 1)
    spread(below_ref, spread_ref, 2)
    noise = noise_ref[0]

    def group(g, sums):
        for j in range(GROUP):
            tile = g * GROUP + j
            here = lanes(tile)
            own0 = banded(spread_ref, 0, inner_ref, 0, tile)
            next0 = banded(spread_ref, 1, inner_ref, 1, tile)
            own1 = banded(spread_ref, 1, inner_ref, 3, tile)
            next1 = banded(spread_ref, 2, outer_ref, 1, tile)
            for ref, own, after in ((g0_ref, own0, next0), (g1_ref, own1, next1)):
                v = ref[:, here]
                image = noise * v + own + 2.0 * after
                sums = add_product(sums, v, image, halves(v), halves(image))
        return sums

    zero = jnp.zeros((ROWS, TILE), F32)
    high, low = lines((lax.fori_loop(0, GX // GROUP, group, (zero, zero)),), 6)
    both = jnp.concatenate([high + sums_ref[0:1, :], low + sums_ref[1:2, :]], axis=0)
    out_ref[...] = jnp.broadcast_to(both[None], out_ref.shape)


def finish_kernel(
    points,
    cell_ref,
    noise_ref,
    parts_ref,
    b0_ref,
    b1_ref,
    f0_ref,
    f1_ref,
    g0_ref,
    g1_ref,
    out_ref,
    quad_ref,
    grid_ref,
):
    high, low = parts_ref[:, 0, :], parts_ref[:, 1, :]
    while high.shape[0] > 8:
        half = high.shape[0] // 2
        high, left = two_sum(high[:half], high[half:])
        low = (low[:half] + low[half:]) + left
    for shift in (4, 2, 1):
        high, left = two_sum(high, pltpu.roll(high, shift, 0))
        low = (low + pltpu.roll(low, shift, 0)) + left
    high, low = quick_sum(high, low)
    bb, bf, bg, ff, fg, gg, gag = (
        Pair(high, low)
        if k == 0
        else Pair(pltpu.roll(high, TILE - ROWS * k, 1), pltpu.roll(low, TILE - ROWS * k, 1))
        for k in range(7)
    )
    zero = jnp.zeros_like(high)
    none = Pair(zero, zero)
    one = Pair(zero + 1.0, zero)
    most = 1.0 / jnp.full(high.shape, noise_ref[0], F32)

    floor = bb.high * 1e-11

    def step(square, product):
        good = (square.high > floor) & (product.high > 0.0)
        ratio = square / product.where(good, one)
        fits = ratio.high < most
        return ratio.where(fits, Pair(most, zero)).where(good, none), good

    def over(a, b, good):
        return (a / b.where(good, one)).where(good, none)

    alpha0, good0 = step(bb, bf)
    rr1 = bb - alpha0 * (bf * 2.0 - alpha0 * ff)
    beta0 = over(rr1, bb, good0)
    p0, p1 = one + beta0, -alpha0
    alpha1, good1 = step(rr1, p0 * (p0 * bf + p1 * (bg + ff)) + p1 * p1 * fg)
    r1, r2 = -(alpha0 + alpha1 * p0), -(alpha1 * p1)
    rr2 = bb + r1 * (bf * 2.0 + r1 * ff) + r2 * (bg * 2.0 + r1 * fg * 2.0 + r2 * gg)
    beta1 = over(rr2, rr1, good1)
    q0, q1, q2 = one + beta1 * p0, r1 + beta1 * p1, r2
    alpha2, good2 = step(
        rr2,
        q0 * (q0 * bf + q1 * (bg + ff) + q2 * fg * 2.0)
        + q1 * (q1 * fg + q2 * gg * 2.0)
        + q2 * q2 * gag,
    )
    alpha2 = alpha2.where(good1, none)
    on_b = alpha0 + alpha1 * p0 + alpha2 * q0
    on_f = alpha1 * p1 + alpha2 * q1
    on_g = alpha2 * q2
    quad = on_b * bb + on_f * bf + on_g * bg
    quad_ref[...] = (quad.high / points)[0:1, 0:RHS]
    mask = grid_mask(0)
    c0, c1, c2 = (
        jnp.broadcast_to(
            jnp.sum(
                jnp.where(mask, jnp.concatenate([c.high, c.high], axis=0), 0.0), axis=1, keepdims=True
            ),
            (ROWS, TILE),
        )
        for c in (on_b, on_f, on_g)
    )
    for half, (b_ref, f_ref, g_ref) in enumerate(
        ((b0_ref, f0_ref, g0_ref), (b1_ref, f1_ref, g1_ref))
    ):
        for tile in range(GX):
            here = slice(tile * TILE, (tile + 1) * TILE)
            grid_ref[half * GX + tile] = (
                c0 * b_ref[:, here] + c1 * f_ref[:, here] + c2 * g_ref[:, here]
            )
    for s in range(cell_ref.shape[0]):
        out_ref[:, s * TILE : (s + 1) * TILE] = grid_ref[cell_ref[s], 0:RHS, :]


def shards(offsets, tile_cell, probes, target, lengthscale, amplitude, noise):
    size = lax.axis_size("rows")
    points = size * tile_cell.shape[0] * TILE
    down = [(i, i + 1) for i in range(size - 1)]
    up = [(i + 1, i) for i in range(size - 1)]

    first, second = call(
        pack_kernel, "pack", (grid_row(), grid_row()), [SMEM, VMEM, VMEM, VMEM], flops=1 << 20
    )(tile_cell, offsets, probes, target.reshape(1, -1))
    above = lax.ppermute(second, "rows", down)
    below = lax.ppermute(first, "rows", up)
    feats = pltpu.VMEM((2, PAD, TILE, FEATURES), BF16)
    inner = call(
        inner_kernel,
        "inner",
        pltpu.VMEM((4, GX, BAND, TILE), BF16),
        [SMEM, SMEM, VMEM, VMEM],
        [feats],
        flops=1 << 30,
    )(lengthscale, amplitude, first, second)
    spread4 = pltpu.VMEM((4, 2 * ROWS, PAD * 2 * TILE), BF16)
    outer, f0, f1 = call(
        outer_kernel,
        "outer",
        (pltpu.VMEM((2, GX, BAND, TILE), BF16), grid_row(), grid_row()),
        [SMEM, SMEM, SMEM, VMEM, VMEM, VMEM, VMEM, VMEM],
        [feats, spread4],
        flops=1 << 30,
    )(lengthscale, amplitude, noise, above, first, second, below, inner)
    f_above = lax.ppermute(f1, "rows", down)
    f_below = lax.ppermute(f0, "rows", up)
    g0, g1 = call(
        product_kernel,
        "product",
        (grid_row(), grid_row()),
        [SMEM] + [VMEM] * 6,
        [spread4],
        flops=1 << 30,
    )(noise, f_above, f0, f1, f_below, inner, outer)
    g_below = lax.ppermute(g0, "rows", up)
    sums = call(
        gram_kernel, "gram", jax.ShapeDtypeStruct((2, TILE), F32), [VMEM] * 6, flops=1 << 28
    )(first, second, f0, f1, g0, g1)
    parts = call(
        moment_kernel,
        "moment",
        jax.ShapeDtypeStruct((size, 2, TILE), F32),
        [SMEM] + [VMEM] * 6,
        [pltpu.VMEM((3, 2 * ROWS, PAD * 2 * TILE), BF16)],
        flops=1 << 29,
    )(noise, sums, g0, g1, g_below, inner, outer)
    parts = lax.all_to_all(parts, "rows", split_axis=0, concat_axis=0, tiled=True)

    def finish(*refs):
        finish_kernel(float(points), *refs)

    solutions, quad = call(
        finish,
        "finish",
        (
            jax.ShapeDtypeStruct((RHS, tile_cell.shape[0] * TILE), F32),
            jax.ShapeDtypeStruct((1, RHS), F32),
        ),
        [SMEM, SMEM] + [VMEM] * 7,
        [pltpu.VMEM((tile_cell.shape[0], ROWS, TILE), F32)],
        flops=1 << 20,
    )(tile_cell, noise, parts, first, second, f0, f1, g0, g1)
    return (solutions, quad.reshape(RHS))


def solution(mesh):
    return jax.shard_map(
        shards,
        mesh=mesh,
        in_specs=(
            P(None, "rows"),
            P("rows"),
            P(None, "rows"),
            P("rows"),
            P("hyp"),
            P("hyp"),
            P("hyp"),
        ),
        out_specs=(P("hyp", "rows"), P("hyp")),
        check_vma=False,
    )
```

profile of v0, /device:TPU:2, one launch (start us, length us, event | category | flops | bytes accessed | tf_op | source)
XLA Modules:
  0.0 92.4 jit_solution(15461336622569883569)
XLA Ops:
  0.6 0.0 copy-start
  0.6 0.9 copy-done
  1.5 0.0 copy-start.1
  1.5 0.8 copy-done.1
  2.3 0.0 copy-start.2
  2.3 0.7 copy-done.2
  3.0 0.0 copy-start.3
  3.0 0.7 copy-done.3
  3.7 1.0 %pack.1 = (f32[16,2048]{1,0:T(8,128)S(1)}, f32[16,2048]{1,0:T(8,128)S(1)}) custom-call(s32[32]{0:T(128)S(1)} %copy-done.3, f32[2,4096]{1,0:T(2,128)S(1)} %copy-done.1, s32[8,4096]{1,0:T(8,128)S(1)} %copy-done, f32[1,4096]{1,0:T(1,128)S(1)} %bitcast.2), custom_call_target="tpu_custom_call" | custom-call | flops 1048576 | bytes 1048576 | tf_op jit(solution)/shard_map/pack/pallas_call | solution.py:474
  4.6 1.3 %collective-permute-start.1 = (f32[16,2048]{1,0:T(8,128)S(1)}, f32[16,2048]{1,0:T(8,128)S(1)}, u32[]{:S(2)}, u32[]{:S(2)}) collective-permute-start(f32[16,2048]{1,0:T(8,128)S(1)} %get-tuple-element.11.first_ref.b0_ref.refs_3_), channel_id=1, source_target_pairs={{1,0},{2,1},{3,2},{4,3},{5,4},{6,5},{7,6},{8,7},{9,8},{10,9},{11,1... | collective-permute-start | bytes 393224 | tf_op jit(solution)/shard_map/ppermute | solution.py:478
  5.9 4.6 %collective-permute-start = (f32[16,2048]{1,0:T(8,128)S(1)}, f32[16,2048]{1,0:T(8,128)S(1)}, u32[]{:S(2)}, u32[]{:S(2)}) collective-permute-start(f32[16,2048]{1,0:T(8,128)S(1)} %get-tuple-element.12.second_ref.b1_ref.refs_4_), channel_id=1, source_target_pairs={{0,1},{1,2},{2,3},{3,4},{4,5},{5,6},{6,7},{7,8},{8,9},{9,10},{10,1... | collective-permute-start | bytes 393224 | tf_op jit(solution)/shard_map/ppermute | solution.py:477
  12.4 12.2 %inner.1.inner_ref = bf16[4,16,768,128]{3,2,1,0:T(8,128)(2,1)S(1)} custom-call(f32[1]{0:T(128)S(6)} %copy.9.scale_ref, f32[1]{0:T(128)S(6)} %copy.10.amp_ref, f32[16,2048]{1,0:T(8,128)S(1)} %get-tuple-element.11.first_ref.b0_ref.refs_3_, f32[16,2048]{1,0:T(8,128)S(1)} %get-tuple-element.12.second_ref.b1_ref.refs_4_), custom_call_target="tpu_custom_call" | custom-call | flops 1073741824 | bytes 1048576 | tf_op jit(solution)/shard_map/inner/pallas_call | solution.py:480
  24.6 0.0 collective-permute-done.1.below_ref
  24.6 0.0 collective-permute-done.above_ref
  24.6 10.5 %outer.1 = (bf16[2,16,768,128]{3,2,1,0:T(8,128)(2,1)S(1)}, f32[16,2048]{1,0:T(8,128)S(1)}, f32[16,2048]{1,0:T(8,128)S(1)}) custom-call(f32[1]{0:T(128)S(6)} %copy.9.scale_ref, f32[1]{0:T(128)S(6)} %copy.10.amp_ref, f32[1]{0:T(128)S(6)} %copy.11.noise_ref.refs_1_, f32[16,2048]{1,0:T(8,128)S(1)} %collective-permute-done.above_ref, ...), custom_call_target="tpu_custom_call" | custom-call | flops 1073741824 | bytes 1048576 | tf_op jit(solution)/shard_map/outer/pallas_call | solution.py:489
  35.1 1.3 %collective-permute-start.3 = (f32[16,2048]{1,0:T(8,128)S(1)}, f32[16,2048]{1,0:T(8,128)S(1)}, u32[]{:S(2)}, u32[]{:S(2)}) collective-permute-start(f32[16,2048]{1,0:T(8,128)S(1)} %get-tuple-element.13.first_ref.f0_ref.refs_5_), channel_id=1, source_target_pairs={{1,0},{2,1},{3,2},{4,3},{5,4},{6,5},{7,6},{8,7},{9,8},{10,9},{11,1... | collective-permute-start | bytes 393224 | tf_op jit(solution)/shard_map/ppermute | solution.py:498
  36.4 4.6 %collective-permute-start.2 = (f32[16,2048]{1,0:T(8,128)S(1)}, f32[16,2048]{1,0:T(8,128)S(1)}, u32[]{:S(2)}, u32[]{:S(2)}) collective-permute-start(f32[16,2048]{1,0:T(8,128)S(1)} %get-tuple-element.14.second_ref.f1_ref.refs_6_), channel_id=1, source_target_pairs={{0,1},{1,2},{2,3},{3,4},{4,5},{5,6},{6,7},{7,8},{8,9},{9,10},{10,1... | collective-permute-start | bytes 393224 | tf_op jit(solution)/shard_map/ppermute | solution.py:497
  41.0 1.0 %collective-permute-done.3.below_ref = f32[16,2048]{1,0:T(8,128)S(1)} collective-permute-done((f32[16,2048]{1,0:T(8,128)S(1)}, f32[16,2048]{1,0:T(8,128)S(1)}, u32[]{:S(2)}, u32[]{:S(2)}) %collective-permute-start.3) | collective-permute-done | bytes 131104 | tf_op jit(solution)/shard_map/ppermute | solution.py:498
  42.0 1.5 %collective-permute-done.2.above_ref = f32[16,2048]{1,0:T(8,128)S(1)} collective-permute-done((f32[16,2048]{1,0:T(8,128)S(1)}, f32[16,2048]{1,0:T(8,128)S(1)}, u32[]{:S(2)}, u32[]{:S(2)}) %collective-permute-start.2) | collective-permute-done | bytes 131104 | tf_op jit(solution)/shard_map/ppermute | solution.py:497
  43.5 3.5 %product.1 = (f32[16,2048]{1,0:T(8,128)S(1)}, f32[16,2048]{1,0:T(8,128)S(1)}) custom-call(f32[1]{0:T(128)S(6)} %copy.11.noise_ref.refs_1_, f32[16,2048]{1,0:T(8,128)S(1)} %collective-permute-done.2.above_ref, f32[16,2048]{1,0:T(8,128)S(1)} %get-tuple-element.13.first_ref.f0_ref.refs_5_, f32[16,2048]{1,0:T(8,128)S(1)} %get-tuple-element.14.second_ref.f1_ref.refs_6_, ...), custom_call_target="tpu_custom_call" | custom-call | flops 1073741824 | bytes 1048576 | tf_op jit(solution)/shard_map/product/pallas_call | solution.py:499
  46.9 1.3 %collective-permute-start.4 = (f32[16,2048]{1,0:T(8,128)S(1)}, f32[16,2048]{1,0:T(8,128)S(1)}, u32[]{:S(2)}, u32[]{:S(2)}) collective-permute-start(f32[16,2048]{1,0:T(8,128)S(1)} %get-tuple-element.16.g0_ref.refs_7_), channel_id=1, source_target_pairs={{1,0},{2,1},{3,2},{4,3},{5,4},{6,5},{7,6},{8,7},{9,8},{10,9},{11,1... | collective-permute-start | bytes 393224 | tf_op jit(solution)/shard_map/ppermute | solution.py:507
  48.2 1.6 %gram.1.sums_ref = f32[2,128]{1,0:T(2,128)S(1)} custom-call(f32[16,2048]{1,0:T(8,128)S(1)} %get-tuple-element.11.first_ref.b0_ref.refs_3_, f32[16,2048]{1,0:T(8,128)S(1)} %get-tuple-element.12.second_ref.b1_ref.refs_4_, f32[16,2048]{1,0:T(8,128)S(1)} %get-tuple-element.13.first_ref.f0_ref.refs_5_, ...), custom_call_target="tpu_custom_call" | custom-call | flops 268435456 | bytes 1048576 | tf_op jit(solution)/shard_map/gram/pallas_call | solution.py:508
  49.9 4.4 %collective-permute-done.4.below_ref = f32[16,2048]{1,0:T(8,128)S(1)} collective-permute-done((f32[16,2048]{1,0:T(8,128)S(1)}, f32[16,2048]{1,0:T(8,128)S(1)}, u32[]{:S(2)}, u32[]{:S(2)}) %collective-permute-start.4) | collective-permute-done | bytes 131104 | tf_op jit(solution)/shard_map/ppermute | solution.py:507
  54.2 3.0 %moment.1 = f32[64,2,128]{2,1,0:T(2,128)S(1)} custom-call(f32[1]{0:T(128)S(6)} %copy.11.noise_ref.refs_1_, f32[2,128]{1,0:T(2,128)S(1)} %gram.1.sums_ref, f32[16,2048]{1,0:T(8,128)S(1)} %get-tuple-element.16.g0_ref.refs_7_, f32[16,2048]{1,0:T(8,128)S(1)} %get-tuple-element.17.g1_ref.refs_8_, f32[16,2048]{1,0:T(8,128)S(1)} %collective-permute-done.4.below_ref, ...), custom_call_target="tpu_custom_call" | custom-call | flops 536870912 | bytes 1048576 | tf_op jit(solution)/shard_map/moment/pallas_call | solution.py:511
  57.3 33.2 %all_to_all.5.refs_2_ = f32[64,2,128]{2,1,0:T(2,128)S(1)} all-to-all(f32[64,2,128]{2,1,0:T(2,128)S(1)} %moment.1), channel_id=1, replica_groups=mesh['hyp'=8,'rows'=64] {'rows'}, dimensions={0} | all-to-all | bytes 131072 | tf_op jit(solution)/shard_map/all_to_all | solution.py:519
  90.4 2.0 %finish.1 = (f32[9,4096]{1,0:T(8,128)}, f32[1,9]{1,0:T(1,128)}) custom-call(s32[32]{0:T(128)S(1)} %copy-done.3, f32[1]{0:T(128)S(6)} %copy.11.noise_ref.refs_1_, f32[64,2,128]{2,1,0:T(2,128)S(1)} %all_to_all.5.refs_2_, f32[16,2048]{1,0:T(8,128)S(1)} %get-tuple-element.11.first_ref.b0_ref.refs_3_, f32[16,2048]{1,0:T(8,128)S(1)} %get-tuple-element.12.second_ref.b1_ref.refs_4_, ...), custom_call_target="tpu_custom_call" | custom-call | flops 1048576 | bytes 1048576 | tf_op jit(solution)/shard_map/finish/pallas_call | solution.py:524
Async XLA Ops:
  0.6 0.9 copy-start
  1.5 0.8 copy-start.1
  2.3 0.7 copy-start.2
  3.0 0.7 copy-start.3
  4.6 20.0 %collective-permute-start.1 = (f32[16,2048]{1,0:T(8,128)S(1)}, f32[16,2048]{1,0:T(8,128)S(1)}, u32[]{:S(2)}, u32[]{:S(2)}) collective-permute-start(f32[16,2048]{1,0:T(8,128)S(1)} %get-tuple-element.11.first_ref.b0_ref.refs_3_), channel_id=1, source_target_pairs={{1,0},{2,1},{3,2},{4,3},{5,4},{6,5},{7,6},{8,7},{9,8},{10,9},{11,1... | collective-permute-start | bytes 393224 | tf_op jit(solution)/shard_map/ppermute | solution.py:478
  5.9 18.7 %collective-permute-start = (f32[16,2048]{1,0:T(8,128)S(1)}, f32[16,2048]{1,0:T(8,128)S(1)}, u32[]{:S(2)}, u32[]{:S(2)}) collective-permute-start(f32[16,2048]{1,0:T(8,128)S(1)} %get-tuple-element.12.second_ref.b1_ref.refs_4_), channel_id=1, source_target_pairs={{0,1},{1,2},{2,3},{3,4},{4,5},{5,6},{6,7},{7,8},{8,9},{9,10},{10,1... | collective-permute-start | bytes 393224 | tf_op jit(solution)/shard_map/ppermute | solution.py:477
  35.1 6.9 %collective-permute-start.3 = (f32[16,2048]{1,0:T(8,128)S(1)}, f32[16,2048]{1,0:T(8,128)S(1)}, u32[]{:S(2)}, u32[]{:S(2)}) collective-permute-start(f32[16,2048]{1,0:T(8,128)S(1)} %get-tuple-element.13.first_ref.f0_ref.refs_5_), channel_id=1, source_target_pairs={{1,0},{2,1},{3,2},{4,3},{5,4},{6,5},{7,6},{8,7},{9,8},{10,9},{11,1... | collective-permute-start | bytes 393224 | tf_op jit(solution)/shard_map/ppermute | solution.py:498
  36.4 7.1 %collective-permute-start.2 = (f32[16,2048]{1,0:T(8,128)S(1)}, f32[16,2048]{1,0:T(8,128)S(1)}, u32[]{:S(2)}, u32[]{:S(2)}) collective-permute-start(f32[16,2048]{1,0:T(8,128)S(1)} %get-tuple-element.14.second_ref.f1_ref.refs_6_), channel_id=1, source_target_pairs={{0,1},{1,2},{2,3},{3,4},{4,5},{5,6},{6,7},{7,8},{8,9},{9,10},{10,1... | collective-permute-start | bytes 393224 | tf_op jit(solution)/shard_map/ppermute | solution.py:497
  46.9 7.3 %collective-permute-start.4 = (f32[16,2048]{1,0:T(8,128)S(1)}, f32[16,2048]{1,0:T(8,128)S(1)}, u32[]{:S(2)}, u32[]{:S(2)}) collective-permute-start(f32[16,2048]{1,0:T(8,128)S(1)} %get-tuple-element.16.g0_ref.refs_7_), channel_id=1, source_target_pairs={{1,0},{2,1},{3,2},{4,3},{5,4},{6,5},{7,6},{8,7},{9,8},{10,9},{11,1... | collective-permute-start | bytes 393224 | tf_op jit(solution)/shard_map/ppermute | solution.py:507
where the time goes:
time: 92.8 us; the launch traced here: 92.4 us
  Pallas kernels  33.7 us (36%)
  blocking collectives  33.2 us (36%)
  starting transfers between devices  13 us (14%)
  waiting for transfers between devices  6.88 us (7%)
  local copies, waits for them, and re-layouts  3.03 us (3%)
  between operations  2.69 us (3%)
    all_to_all x1, blocking collectives, shards(): lax.all_to_all(parts, 'rows', split_axis=0, concat_axis=0, tiled=True)  33.2 us
    pallas_call x1, Pallas kernels, shards(): call(inner_kernel, 'inner', pltpu.VMEM((4, GX, BAND, TILE), BF16), [SMEM,...  12.2 us
    pallas_call x1, Pallas kernels, shards(): call(outer_kernel, 'outer', (pltpu.VMEM((2, GX, BAND, TILE), BF16), grid_...  10.5 us
    ppermute x1, starting transfers between devices, shards(): above = lax.ppermute(second, 'rows', down)  4.55 us
    ppermute x1, starting transfers between devices, shards(): f_above = lax.ppermute(f1, 'rows', down)  4.55 us
    ppermute x1, waiting for transfers between devices, shards(): g_below = lax.ppermute(g0, 'rows', up)  4.38 us
    pallas_call x1, Pallas kernels, shards(): call(product_kernel, 'product', (grid_row(), grid_row()), [SMEM] + [VMEM]...  3.46 us
    pallas_call x1, Pallas kernels, shards(): call(moment_kernel, 'moment', jax.ShapeDtypeStruct((size, 2, TILE), F32),...  3.03 us
  transfers between devices with their start and end apart: 5, of which 3 were waited for; matrix products, arithmetic and copies ran while one was open for 0% of the time, Pallas kernels for 15%

commit v1 on v0

v1 whole, which is shorter than its diff:
```python
import jax
import jax.numpy as jnp
from jax import lax
from jax.experimental import pallas as pl
from jax.experimental.pallas import tpu as pltpu
from jax.sharding import PartitionSpec as P

TILE = 128
GX = 16
RHS = 9
ROWS = 16
WIDE = GX * TILE
FEATURES = 32
PAD = GX + 2
BAND = 3 * 2 * TILE
F32 = jnp.float32
BF16 = jnp.bfloat16
TINY = 1e-30

VMEM = pl.BlockSpec(memory_space=pltpu.VMEM)
HBM = pl.BlockSpec(memory_space=pltpu.HBM)
SMEM = pl.BlockSpec(memory_space=pltpu.SMEM)
REACH, TOP, FACTOR, NOISE = range(4)


def call(kernel, name, out_shape, in_specs, scratch=(), flops=0, limit=12):
    return pl.pallas_call(
        kernel,
        name=name,
        out_shape=out_shape,
        in_specs=in_specs,
        out_specs=jax.tree.map(lambda _: VMEM, out_shape),
        scratch_shapes=list(scratch),
        cost_estimate=pl.CostEstimate(flops=flops, bytes_accessed=1 << 20, transcendentals=0),
        compiler_params=pltpu.CompilerParams(vmem_limit_bytes=int(limit * 2**20)),
    )


def grid_row():
    return jax.ShapeDtypeStruct((ROWS, WIDE), F32)


def spread_row():
    return pltpu.VMEM((2 * ROWS, PAD * 2 * TILE), BF16)


def weight_rows(count):
    return pltpu.VMEM((count, GX, BAND, TILE), BF16)


def feature_tiles():
    return pltpu.VMEM((PAD, TILE, FEATURES), BF16)


def lanes(tile, width=TILE):
    return pl.ds(pl.multiple_of(tile * width, width), width)


def pack_kernel(
    cell_hbm,
    offsets_hbm,
    probes_hbm,
    target_hbm,
    scale_ref,
    amp_ref,
    noise_ref,
    first_ref,
    second_ref,
    consts_ref,
    cell_ref,
    offsets_ref,
    probes_ref,
    target_ref,
    sems,
):
    copies = [
        pltpu.make_async_copy(source, dest, sems.at[i])
        for i, (source, dest) in enumerate(
            (
                (cell_hbm, cell_ref),
                (offsets_hbm, offsets_ref),
                (probes_hbm, probes_ref),
                (target_hbm, target_ref),
            )
        )
    ]
    for copy in copies:
        copy.start()
    for copy in copies:
        copy.wait()
    filler = jnp.zeros((ROWS - RHS - 2, TILE), F32)
    for s in range(cell_ref.shape[0]):
        here = slice(s * TILE, (s + 1) * TILE)
        signs = 2.0 * probes_ref[:, here].astype(F32) - 1.0
        rest = jnp.concatenate([target_ref[:, here], offsets_ref[:, here], filler], axis=0)
        cell = cell_ref[s]

        def put(ref, column, signs=signs, rest=rest):
            ref[0:8, lanes(column)] = signs
            ref[8:16, lanes(column)] = rest

        @pl.when(cell < GX)
        def _():
            put(first_ref, cell)

        @pl.when(cell >= GX)
        def _():
            put(second_ref, cell - GX)

    amp = jnp.full((1, TILE), amp_ref[0], F32)
    reach = jnp.exp(0.2 * jnp.log(4.0 * amp))
    square = reach * reach
    consts_ref[REACH : REACH + 1, :] = reach
    consts_ref[TOP : TOP + 1, :] = 5.0 * amp / (square * square)
    consts_ref[FACTOR : FACTOR + 1, :] = reach / jnp.full((1, TILE), scale_ref[0], F32)
    consts_ref[NOISE : NOISE + 1, :] = jnp.full((1, TILE), noise_ref[0], F32)


def constant(consts_ref, which):
    return consts_ref[which : which + 1, :]


def split_rows(values, level):
    first = values.astype(BF16).astype(F32)
    rest = values - first
    second = rest.astype(BF16).astype(F32)
    third = rest - second
    return jnp.where(level == 0, first, jnp.where(level == 1, second, third))


def feature_rows():
    row = lax.broadcasted_iota(jnp.int32, (FEATURES, TILE), 0)

    def level(order):
        out = jnp.zeros_like(row)
        for k, v in enumerate(order):
            if v:
                out = jnp.where(row == k, v, out)
        return out

    source = level([0, 0, 1, 1, 0, 2] * 2 + [0, 1, 2] + [0, 0, 0])
    target = level([0, 1, 0, 1, 2, 0] * 2 + [0, 0, 0] + [0, 1, 2])
    kind = jnp.where(row < 6, 0, jnp.where(row < 12, 1, jnp.where(row < 15, 2, jnp.where(row < 18, 3, 4))))
    return kind, source, target


def choose(kind, a, b, c, d):
    return jnp.where(
        kind == 0, a, jnp.where(kind == 1, b, jnp.where(kind == 2, c, jnp.where(kind == 3, d, 0.0)))
    )


def source_features(row_ref, factor, rows, out_ref):
    kind, source, _ = rows
    zero = jnp.zeros((TILE, FEATURES), BF16)
    out_ref[0] = zero
    out_ref[PAD - 1] = zero

    def one(tile, carry):
        a = factor * (row_ref[9:10, lanes(tile)] - 0.5)
        b = factor * (row_ref[10:11, lanes(tile)] - 0.5)
        values = choose(kind, a, b, a * a + b * b, 1.0)
        out_ref[tile + 1] = split_rows(values, source).T.astype(BF16)
        return carry

    lax.fori_loop(0, GX, one, 0, unroll=4)


def target_features(row_ref, tile, row_shift, col_shift, factor, rows):
    kind, _, target = rows
    a = factor * ((row_shift + 0.5) - row_ref[9:10, lanes(tile)])
    b = factor * ((col_shift + 0.5) - row_ref[10:11, lanes(tile)])
    values = choose(kind, 2.0 * a, 2.0 * b, 1.0, a * a + b * b)
    return split_rows(values, target).astype(BF16)


def fill_weights(target_ref, row_shift, feats_ref, weights_ref, combo, consts_ref, rows):
    factor = constant(consts_ref, FACTOR)
    reach = jnp.broadcast_to(constant(consts_ref, REACH), (16, TILE))
    top = jnp.broadcast_to(constant(consts_ref, TOP), (16, TILE))

    def one(tile, carry):
        for k in range(3):
            wanted = target_features(target_ref, tile, float(row_shift), float(k - 1), factor, rows)
            square = lax.dot_general(
                feats_ref[tile + k],
                wanted,
                (((1,), (0,)), ((), ())),
                preferred_element_type=F32,
            )
            for part in range(TILE // 16):
                here = jnp.maximum(square[part * 16 : (part + 1) * 16, :], 1e-12)
                close = jnp.maximum(reach - here * lax.rsqrt(here), 0.0)
                second = close * close
                weight = (second * second) * (top - close)
                high = weight.astype(BF16)
                low = (weight - high.astype(F32)).astype(BF16)
                base = k * 2 * TILE + part * 16
                weights_ref[combo, tile, base : base + 16, :] = high
                weights_ref[combo, tile, base + TILE : base + TILE + 16, :] = low
        return carry

    lax.fori_loop(0, GX, one, 0, unroll=8)


def spread_ends(out_ref):
    empty = jnp.zeros((2 * ROWS, 2 * TILE), BF16)
    out_ref[:, 0 : 2 * TILE] = empty
    out_ref[:, (PAD - 1) * 2 * TILE :] = empty


def spread_tile(values, out_ref, tile):
    high = values.astype(BF16)
    low = (values - high.astype(F32)).astype(BF16)
    both = jnp.concatenate([high, low], axis=0)
    at = pl.multiple_of((tile + 1) * 2 * TILE, 2 * TILE)
    out_ref[:, pl.ds(at, 2 * TILE)] = jnp.concatenate([both, both], axis=1)


def spread(row_ref, out_ref):
    spread_ends(out_ref)
    for tile in range(GX):
        spread_tile(row_ref[:, tile * TILE : (tile + 1) * TILE], out_ref, tile)


def banded(spread_ref, weights_ref, combo, tile):
    at = pl.multiple_of(tile * 2 * TILE, 2 * TILE)
    both = jnp.dot(
        spread_ref[:, pl.ds(at, BAND)],
        weights_ref[combo, tile],
        preferred_element_type=F32,
    )
    return both[0:ROWS] + both[ROWS:]


GROUP = 8


def apply_row(own_ref, terms, consts_ref, out_ref, out_spread_ref):
    noise = constant(consts_ref, NOISE)
    spread_ends(out_spread_ref)

    def group(g, carry):
        for j in range(GROUP):
            tile = g * GROUP + j
            here = lanes(tile)
            total = noise * own_ref[:, here]
            for term in terms:
                total = total + banded(*term, tile)
            out_ref[:, here] = total
            spread_tile(total, out_spread_ref, tile)
        return carry

    lax.fori_loop(0, GX // GROUP, group, 0)


def two_sum(a, b):
    total = a + b
    part = total - a
    return total, (a - (total - part)) + (b - part)


def quick_sum(a, b):
    total = a + b
    return total, b - (total - a)


def halves(a):
    scaled = 4097.0 * a
    high = scaled - (scaled - a)
    return high, a - high


def two_product(a, b, a_halves=None, b_halves=None):
    a1, a2 = halves(a) if a_halves is None else a_halves
    b1, b2 = halves(b) if b_halves is None else b_halves
    product = a * b
    return product, ((a1 * b1 - product) + a1 * b2 + a2 * b1) + a2 * b2


class Pair:
    def __init__(self, high, low):
        self.high, self.low = high, low

    def __add__(self, other):
        total, error = two_sum(self.high, other.high)
        return Pair(*quick_sum(total, error + (self.low + other.low)))

    def __neg__(self):
        return Pair(-self.high, -self.low)

    def __sub__(self, other):
        return self + (-other)

    def __mul__(self, other):
        if not isinstance(other, Pair):
            return Pair(self.high * other, self.low * other)
        product, error = two_product(self.high, other.high)
        return Pair(*quick_sum(product, error + (self.high * other.low + self.low * other.high)))

    def __truediv__(self, other):
        first = self.high / other.high
        rest = self - other * Pair(first, jnp.zeros_like(first))
        return Pair(*quick_sum(first, rest.high / other.high))

    def where(self, keep, other):
        return Pair(jnp.where(keep, self.high, other.high), jnp.where(keep, self.low, other.low))


def grid_mask(k):
    lane = lax.broadcasted_iota(jnp.int32, (ROWS, TILE), 1)
    row = lax.broadcasted_iota(jnp.int32, (ROWS, TILE), 0)
    return lane == row + ROWS * k


def add_product(sums, a, b, a_halves, b_halves):
    product, error = two_product(a, b, a_halves, b_halves)
    total, left = two_sum(sums[0], product)
    return total, sums[1] + (left + error)


def lines(sums, first):
    placed = [jnp.zeros((ROWS, TILE), F32), jnp.zeros((ROWS, TILE), F32)]
    for k, (high, low) in enumerate(sums):
        for shift in (64, 32, 16, 8, 4, 2, 1):
            high, left = two_sum(high, pltpu.roll(high, shift, 1))
            low = (low + pltpu.roll(low, shift, 1)) + left
        high, low = quick_sum(high, low)
        mask = grid_mask(first + k)
        placed = [jnp.where(mask, high, placed[0]), jnp.where(mask, low, placed[1])]
    return [jnp.sum(p, axis=0, keepdims=True) for p in placed]


def inner_kernel(slot, first_ref, second_ref, consts_ref, weights_ref, spread_ref, feats_ref):
    rows = feature_rows()
    own_ref = (first_ref, second_ref)[slot]
    source_features(own_ref, constant(consts_ref, FACTOR), rows, feats_ref)
    fill_weights(first_ref, slot, feats_ref, weights_ref, 0, consts_ref, rows)
    fill_weights(second_ref, slot - 1, feats_ref, weights_ref, 1, consts_ref, rows)
    spread(own_ref, spread_ref)


def outer_kernel(
    slot,
    other_ref,
    own_ref,
    consts_ref,
    left_ref,
    right_ref,
    spread0_ref,
    spread1_ref,
    weights_ref,
    out_ref,
    out_spread_ref,
    feats_ref,
    spread_ref,
):
    rows = feature_rows()
    source_features(other_ref, constant(consts_ref, FACTOR), rows, feats_ref)
    fill_weights(own_ref, 2 * slot - 1, feats_ref, weights_ref, 0, consts_ref, rows)
    spread(other_ref, spread_ref)
    terms = ((spread_ref, weights_ref, 0), (spread0_ref, left_ref, slot), (spread1_ref, right_ref, slot))
    apply_row(own_ref, terms, consts_ref, out_ref, out_spread_ref)


def product_kernel(
    slot,
    other_ref,
    own_ref,
    consts_ref,
    left_ref,
    right_ref,
    weights_ref,
    spread0_ref,
    spread1_ref,
    out_ref,
    out_spread_ref,
    spread_ref,
):
    spread(other_ref, spread_ref)
    terms = ((spread_ref, weights_ref, 0), (spread0_ref, left_ref, slot), (spread1_ref, right_ref, slot))
    apply_row(own_ref, terms, consts_ref, out_ref, out_spread_ref)


def gram_kernel(
    b0_ref,
    b1_ref,
    f0_ref,
    f1_ref,
    g0_ref,
    g1_ref,
    consts_ref,
    left_ref,
    right_ref,
    spread0_ref,
    spread1_ref,
    sums_ref,
):
    zero = jnp.zeros((ROWS, TILE), F32)
    noise = constant(consts_ref, NOISE)

    def group(g, sums):
        sums = list(sums)
        for j in range(4):
            tile = g * 4 + j
            here = lanes(tile)
            for half, refs in enumerate(((b0_ref, f0_ref, g0_ref), (b1_ref, f1_ref, g1_ref))):
                values = [ref[:, here] for ref in refs]
                parts = [halves(v) for v in values]
                for k, (i, j2) in enumerate(((0, 0), (0, 1), (0, 2), (1, 1), (1, 2), (2, 2))):
                    sums[k] = add_product(sums[k], values[i], values[j2], parts[i], parts[j2])
                image = noise * values[2]
                if half == 0:
                    image = image + banded(spread0_ref, left_ref, 0, tile)
                    image = image + 2.0 * banded(spread1_ref, right_ref, 0, tile)
                else:
                    image = image + banded(spread1_ref, right_ref, 1, tile)
                sums[6] = add_product(sums[6], values[2], image, parts[2], halves(image))
        return tuple(sums)

    high, low = lines(lax.fori_loop(0, GX // 4, group, ((zero, zero),) * 7), 0)
    sums_ref[0:1, :] = high
    sums_ref[1:2, :] = low


def moment_kernel(sums_ref, below_ref, own_ref, weights_ref, out_ref, spread_ref):
    spread(below_ref, spread_ref)

    def group(g, sums):
        for j in range(GROUP):
            tile = g * GROUP + j
            v = own_ref[:, lanes(tile)]
            image = 2.0 * banded(spread_ref, weights_ref, 0, tile)
            sums = add_product(sums, v, image, halves(v), halves(image))
        return sums

    zero = jnp.zeros((ROWS, TILE), F32)
    high, low = lines((lax.fori_loop(0, GX // GROUP, group, (zero, zero)),), 6)
    total, left = two_sum(sums_ref[0:1, :], high)
    both = jnp.concatenate([total, left + (low + sums_ref[1:2, :])], axis=0)
    out_ref[...] = jnp.broadcast_to(both[None], out_ref.shape)


def finish_kernel(
    points,
    cell_hbm,
    consts_ref,
    parts_ref,
    b0_ref,
    b1_ref,
    f0_ref,
    f1_ref,
    g0_ref,
    g1_ref,
    out_ref,
    quad_ref,
    cell_ref,
    grid_ref,
    sem,
):
    copy = pltpu.make_async_copy(cell_hbm, cell_ref, sem)
    copy.start()
    high, low = parts_ref[:, 0, :], parts_ref[:, 1, :]
    while high.shape[0] > 8:
        half = high.shape[0] // 2
        high, left = two_sum(high[:half], high[half:])
        low = (low[:half] + low[half:]) + left
    for shift in (4, 2, 1):
        high, left = two_sum(high, pltpu.roll(high, shift, 0))
        low = (low + pltpu.roll(low, shift, 0)) + left
    high, low = quick_sum(high, low)
    bb, bf, bg, ff, fg, gg, gag = (
        Pair(high, low)
        if k == 0
        else Pair(pltpu.roll(high, TILE - ROWS * k, 1), pltpu.roll(low, TILE - ROWS * k, 1))
        for k in range(7)
    )
    zero = jnp.zeros_like(high)
    none = Pair(zero, zero)
    one = Pair(zero + 1.0, zero)
    most = jnp.broadcast_to(1.0 / constant(consts_ref, NOISE), high.shape)

    floor = bb.high * 1e-11

    def step(square, product):
        good = (square.high > floor) & (product.high > 0.0)
        ratio = square / product.where(good, one)
        fits = ratio.high < most
        return ratio.where(fits, Pair(most, zero)).where(good, none), good

    def over(a, b, good):
        return (a / b.where(good, one)).where(good, none)

    alpha0, good0 = step(bb, bf)
    rr1 = bb - alpha0 * (bf * 2.0 - alpha0 * ff)
    beta0 = over(rr1, bb, good0)
    p0, p1 = one + beta0, -alpha0
    alpha1, good1 = step(rr1, p0 * (p0 * bf + p1 * (bg + ff)) + p1 * p1 * fg)
    r1, r2 = -(alpha0 + alpha1 * p0), -(alpha1 * p1)
    rr2 = bb + r1 * (bf * 2.0 + r1 * ff) + r2 * (bg * 2.0 + r1 * fg * 2.0 + r2 * gg)
    beta1 = over(rr2, rr1, good1)
    q0, q1, q2 = one + beta1 * p0, r1 + beta1 * p1, r2
    alpha2, good2 = step(
        rr2,
        q0 * (q0 * bf + q1 * (bg + ff) + q2 * fg * 2.0)
        + q1 * (q1 * fg + q2 * gg * 2.0)
        + q2 * q2 * gag,
    )
    alpha2 = alpha2.where(good1, none)
    on_b = alpha0 + alpha1 * p0 + alpha2 * q0
    on_f = alpha1 * p1 + alpha2 * q1
    on_g = alpha2 * q2
    quad = on_b * bb + on_f * bf + on_g * bg
    quad_ref[...] = (quad.high / points)[0:1, 0:RHS]
    mask = grid_mask(0)
    c0, c1, c2 = (
        jnp.broadcast_to(
            jnp.sum(
                jnp.where(mask, jnp.concatenate([c.high, c.high], axis=0), 0.0), axis=1, keepdims=True
            ),
            (ROWS, TILE),
        )
        for c in (on_b, on_f, on_g)
    )
    for half, (b_ref, f_ref, g_ref) in enumerate(
        ((b0_ref, f0_ref, g0_ref), (b1_ref, f1_ref, g1_ref))
    ):
        for tile in range(GX):
            here = slice(tile * TILE, (tile + 1) * TILE)
            grid_ref[half * GX + tile] = (
                c0 * b_ref[:, here] + c1 * f_ref[:, here] + c2 * g_ref[:, here]
            )
    copy.wait()
    for s in range(cell_ref.shape[0]):
        out_ref[:, s * TILE : (s + 1) * TILE] = grid_ref[cell_ref[s], 0:RHS, :]


def shards(offsets, tile_cell, probes, target, lengthscale, amplitude, noise):
    size = lax.axis_size("rows")
    points = size * tile_cell.shape[0] * TILE
    down = [(i, i + 1) for i in range(size - 1)]
    up = [(i + 1, i) for i in range(size - 1)]

    tiles = tile_cell.shape[0]
    first, second, consts = call(
        pack_kernel,
        "pack",
        (pltpu.VMEM((ROWS, WIDE), F32), pltpu.VMEM((ROWS, WIDE), F32), pltpu.VMEM((8, TILE), F32)),
        [HBM] * 4 + [SMEM] * 3,
        [
            pltpu.SMEM((tiles,), jnp.int32),
            pltpu.VMEM((2, tiles * TILE), F32),
            pltpu.VMEM((8, tiles * TILE), jnp.int32),
            pltpu.VMEM((1, tiles * TILE), F32),
            pltpu.SemaphoreType.DMA((4,)),
        ],
        flops=1 << 20,
        limit=60.5,
    )(
        tile_cell,
        offsets,
        probes,
        target.reshape(1, -1),
        lengthscale,
        amplitude,
        noise,
    )

    def inner(slot):
        return call(
            lambda *refs: inner_kernel(slot, *refs),
            f"inner{slot}",
            (weight_rows(2), spread_row()),
            [VMEM] * 3,
            [feature_tiles()],
            flops=1 << 30,
        )(first, second, consts)

    def outer(slot, other, own):
        return call(
            lambda *refs: outer_kernel(slot, *refs),
            f"outer{slot}",
            (weight_rows(1), grid_row(), spread_row()),
            [VMEM] * 7,
            [feature_tiles(), spread_row()],
            flops=1 << 30,
        )(other, own, consts, left, right, b0_spread, b1_spread)

    def product(slot, other, own, weights):
        return call(
            lambda *refs: product_kernel(slot, *refs),
            f"product{slot}",
            (grid_row(), spread_row()),
            [VMEM] * 8,
            [spread_row()],
            flops=1 << 29,
        )(other, own, consts, left, right, weights, f0_spread, f1_spread)

    above = lax.ppermute(second, "rows", down)
    left, b0_spread = inner(0)
    gated, left = lax.optimization_barrier((first, left))
    below = lax.ppermute(gated, "rows", up)
    right, b1_spread = inner(1)
    over, f0, f0_spread = outer(0, above, first)
    f_below = lax.ppermute(f0, "rows", up)
    under, f1, f1_spread = outer(1, below, second)
    f_above = lax.ppermute(f1, "rows", down)
    g1, g1_spread = product(1, f_below, f1, under)
    g0, g0_spread = product(0, f_above, f0, over)
    g_below = lax.ppermute(g0, "rows", up)
    sums = call(
        gram_kernel, "gram", jax.ShapeDtypeStruct((2, TILE), F32), [VMEM] * 11, flops=1 << 29
    )(first, second, f0, f1, g0, g1, consts, left, right, g0_spread, g1_spread)
    parts = call(
        moment_kernel,
        "moment",
        jax.ShapeDtypeStruct((size, 2, TILE), F32),
        [VMEM] * 4,
        [spread_row()],
        flops=1 << 29,
    )(sums, g_below, g1, under)
    parts = lax.all_to_all(parts, "rows", split_axis=0, concat_axis=0, tiled=True)

    solutions, quad = call(
        lambda *refs: finish_kernel(float(points), *refs),
        "finish",
        (
            jax.ShapeDtypeStruct((RHS, tiles * TILE), F32),
            jax.ShapeDtypeStruct((1, RHS), F32),
        ),
        [HBM] + [VMEM] * 8,
        [
            pltpu.SMEM((tiles,), jnp.int32),
            pltpu.VMEM((tiles, ROWS, TILE), F32),
            pltpu.SemaphoreType.DMA,
        ],
        flops=1 << 20,
    )(tile_cell, consts, parts, first, second, f0, f1, g0, g1)
    return (solutions, quad.reshape(RHS))


def solution(mesh):
    return jax.shard_map(
        shards,
        mesh=mesh,
        in_specs=(
            P(None, "rows"),
            P("rows"),
            P(None, "rows"),
            P("rows"),
            P("hyp"),
            P("hyp"),
            P("hyp"),
        ),
        out_specs=(P("hyp", "rows"), P("hyp")),
        check_vma=False,
    )
```

time: 92.8 us -> 74.4 us (0.80)
  Pallas kernels: 33.7 us -> 26.9 us
  waiting for transfers between devices: 6.88 us -> 2.53 us
  blocking collectives: 33.2 us -> 30 us
  local copies, waits for them, and re-layouts: 3.03 us -> 0.01 us
  starting transfers between devices: 13 us -> 11.9 us
    pallas_call x5 -> x8, Pallas kernels: 29 us -> 22.8 us  [the longest x2 8.38 us: inner(): call(lambda *refs: inner_kernel(slot, *refs), f'inner{slot}', (weight_row...]
    ppermute x1, waiting for transfers between devices: 4.38 us -> 0.01 us  [shards(): g_below = lax.ppermute(g0, 'rows', up)]
    all_to_all x1, blocking collectives: 33.2 us -> 30 us  [shards(): lax.all_to_all(parts, 'rows', split_axis=0, concat_axis=0, tiled=True)]
    unnamed x8 -> x2, local copies, waits for them, and re-layouts: 3.03 us -> 0.01 us
    pallas_call x1, Pallas kernels: 3.03 us -> 1.3 us  [shards(): call(moment_kernel, 'moment', jax.ShapeDtypeStruct((size, 2, TILE), F32),...]
    ppermute x1, waiting for transfers between devices: 1 us -> 2.52 us  [shards(): f_below = lax.ppermute(f0, 'rows', up)]
    ppermute x1, waiting for transfers between devices: 1.5 us -> 0.01 us  [shards(): f_above = lax.ppermute(f1, 'rows', down)]
    pallas_call x1, Pallas kernels: 1.61 us -> 2.84 us  [shards(): call(gram_kernel, 'gram', jax.ShapeDtypeStruct((2, TILE), F32), [VMEM] *...]
  transfers between devices with their start and end apart: 5 -> 5, of which waited for: 3 -> 1; matrix products, arithmetic and copies ran while one was open for 0% -> 0% of each run, Pallas kernels for 15% -> 25%
where the time goes in v1:
time: 74.4 us; the launch traced here: 74 us
  blocking collectives  30 us (40%)
  Pallas kernels  26.9 us (36%)
  starting transfers between devices  11.9 us (16%)
  between operations  2.71 us (4%)
  waiting for transfers between devices  2.53 us (3%)
    all_to_all x1, blocking collectives, shards(): lax.all_to_all(parts, 'rows', split_axis=0, concat_axis=0, tiled=True)  30 us
    pallas_call x2, Pallas kernels, inner(): call(lambda *refs: inner_kernel(slot, *refs), f'inner{slot}', (weight_row...  8.38 us
    pallas_call x2, Pallas kernels, outer(): call(lambda *refs: outer_kernel(slot, *refs), f'outer{slot}', (weight_row...  8.1 us
    ppermute x1, starting transfers between devices, shards(): above = lax.ppermute(second, 'rows', down)  4.55 us
    ppermute x1, starting transfers between devices, shards(): f_above = lax.ppermute(f1, 'rows', down)  3.49 us
    pallas_call x2, Pallas kernels, product(): call(lambda *refs: product_kernel(slot, *refs), f'product{slot}', (grid_r...  3.44 us
    pallas_call x1, Pallas kernels, shards(): call(gram_kernel, 'gram', jax.ShapeDtypeStruct((2, TILE), F32), [VMEM] *...  2.84 us
    ppermute x1, waiting for transfers between devices, shards(): f_below = lax.ppermute(f0, 'rows', up)  2.52 us
  transfers between devices with their start and end apart: 5, of which 1 were waited for; matrix products, arithmetic and copies ran while one was open for 0% of the time, Pallas kernels for 25%

profile of v1, /device:TPU:2, one launch (start us, length us, event | category | flops | bytes accessed | tf_op | source)
XLA Modules:
  0.0 74.0 jit_solution(12450728428345799742)
XLA Ops:
  2.6 1.4 %pack.1 = (f32[16,2048]{1,0:T(8,128)S(1)}, f32[16,2048]{1,0:T(8,128)S(1)}, f32[8,128]{1,0:T(8,128)S(1)}) custom-call(s32[32]{0:T(128)} %refs_0_.1, f32[2,4096]{1,0:T(2,128)} %offsets_hbm.1, s32[8,4096]{1,0:T(8,128)} %probes_hbm.1, f32[1,4096]{1,0:T(1,128)} %bitcast.2, f32[1]{0:T(128)S(6)} %copy.9.scale_ref, f32[1]{0:T(128)S(6)} %copy.10.amp_ref, ...), custom_call_target="tpu_custom_call" | custom-call | flops 1048576 | bytes 1048576 | tf_op jit(solution)/shard_map/pack/pallas_call | solution.py:545
  4.0 4.2 %inner0.1 = (bf16[2,16,768,128]{3,2,1,0:T(8,128)(2,1)S(1)}, bf16[32,4608]{1,0:T(8,128)(2,1)S(1)}) custom-call(f32[16,2048]{1,0:T(8,128)S(1)} %get-tuple-element.32.refs_0_.refs_1_.b0_ref.refs_3_, f32[16,2048]{1,0:T(8,128)S(1)} %get-tuple-element.25.refs_1_.b1_ref.refs_4_, f32[8,128]{1,0:T(8,128)S(1)} %get-tuple-element.23.refs_2_.consts_ref.refs_1_), custom_call_target="tpu_custom_call" | custom-call | flops 1073741824 | bytes 1048576 | tf_op jit(solution)/shard_map/inner0/pallas_call | solution.py:570
  8.2 1.3 %collective-permute-start.1 = (f32[16,2048]{1,0:T(8,128)S(1)}, f32[16,2048]{1,0:T(8,128)S(1)}, u32[]{:S(2)}, u32[]{:S(2)}) collective-permute-start(f32[16,2048]{1,0:T(8,128)S(1)} %get-tuple-element.32.refs_0_.refs_1_.b0_ref.refs_3_), channel_id=1, source_target_pairs={{1,0},{2,1},{3,2},{4,3},{5,4},{6,5},{7,6},{8,7},{9,8},{10,9},{11,1... | collective-permute-start | bytes 393224 | tf_op jit(solution)/shard_map/ppermute | solution.py:602
  9.5 4.6 %collective-permute-start = (f32[16,2048]{1,0:T(8,128)S(1)}, f32[16,2048]{1,0:T(8,128)S(1)}, u32[]{:S(2)}, u32[]{:S(2)}) collective-permute-start(f32[16,2048]{1,0:T(8,128)S(1)} %get-tuple-element.25.refs_1_.b1_ref.refs_4_), channel_id=1, source_target_pairs={{0,1},{1,2},{2,3},{3,4},{4,5},{5,6},{6,7},{7,8},{8,9},{9,10},{10,1... | collective-permute-start | bytes 393224 | tf_op jit(solution)/shard_map/ppermute | solution.py:599
  14.0 4.2 %inner1.1 = (bf16[2,16,768,128]{3,2,1,0:T(8,128)(2,1)S(1)}, bf16[32,4608]{1,0:T(8,128)(2,1)S(1)}) custom-call(f32[16,2048]{1,0:T(8,128)S(1)} %get-tuple-element.32.refs_0_.refs_1_.b0_ref.refs_3_, f32[16,2048]{1,0:T(8,128)S(1)} %get-tuple-element.25.refs_1_.b1_ref.refs_4_, f32[8,128]{1,0:T(8,128)S(1)} %get-tuple-element.23.refs_2_.consts_ref.refs_1_), custom_call_target="tpu_custom_call" | custom-call | flops 1073741824 | bytes 1048576 | tf_op jit(solution)/shard_map/inner1/pallas_call | solution.py:570
  18.2 0.0 collective-permute-done.1.refs_0_
  18.2 4.0 %outer1.1 = (bf16[1,16,768,128]{3,2,1,0:T(8,128)(2,1)S(1)}, f32[16,2048]{1,0:T(8,128)S(1)}, bf16[32,4608]{1,0:T(8,128)(2,1)S(1)}) custom-call(f32[16,2048]{1,0:T(8,128)S(1)} %collective-permute-done.1.refs_0_, f32[16,2048]{1,0:T(8,128)S(1)} %get-tuple-element.25.refs_1_.b1_ref.refs_4_, f32[8,128]{1,0:T(8,128)S(1)} %get-tuple-element.23.refs_2_.consts_ref.refs_1_, ...), custom_call_target="tpu_custom_call" | custom-call | flops 1073741824 | bytes 1048576 | tf_op jit(solution)/shard_map/outer1/pallas_call | solution.py:580
  22.3 3.5 %collective-permute-start.2 = (f32[16,2048]{1,0:T(8,128)S(1)}, f32[16,2048]{1,0:T(8,128)S(1)}, u32[]{:S(2)}, u32[]{:S(2)}) collective-permute-start(f32[16,2048]{1,0:T(8,128)S(1)} %get-tuple-element.33.refs_1_.f1_ref.refs_6_), channel_id=1, source_target_pairs={{0,1},{1,2},{2,3},{3,4},{4,5},{5,6},{6,7},{7,8},{8,9},{9,10},{10,1... | collective-permute-start | bytes 393224 | tf_op jit(solution)/shard_map/ppermute | solution.py:607
  25.8 0.0 collective-permute-done.refs_0_
  25.8 4.1 %outer0.1 = (bf16[1,16,768,128]{3,2,1,0:T(8,128)(2,1)S(1)}, f32[16,2048]{1,0:T(8,128)S(1)}, bf16[32,4608]{1,0:T(8,128)(2,1)S(1)}) custom-call(f32[16,2048]{1,0:T(8,128)S(1)} %collective-permute-done.refs_0_, f32[16,2048]{1,0:T(8,128)S(1)} %get-tuple-element.32.refs_0_.refs_1_.b0_ref.refs_3_, f32[8,128]{1,0:T(8,128)S(1)} %get-tuple-element.23.refs_2_.consts_ref.refs_1_, ...), custom_call_target="tpu_custom_call" | custom-call | flops 1073741824 | bytes 1048576 | tf_op jit(solution)/shard_map/outer0/pallas_call | solution.py:580
  29.8 1.3 %collective-permute-start.3 = (f32[16,2048]{1,0:T(8,128)S(1)}, f32[16,2048]{1,0:T(8,128)S(1)}, u32[]{:S(2)}, u32[]{:S(2)}) collective-permute-start(f32[16,2048]{1,0:T(8,128)S(1)} %get-tuple-element.31.refs_1_.f0_ref.refs_5_), channel_id=1, source_target_pairs={{1,0},{2,1},{3,2},{4,3},{5,4},{6,5},{7,6},{8,7},{9,8},{10,9},{11,1... | collective-permute-start | bytes 393224 | tf_op jit(solution)/shard_map/ppermute | solution.py:605
  31.1 0.0 collective-permute-done.2.refs_0_
  31.2 1.7 %product0.1 = (f32[16,2048]{1,0:T(8,128)S(1)}, bf16[32,4608]{1,0:T(8,128)(2,1)S(1)}) custom-call(f32[16,2048]{1,0:T(8,128)S(1)} %collective-permute-done.2.refs_0_, f32[16,2048]{1,0:T(8,128)S(1)} %get-tuple-element.31.refs_1_.f0_ref.refs_5_, f32[8,128]{1,0:T(8,128)S(1)} %get-tuple-element.23.refs_2_.consts_ref.refs_1_, ...), custom_call_target="tpu_custom_call" | custom-call | flops 536870912 | bytes 1048576 | tf_op jit(solution)/shard_map/product0/pallas_call | solution.py:590
  32.9 1.3 %collective-permute-start.4 = (f32[16,2048]{1,0:T(8,128)S(1)}, f32[16,2048]{1,0:T(8,128)S(1)}, u32[]{:S(2)}, u32[]{:S(2)}) collective-permute-start(f32[16,2048]{1,0:T(8,128)S(1)} %get-tuple-element.37.g0_ref.refs_7_), channel_id=1, source_target_pairs={{1,0},{2,1},{3,2},{4,3},{5,4},{6,5},{7,6},{8,7},{9,8},{10,9},{11,1... | collective-permute-start | bytes 393224 | tf_op jit(solution)/shard_map/ppermute | solution.py:610
  34.2 2.5 %collective-permute-done.3.refs_0_ = f32[16,2048]{1,0:T(8,128)S(1)} collective-permute-done((f32[16,2048]{1,0:T(8,128)S(1)}, f32[16,2048]{1,0:T(8,128)S(1)}, u32[]{:S(2)}, u32[]{:S(2)}) %collective-permute-start.3) | collective-permute-done | bytes 131104 | tf_op jit(solution)/shard_map/ppermute | solution.py:605
  36.7 1.7 %product1.1 = (f32[16,2048]{1,0:T(8,128)S(1)}, bf16[32,4608]{1,0:T(8,128)(2,1)S(1)}) custom-call(f32[16,2048]{1,0:T(8,128)S(1)} %collective-permute-done.3.refs_0_, f32[16,2048]{1,0:T(8,128)S(1)} %get-tuple-element.33.refs_1_.f1_ref.refs_6_, f32[8,128]{1,0:T(8,128)S(1)} %get-tuple-element.23.refs_2_.consts_ref.refs_1_, ...), custom_call_target="tpu_custom_call" | custom-call | flops 536870912 | bytes 1048576 | tf_op jit(solution)/shard_map/product1/pallas_call | solution.py:590
  38.4 0.0 copy-start
  38.4 2.8 %gram.1.sums_ref = f32[2,128]{1,0:T(2,128)S(1)} custom-call(f32[16,2048]{1,0:T(8,128)S(1)} %get-tuple-element.32.refs_0_.refs_1_.b0_ref.refs_3_, f32[16,2048]{1,0:T(8,128)S(1)} %get-tuple-element.25.refs_1_.b1_ref.refs_4_, f32[16,2048]{1,0:T(8,128)S(1)} %get-tuple-element.31.refs_1_.f0_ref.refs_5_, f32[16,2048]{1,0:T(8,128)S(1)} %get-tuple-element.33.refs_1_.f1_ref.refs_6_, ...), custom_call_target="tpu_custom_call" | custom-call | flops 536870912 | bytes 1048576 | tf_op jit(solution)/shard_map/gram/pallas_call | solution.py:611
  41.3 0.0 collective-permute-done.4.below_ref
  41.3 1.3 %moment.1 = f32[64,2,128]{2,1,0:T(2,128)S(1)} custom-call(f32[2,128]{1,0:T(2,128)S(1)} %gram.1.sums_ref, f32[16,2048]{1,0:T(8,128)S(1)} %collective-permute-done.4.below_ref, f32[16,2048]{1,0:T(8,128)S(1)} %get-tuple-element.39.g1_ref.own_ref.refs_8_, bf16[1,16,768,128]{3,2,1,0:T(8,128)(2,1)S(1)} %get-tuple-element.38.refs_5_.weights_ref), custom_call_target="tpu_custom_call" | custom-call | flops 536870912 | bytes 1048576 | tf_op jit(solution)/shard_map/moment/pallas_call | solution.py:614
  42.6 30.0 %all_to_all.5.refs_2_ = f32[64,2,128]{2,1,0:T(2,128)S(1)} all-to-all(f32[64,2,128]{2,1,0:T(2,128)S(1)} %moment.1), channel_id=1, replica_groups=mesh['hyp'=8,'rows'=64] {'rows'}, dimensions={0} | all-to-all | bytes 131072 | tf_op jit(solution)/shard_map/all_to_all | solution.py:622
  72.6 0.0 copy-done
  72.6 1.5 %finish.1 = (f32[9,4096]{1,0:T(8,128)}, f32[1,9]{1,0:T(1,128)}) custom-call(s32[32]{0:T(128)S(1)} %copy-done, f32[8,128]{1,0:T(8,128)S(1)} %get-tuple-element.23.refs_2_.consts_ref.refs_1_, f32[64,2,128]{2,1,0:T(2,128)S(1)} %all_to_all.5.refs_2_, f32[16,2048]{1,0:T(8,128)S(1)} %get-tuple-element.32.refs_0_.refs_1_.b0_ref.refs_3_, ...), custom_call_target="tpu_custom_call" | custom-call | flops 1048576 | bytes 1048576 | tf_op jit(solution)/shard_map/finish/pallas_call | solution.py:624
Async XLA Ops:
  8.2 10.1 %collective-permute-start.1 = (f32[16,2048]{1,0:T(8,128)S(1)}, f32[16,2048]{1,0:T(8,128)S(1)}, u32[]{:S(2)}, u32[]{:S(2)}) collective-permute-start(f32[16,2048]{1,0:T(8,128)S(1)} %get-tuple-element.32.refs_0_.refs_1_.b0_ref.refs_3_), channel_id=1, source_target_pairs={{1,0},{2,1},{3,2},{4,3},{5,4},{6,5},{7,6},{8,7},{9,8},{10,9},{11,1... | collective-permute-start | bytes 393224 | tf_op jit(solution)/shard_map/ppermute | solution.py:602
  9.5 16.3 %collective-permute-start = (f32[16,2048]{1,0:T(8,128)S(1)}, f32[16,2048]{1,0:T(8,128)S(1)}, u32[]{:S(2)}, u32[]{:S(2)}) collective-permute-start(f32[16,2048]{1,0:T(8,128)S(1)} %get-tuple-element.25.refs_1_.b1_ref.refs_4_), channel_id=1, source_target_pairs={{0,1},{1,2},{2,3},{3,4},{4,5},{5,6},{6,7},{7,8},{8,9},{9,10},{10,1... | collective-permute-start | bytes 393224 | tf_op jit(solution)/shard_map/ppermute | solution.py:599
  22.3 8.9 %collective-permute-start.2 = (f32[16,2048]{1,0:T(8,128)S(1)}, f32[16,2048]{1,0:T(8,128)S(1)}, u32[]{:S(2)}, u32[]{:S(2)}) collective-permute-start(f32[16,2048]{1,0:T(8,128)S(1)} %get-tuple-element.33.refs_1_.f1_ref.refs_6_), channel_id=1, source_target_pairs={{0,1},{1,2},{2,3},{3,4},{4,5},{5,6},{6,7},{7,8},{8,9},{9,10},{10,1... | collective-permute-start | bytes 393224 | tf_op jit(solution)/shard_map/ppermute | solution.py:607
  29.8 6.9 %collective-permute-start.3 = (f32[16,2048]{1,0:T(8,128)S(1)}, f32[16,2048]{1,0:T(8,128)S(1)}, u32[]{:S(2)}, u32[]{:S(2)}) collective-permute-start(f32[16,2048]{1,0:T(8,128)S(1)} %get-tuple-element.31.refs_1_.f0_ref.refs_5_), channel_id=1, source_target_pairs={{1,0},{2,1},{3,2},{4,3},{5,4},{6,5},{7,6},{8,7},{9,8},{10,9},{11,1... | collective-permute-start | bytes 393224 | tf_op jit(solution)/shard_map/ppermute | solution.py:605
  32.9 8.4 %collective-permute-start.4 = (f32[16,2048]{1,0:T(8,128)S(1)}, f32[16,2048]{1,0:T(8,128)S(1)}, u32[]{:S(2)}, u32[]{:S(2)}) collective-permute-start(f32[16,2048]{1,0:T(8,128)S(1)} %get-tuple-element.37.g0_ref.refs_7_), channel_id=1, source_target_pairs={{1,0},{2,1},{3,2},{4,3},{5,4},{6,5},{7,6},{8,7},{9,8},{10,9},{11,1... | collective-permute-start | bytes 393224 | tf_op jit(solution)/shard_map/ppermute | solution.py:610
  38.4 34.2 %copy-start = (s32[32]{0:T(128)S(1)}, s32[32]{0:T(128)}, u32[]{:S(2)}) copy-start(s32[32]{0:T(128)} %refs_0_.1) | copy-start | bytes 388

commit v2 on v1

--- a/solution.py
+++ b/solution.py
@@ -40,8 +40,8 @@
     return jax.ShapeDtypeStruct((ROWS, WIDE), F32)
 
 
-def spread_row():
-    return pltpu.VMEM((2 * ROWS, PAD * 2 * TILE), BF16)
+def spread_row(rows=2 * ROWS):
+    return pltpu.VMEM((rows, PAD * 2 * TILE), BF16)
 
 
 def weight_rows(count):
@@ -163,7 +163,7 @@
         out_ref[tile + 1] = split_rows(values, source).T.astype(BF16)
         return carry
 
-    lax.fori_loop(0, GX, one, 0, unroll=4)
+    lax.fori_loop(0, GX, one, 0, unroll=8)
 
 
 def target_features(row_ref, tile, row_shift, col_shift, factor, rows):
@@ -223,17 +223,38 @@
         spread_tile(row_ref[:, tile * TILE : (tile + 1) * TILE], out_ref, tile)
 
 
+def spread_sides(row_ref, out_ref):
+    empty = jnp.zeros((ROWS, 2 * TILE), BF16)
+    out_ref[:, 0 : 2 * TILE] = empty
+    out_ref[:, (PAD - 1) * 2 * TILE :] = empty
+    row = lax.broadcasted_iota(jnp.int32, (8, TILE), 0)
+    for tile in range(GX):
+        here = slice(tile * TILE, (tile + 1) * TILE)
+        target = row_ref[8:9, here]
+        high = target.astype(BF16).astype(F32)
+        rest = jnp.where(row == 0, high, jnp.where(row == 1, target - high, 0.0))
+        both = jnp.concatenate([row_ref[0:8, here], rest], axis=0).astype(BF16)
+        at = (tile + 1) * 2 * TILE
+        out_ref[:, at : at + 2 * TILE] = jnp.concatenate([both, both], axis=1)
+
+
 def banded(spread_ref, weights_ref, combo, tile):
     at = pl.multiple_of(tile * 2 * TILE, 2 * TILE)
-    both = jnp.dot(
+    return jnp.dot(
         spread_ref[:, pl.ds(at, BAND)],
         weights_ref[combo, tile],
         preferred_element_type=F32,
     )
-    return both[0:ROWS] + both[ROWS:]
-
-
-GROUP = 8
+
+
+def joined(both):
+    if both.shape[0] == 2 * ROWS:
+        return both[0:ROWS] + both[ROWS:]
+    row = lax.broadcasted_iota(jnp.int32, both.shape, 0)
+    return both + jnp.where(row == 8, pltpu.roll(both, ROWS - 1, 0), 0.0)
+
+
+GROUP = 16
 
 
 def apply_row(own_ref, terms, consts_ref, out_ref, out_spread_ref):
@@ -244,9 +265,10 @@
         for j in range(GROUP):
             tile = g * GROUP + j
             here = lanes(tile)
-            total = noise * own_ref[:, here]
-            for term in terms:
-                total = total + banded(*term, tile)
+            both = banded(*terms[0], tile)
+            for term in terms[1:]:
+                both = both + banded(*term, tile)
+            total = noise * own_ref[:, here] + joined(both)
             out_ref[:, here] = total
             spread_tile(total, out_spread_ref, tile)
         return carry
@@ -271,9 +293,9 @@
     return high, a - high
 
 
-def two_product(a, b, a_halves=None, b_halves=None):
-    a1, a2 = halves(a) if a_halves is None else a_halves
-    b1, b2 = halves(b) if b_halves is None else b_halves
+def two_product(a, b):
+    a1, a2 = halves(a)
+    b1, b2 = halves(b)
     product = a * b
     return product, ((a1 * b1 - product) + a1 * b2 + a2 * b1) + a2 * b2
 
@@ -313,10 +335,9 @@
     return lane == row + ROWS * k
 
 
-def add_product(sums, a, b, a_halves, b_halves):
-    product, error = two_product(a, b, a_halves, b_halves)
-    total, left = two_sum(sums[0], product)
-    return total, sums[1] + (left + error)
+def accumulate(sums, term):
+    total, left = two_sum(sums[0], term)
+    return total, sums[1] + left
 
 
 def lines(sums, first):
@@ -331,13 +352,17 @@
     return [jnp.sum(p, axis=0, keepdims=True) for p in placed]
 
 
-def inner_kernel(slot, first_ref, second_ref, consts_ref, weights_ref, spread_ref, feats_ref):
+def inner_kernel(
+    first_ref, second_ref, consts_ref, left_ref, right_ref, spread0_ref, spread1_ref, feats_ref
+):
     rows = feature_rows()
-    own_ref = (first_ref, second_ref)[slot]
-    source_features(own_ref, constant(consts_ref, FACTOR), rows, feats_ref)
-    fill_weights(first_ref, slot, feats_ref, weights_ref, 0, consts_ref, rows)
-    fill_weights(second_ref, slot - 1, feats_ref, weights_ref, 1, consts_ref, rows)
-    spread(own_ref, spread_ref)
+    for slot, (own_ref, weights_ref, spread_ref) in enumerate(
+        ((first_ref, left_ref, spread0_ref), (second_ref, right_ref, spread1_ref))
+    ):
+        source_features(own_ref, constant(consts_ref, FACTOR), rows, feats_ref)
+        fill_weights(first_ref, slot, feats_ref, weights_ref, 0, consts_ref, rows)
+        fill_weights(second_ref, slot - 1, feats_ref, weights_ref, 1, consts_ref, rows)
+        spread_sides(own_ref, spread_ref)
 
 
 def outer_kernel(
@@ -358,13 +383,12 @@
     rows = feature_rows()
     source_features(other_ref, constant(consts_ref, FACTOR), rows, feats_ref)
     fill_weights(own_ref, 2 * slot - 1, feats_ref, weights_ref, 0, consts_ref, rows)
-    spread(other_ref, spread_ref)
+    spread_sides(other_ref, spread_ref)
     terms = ((spread_ref, weights_ref, 0), (spread0_ref, left_ref, slot), (spread1_ref, right_ref, slot))
     apply_row(own_ref, terms, consts_ref, out_ref, out_spread_ref)
 
 
 def product_kernel(
-    slot,
     other_ref,
     own_ref,
     consts_ref,
@@ -378,66 +402,73 @@
     spread_ref,
 ):
     spread(other_ref, spread_ref)
-    terms = ((spread_ref, weights_ref, 0), (spread0_ref, left_ref, slot), (spread1_ref, right_ref, slot))
+    terms = ((spread_ref, weights_ref, 0), (spread0_ref, left_ref, 0), (spread1_ref, right_ref, 0))
     apply_row(own_ref, terms, consts_ref, out_ref, out_spread_ref)
 
 
 def gram_kernel(
+    below_ref,
     b0_ref,
     b1_ref,
     f0_ref,
     f1_ref,
     g0_ref,
-    g1_ref,
     consts_ref,
     left_ref,
     right_ref,
-    spread0_ref,
-    spread1_ref,
+    under_ref,
+    f0_spread_ref,
+    f1_spread_ref,
+    g0_spread_ref,
+    g1_ref,
     sums_ref,
+    spread_ref,
+    g1_spread_ref,
 ):
+    spread(below_ref, spread_ref)
+    terms = ((spread_ref, under_ref, 0), (f0_spread_ref, left_ref, 1), (f1_spread_ref, right_ref, 1))
+    apply_row(f1_ref, terms, consts_ref, g1_ref, g1_spread_ref)
     zero = jnp.zeros((ROWS, TILE), F32)
     noise = constant(consts_ref, NOISE)
 
     def group(g, sums):
         sums = list(sums)
-        for j in range(4):
-            tile = g * 4 + j
+        terms = [zero] * 7
+        for j in range(8):
+            tile = g * 8 + j
             here = lanes(tile)
             for half, refs in enumerate(((b0_ref, f0_ref, g0_ref), (b1_ref, f1_ref, g1_ref))):
-                values = [ref[:, here] for ref in refs]
-                parts = [halves(v) for v in values]
-                for k, (i, j2) in enumerate(((0, 0), (0, 1), (0, 2), (1, 1), (1, 2), (2, 2))):
-                    sums[k] = add_product(sums[k], values[i], values[j2], parts[i], parts[j2])
-                image = noise * values[2]
+                v = [ref[:, here] for ref in refs]
+                for k, (i, m) in enumerate(((0, 0), (0, 1), (0, 2), (1, 1), (1, 2), (2, 2))):
+                    terms[k] = terms[k] + v[i] * v[m]
                 if half == 0:
-                    image = image + banded(spread0_ref, left_ref, 0, tile)
-                    image = image + 2.0 * banded(spread1_ref, right_ref, 0, tile)
+                    both = banded(g0_spread_ref, left_ref, 0, tile)
+                    both = both + 2.0 * banded(g1_spread_ref, right_ref, 0, tile)
                 else:
-                    image = image + banded(spread1_ref, right_ref, 1, tile)
-                sums[6] = add_product(sums[6], values[2], image, parts[2], halves(image))
+                    both = banded(g1_spread_ref, right_ref, 1, tile)
+                terms[6] = terms[6] + v[2] * (noise * v[2] + joined(both))
+            if j % 2 == 1:
+                sums = [accumulate(s, t) for s, t in zip(sums, terms)]
+                terms = [zero] * 7
         return tuple(sums)
 
-    high, low = lines(lax.fori_loop(0, GX // 4, group, ((zero, zero),) * 7), 0)
+    high, low = lines(lax.fori_loop(0, GX // 8, group, ((zero, zero),) * 7), 0)
     sums_ref[0:1, :] = high
     sums_ref[1:2, :] = low
 
 
 def moment_kernel(sums_ref, below_ref, own_ref, weights_ref, out_ref, spread_ref):
     spread(below_ref, spread_ref)
-
-    def group(g, sums):
-        for j in range(GROUP):
-            tile = g * GROUP + j
-            v = own_ref[:, lanes(tile)]
-            image = 2.0 * banded(spread_ref, weights_ref, 0, tile)
-            sums = add_product(sums, v, image, halves(v), halves(image))
-        return sums
-
     zero = jnp.zeros((ROWS, TILE), F32)
-    high, low = lines((lax.fori_loop(0, GX // GROUP, group, (zero, zero)),), 6)
+    sums, term = (zero, zero), zero
+    for tile in range(GX):
+        image = joined(banded(spread_ref, weights_ref, 0, tile))
+        term = term + own_ref[:, tile * TILE : (tile + 1) * TILE] * (2.0 * image)
+        if tile % 4 == 3:
+            sums, term = accumulate(sums, term), zero
+    high, low = lines((sums,), 6)
     total, left = two_sum(sums_ref[0:1, :], high)
-    both = jnp.concatenate([total, left + (low + sums_ref[1:2, :])], axis=0)
+    both = jnp.concatenate([total, left + (low + sums_ref[1:2, :])], axis=1)
     out_ref[...] = jnp.broadcast_to(both[None], out_ref.shape)
 
 
@@ -460,7 +491,7 @@
 ):
     copy = pltpu.make_async_copy(cell_hbm, cell_ref, sem)
     copy.start()
-    high, low = parts_ref[:, 0, :], parts_ref[:, 1, :]
+    high, low = parts_ref[:, 0, 0:TILE], parts_ref[:, 0, TILE:]
     while high.shape[0] > 8:
         half = high.shape[0] // 2
         high, left = two_sum(high[:half], high[half:])
@@ -566,55 +597,51 @@
         noise,
     )
 
-    def inner(slot):
-        return call(
-            lambda *refs: inner_kernel(slot, *refs),
-            f"inner{slot}",
-            (weight_rows(2), spread_row()),
-            [VMEM] * 3,
-            [feature_tiles()],
-            flops=1 << 30,
-        )(first, second, consts)
-
     def outer(slot, other, own):
         return call(
             lambda *refs: outer_kernel(slot, *refs),
             f"outer{slot}",
             (weight_rows(1), grid_row(), spread_row()),
             [VMEM] * 7,
-            [feature_tiles(), spread_row()],
+            [feature_tiles(), spread_row(ROWS)],
             flops=1 << 30,
         )(other, own, consts, left, right, b0_spread, b1_spread)
 
-    def product(slot, other, own, weights):
-        return call(
-            lambda *refs: product_kernel(slot, *refs),
-            f"product{slot}",
-            (grid_row(), spread_row()),
-            [VMEM] * 8,
-            [spread_row()],
-            flops=1 << 29,
-        )(other, own, consts, left, right, weights, f0_spread, f1_spread)
-
     above = lax.ppermute(second, "rows", down)
-    left, b0_spread = inner(0)
-    gated, left = lax.optimization_barrier((first, left))
-    below = lax.ppermute(gated, "rows", up)
-    right, b1_spread = inner(1)
+    below = lax.ppermute(first, "rows", up)
+    left, right, b0_spread, b1_spread = call(
+        inner_kernel,
+        "inner",
+        (weight_rows(2), weight_rows(2), spread_row(ROWS), spread_row(ROWS)),
+        [VMEM] * 3,
+        [feature_tiles()],
+        flops=1 << 30,
+    )(first, second, consts)
     over, f0, f0_spread = outer(0, above, first)
     f_below = lax.ppermute(f0, "rows", up)
     under, f1, f1_spread = outer(1, below, second)
     f_above = lax.ppermute(f1, "rows", down)
-    g1, g1_spread = product(1, f_below, f1, under)
-    g0, g0_spread = product(0, f_above, f0, over)
+    g0, g0_spread = call(
+        product_kernel,
+        "product",
+        (grid_row(), spread_row()),
+        [VMEM] * 8,
+        [spread_row()],
+        flops=1 << 29,
+    )(f_above, f0, consts, left, right, over, f0_spread, f1_spread)
     g_below = lax.ppermute(g0, "rows", up)
-    sums = call(
-        gram_kernel, "gram", jax.ShapeDtypeStruct((2, TILE), F32), [VMEM] * 11, flops=1 << 29
-    )(first, second, f0, f1, g0, g1, consts, left, right, g0_spread, g1_spread)
+    g1, sums = call(
+        gram_kernel,
+        "gram",
+        (grid_row(), jax.ShapeDtypeStruct((2, TILE), F32)),
+        [VMEM] * 13,
+        [spread_row(), spread_row()],
+        flops=1 << 29,
+    )(f_below, first, second, f0, f1, g0, consts, left, right, under, f0_spread, f1_spread, g0_spread)
     parts = call(
         moment_kernel,
         "moment",
-        jax.ShapeDtypeStruct((size, 2, TILE), F32),
+        jax.ShapeDtypeStruct((size, 1, 2 * TILE), F32),
         [VMEM] * 4,
         [spread_row()],
         flops=1 << 29,

time: 74.4 us -> 72.8 us (0.978)
  Pallas kernels: 26.9 us -> 24.4 us
    pallas_call x6 -> x4, Pallas kernels: 16 us -> 14.5 us  [the longest x1 7.99 us: shards(): call(inner_kernel, 'inner', (weight_rows(2), weight_rows(2), spread_row(R...]
    pallas_call x2, Pallas kernels: 8.1 us -> 7.14 us  [outer(): call(lambda *refs: outer_kernel(slot, *refs), f'outer{slot}', (weight_row...]
  transfers between devices with their start and end apart: 5 -> 5, of which waited for: 1 -> 1; matrix products, arithmetic and copies ran while one was open for 0% -> 0% of each run, Pallas kernels for 25% -> 28%
where the time goes in v2:
time: 72.8 us; the launch traced here: 72.5 us
  blocking collectives  30.6 us (42%)
  Pallas kernels  24.4 us (34%)
  starting transfers between devices  12.1 us (17%)
  between operations  2.85 us (4%)
  waiting for transfers between devices  2.5 us (3%)
    all_to_all x1, blocking collectives, shards(): lax.all_to_all(parts, 'rows', split_axis=0, concat_axis=0, tiled=True)  30.6 us
    pallas_call x1, Pallas kernels, shards(): call(inner_kernel, 'inner', (weight_rows(2), weight_rows(2), spread_row(R...  7.99 us
    pallas_call x2, Pallas kernels, outer(): call(lambda *refs: outer_kernel(slot, *refs), f'outer{slot}', (weight_row...  7.14 us
    ppermute x1, starting transfers between devices, shards(): above = lax.ppermute(second, 'rows', down)  4.55 us
    pallas_call x1, Pallas kernels, shards(): call(gram_kernel, 'gram', (grid_row(), jax.ShapeDtypeStruct((2, TILE), F3...  3.81 us
    ppermute x1, starting transfers between devices, shards(): f_above = lax.ppermute(f1, 'rows', down)  3.49 us
    ppermute x1, waiting for transfers between devices, shards(): f_below = lax.ppermute(f0, 'rows', up)  2.49 us
    pallas_call x1, Pallas kernels, shards(): call(product_kernel, 'product', (grid_row(), spread_row()), [VMEM] * 8, [...  1.57 us
  transfers between devices with their start and end apart: 5, of which 1 were waited for; matrix products, arithmetic and copies ran while one was open for 0% of the time, Pallas kernels for 28%

profile of v2, /device:TPU:2, one launch (start us, length us, event | category | flops | bytes accessed | tf_op | source)
XLA Modules:
  0.0 72.5 jit_solution(6970279001277568031)
XLA Ops:
  2.6 1.4 %pack.1 = (f32[16,2048]{1,0:T(8,128)S(1)}, f32[16,2048]{1,0:T(8,128)S(1)}, f32[8,128]{1,0:T(8,128)S(1)}) custom-call(s32[32]{0:T(128)} %refs_0_.1, f32[2,4096]{1,0:T(2,128)} %offsets_hbm.1, s32[8,4096]{1,0:T(8,128)} %probes_hbm.1, f32[1,4096]{1,0:T(1,128)} %bitcast.2, f32[1]{0:T(128)S(6)} %copy.9.scale_ref, f32[1]{0:T(128)S(6)} %copy.10.amp_ref, ...), custom_call_target="tpu_custom_call" | custom-call | flops 1048576 | bytes 1048576 | tf_op jit(solution)/shard_map/pack/pallas_call | solution.py:576
  4.0 1.3 %collective-permute-start.2 = (f32[16,2048]{1,0:T(8,128)S(1)}, f32[16,2048]{1,0:T(8,128)S(1)}, u32[]{:S(2)}, u32[]{:S(2)}) collective-permute-start(f32[16,2048]{1,0:T(8,128)S(1)} %get-tuple-element.23.first_ref.refs_1_.b0_ref.refs_3_), channel_id=1, source_target_pairs={{1,0},{2,1},{3,2},{4,3},{5,4},{6,5},{7,6},{8,7},{9,8},{10,9},{11,1... | collective-permute-start | bytes 393224 | tf_op jit(solution)/shard_map/ppermute | solution.py:611
  5.3 4.6 %collective-permute-start = (f32[16,2048]{1,0:T(8,128)S(1)}, f32[16,2048]{1,0:T(8,128)S(1)}, u32[]{:S(2)}, u32[]{:S(2)}) collective-permute-start(f32[16,2048]{1,0:T(8,128)S(1)} %get-tuple-element.22.second_ref.refs_1_.b1_ref.refs_4_), channel_id=1, source_target_pairs={{0,1},{1,2},{2,3},{3,4},{4,5},{5,6},{6,7},{7,8},{8,9},{9,10},{10,1... | collective-permute-start | bytes 393224 | tf_op jit(solution)/shard_map/ppermute | solution.py:610
  9.8 8.0 %inner.1 = (bf16[2,16,768,128]{3,2,1,0:T(8,128)(2,1)S(1)}, bf16[2,16,768,128]{3,2,1,0:T(8,128)(2,1)S(1)}, bf16[16,4608]{1,0:T(8,128)(2,1)S(1)}, bf16[16,4608]{1,0:T(8,128)(2,1)S(1)}) custom-call(f32[16,2048]{1,0:T(8,128)S(1)} %get-tuple-element.23.first_ref.refs_1_.b0_ref.refs_3_, f32[16,2048]{1,0:T(8,128)S(1)} %get-tuple-element.22.second_ref.refs_1_.b1_ref.refs_4_, ...), custom_call_target="tpu_custom_call" | custom-call | flops 1073741824 | bytes 1048576 | tf_op jit(solution)/shard_map/inner/pallas_call | solution.py:612
  17.8 0.0 collective-permute-done.2.refs_0_
  17.8 3.6 %outer1.1 = (bf16[1,16,768,128]{3,2,1,0:T(8,128)(2,1)S(1)}, f32[16,2048]{1,0:T(8,128)S(1)}, bf16[32,4608]{1,0:T(8,128)(2,1)S(1)}) custom-call(f32[16,2048]{1,0:T(8,128)S(1)} %collective-permute-done.2.refs_0_, f32[16,2048]{1,0:T(8,128)S(1)} %get-tuple-element.22.second_ref.refs_1_.b1_ref.refs_4_, f32[8,128]{1,0:T(8,128)S(1)} %get-tuple-element.21.consts_ref.refs_2_.refs_1_, ...), custom_call_target="tpu_custom_call" | custom-call | flops 1073741824 | bytes 1048576 | tf_op jit(solution)/shard_map/outer1/pallas_call | solution.py:601
  21.4 3.5 %collective-permute-start.3 = (f32[16,2048]{1,0:T(8,128)S(1)}, f32[16,2048]{1,0:T(8,128)S(1)}, u32[]{:S(2)}, u32[]{:S(2)}) collective-permute-start(f32[16,2048]{1,0:T(8,128)S(1)} %get-tuple-element.29.f1_ref.refs_6_), channel_id=1, source_target_pairs={{0,1},{1,2},{2,3},{3,4},{4,5},{5,6},{6,7},{7,8},{8,9},{9,10},{10,1... | collective-permute-start | bytes 393224 | tf_op jit(solution)/shard_map/ppermute | solution.py:623
  24.9 0.0 collective-permute-done.refs_0_
  24.9 3.6 %outer0.1 = (bf16[1,16,768,128]{3,2,1,0:T(8,128)(2,1)S(1)}, f32[16,2048]{1,0:T(8,128)S(1)}, bf16[32,4608]{1,0:T(8,128)(2,1)S(1)}) custom-call(f32[16,2048]{1,0:T(8,128)S(1)} %collective-permute-done.refs_0_, f32[16,2048]{1,0:T(8,128)S(1)} %get-tuple-element.23.first_ref.refs_1_.b0_ref.refs_3_, f32[8,128]{1,0:T(8,128)S(1)} %get-tuple-element.21.consts_ref.refs_2_.refs_1_, ...), custom_call_target="tpu_custom_call" | custom-call | flops 1073741824 | bytes 1048576 | tf_op jit(solution)/shard_map/outer0/pallas_call | solution.py:601
  28.5 1.3 %collective-permute-start.1 = (f32[16,2048]{1,0:T(8,128)S(1)}, f32[16,2048]{1,0:T(8,128)S(1)}, u32[]{:S(2)}, u32[]{:S(2)}) collective-permute-start(f32[16,2048]{1,0:T(8,128)S(1)} %get-tuple-element.28.own_ref.f0_ref.refs_5_), channel_id=1, source_target_pairs={{1,0},{2,1},{3,2},{4,3},{5,4},{6,5},{7,6},{8,7},{9,8},{10,9},{11,1... | collective-permute-start | bytes 393224 | tf_op jit(solution)/shard_map/ppermute | solution.py:621
  29.8 0.0 collective-permute-done.3.other_ref
  29.8 1.6 %product.1 = (f32[16,2048]{1,0:T(8,128)S(1)}, bf16[32,4608]{1,0:T(8,128)(2,1)S(1)}) custom-call(f32[16,2048]{1,0:T(8,128)S(1)} %collective-permute-done.3.other_ref, f32[16,2048]{1,0:T(8,128)S(1)} %get-tuple-element.28.own_ref.f0_ref.refs_5_, f32[8,128]{1,0:T(8,128)S(1)} %get-tuple-element.21.consts_ref.refs_2_.refs_1_, ...), custom_call_target="tpu_custom_call" | custom-call | flops 536870912 | bytes 1048576 | tf_op jit(solution)/shard_map/product/pallas_call | solution.py:624
  31.4 1.5 %collective-permute-start.4 = (f32[16,2048]{1,0:T(8,128)S(1)}, f32[16,2048]{1,0:T(8,128)S(1)}, u32[]{:S(2)}, u32[]{:S(2)}) collective-permute-start(f32[16,2048]{1,0:T(8,128)S(1)} %get-tuple-element.33.g0_ref.refs_7_), channel_id=1, source_target_pairs={{1,0},{2,1},{3,2},{4,3},{5,4},{6,5},{7,6},{8,7},{9,8},{10,9},{11,1... | collective-permute-start | bytes 393224 | tf_op jit(solution)/shard_map/ppermute | solution.py:632
  32.9 2.5 %collective-permute-done.1.below_ref = f32[16,2048]{1,0:T(8,128)S(1)} collective-permute-done((f32[16,2048]{1,0:T(8,128)S(1)}, f32[16,2048]{1,0:T(8,128)S(1)}, u32[]{:S(2)}, u32[]{:S(2)}) %collective-permute-start.1) | collective-permute-done | bytes 131104 | tf_op jit(solution)/shard_map/ppermute | solution.py:621
  35.4 0.0 copy-start
  35.4 3.8 %gram.1 = (f32[16,2048]{1,0:T(8,128)S(1)}, f32[2,128]{1,0:T(2,128)S(1)}) custom-call(f32[16,2048]{1,0:T(8,128)S(1)} %collective-permute-done.1.below_ref, f32[16,2048]{1,0:T(8,128)S(1)} %get-tuple-element.23.first_ref.refs_1_.b0_ref.refs_3_, f32[16,2048]{1,0:T(8,128)S(1)} %get-tuple-element.22.second_ref.refs_1_.b1_ref.refs_4_, ...), custom_call_target="tpu_custom_call" | custom-call | flops 536870912 | bytes 1048576 | tf_op jit(solution)/shard_map/gram/pallas_call | solution.py:633
  39.2 0.0 collective-permute-done.4.below_ref
  39.2 1.1 %moment.1 = f32[64,1,256]{2,1,0:T(1,128)S(1)} custom-call(f32[2,128]{1,0:T(2,128)S(1)} %get-tuple-element.36.sums_ref, f32[16,2048]{1,0:T(8,128)S(1)} %collective-permute-done.4.below_ref, f32[16,2048]{1,0:T(8,128)S(1)} %get-tuple-element.37.own_ref.refs_8_, bf16[1,16,768,128]{3,2,1,0:T(8,128)(2,1)S(1)} %get-tuple-element.34.under_ref.weights_ref), custom_call_target="tpu_custom_call" | custom-call | flops 536870912 | bytes 1048576 | tf_op jit(solution)/shard_map/moment/pallas_call | solution.py:641
  40.3 30.6 %all_to_all.5.refs_2_ = f32[64,1,256]{2,1,0:T(1,128)S(1)} all-to-all(f32[64,1,256]{2,1,0:T(1,128)S(1)} %moment.1), channel_id=1, replica_groups=mesh['hyp'=8,'rows'=64] {'rows'}, dimensions={0} | all-to-all | bytes 131072 | tf_op jit(solution)/shard_map/all_to_all | solution.py:649
  70.9 0.0 copy-done
  70.9 1.5 %finish.1 = (f32[9,4096]{1,0:T(8,128)}, f32[1,9]{1,0:T(1,128)}) custom-call(s32[32]{0:T(128)S(1)} %copy-done, f32[8,128]{1,0:T(8,128)S(1)} %get-tuple-element.21.consts_ref.refs_2_.refs_1_, f32[64,1,256]{2,1,0:T(1,128)S(1)} %all_to_all.5.refs_2_, f32[16,2048]{1,0:T(8,128)S(1)} %get-tuple-element.23.first_ref.refs_1_.b0_ref.refs_3_, ...), custom_call_target="tpu_custom_call" | custom-call | flops 1048576 | bytes 1048576 | tf_op jit(solution)/shard_map/finish/pallas_call | solution.py:651
Async XLA Ops:
  4.0 13.9 %collective-permute-start.2 = (f32[16,2048]{1,0:T(8,128)S(1)}, f32[16,2048]{1,0:T(8,128)S(1)}, u32[]{:S(2)}, u32[]{:S(2)}) collective-permute-start(f32[16,2048]{1,0:T(8,128)S(1)} %get-tuple-element.23.first_ref.refs_1_.b0_ref.refs_3_), channel_id=1, source_target_pairs={{1,0},{2,1},{3,2},{4,3},{5,4},{6,5},{7,6},{8,7},{9,8},{10,9},{11,1... | collective-permute-start | bytes 393224 | tf_op jit(solution)/shard_map/ppermute | solution.py:611
  5.3 19.6 %collective-permute-start = (f32[16,2048]{1,0:T(8,128)S(1)}, f32[16,2048]{1,0:T(8,128)S(1)}, u32[]{:S(2)}, u32[]{:S(2)}) collective-permute-start(f32[16,2048]{1,0:T(8,128)S(1)} %get-tuple-element.22.second_ref.refs_1_.b1_ref.refs_4_), channel_id=1, source_target_pairs={{0,1},{1,2},{2,3},{3,4},{4,5},{5,6},{6,7},{7,8},{8,9},{9,10},{10,1... | collective-permute-start | bytes 393224 | tf_op jit(solution)/shard_map/ppermute | solution.py:610
  21.4 8.4 %collective-permute-start.3 = (f32[16,2048]{1,0:T(8,128)S(1)}, f32[16,2048]{1,0:T(8,128)S(1)}, u32[]{:S(2)}, u32[]{:S(2)}) collective-permute-start(f32[16,2048]{1,0:T(8,128)S(1)} %get-tuple-element.29.f1_ref.refs_6_), channel_id=1, source_target_pairs={{0,1},{1,2},{2,3},{3,4},{4,5},{5,6},{6,7},{7,8},{8,9},{9,10},{10,1... | collective-permute-start | bytes 393224 | tf_op jit(solution)/shard_map/ppermute | solution.py:623
  28.5 6.9 %collective-permute-start.1 = (f32[16,2048]{1,0:T(8,128)S(1)}, f32[16,2048]{1,0:T(8,128)S(1)}, u32[]{:S(2)}, u32[]{:S(2)}) collective-permute-start(f32[16,2048]{1,0:T(8,128)S(1)} %get-tuple-element.28.own_ref.f0_ref.refs_5_), channel_id=1, source_target_pairs={{1,0},{2,1},{3,2},{4,3},{5,4},{6,5},{7,6},{8,7},{9,8},{10,9},{11,1... | collective-permute-start | bytes 393224 | tf_op jit(solution)/shard_map/ppermute | solution.py:621
  31.4 7.8 %collective-permute-start.4 = (f32[16,2048]{1,0:T(8,128)S(1)}, f32[16,2048]{1,0:T(8,128)S(1)}, u32[]{:S(2)}, u32[]{:S(2)}) collective-permute-start(f32[16,2048]{1,0:T(8,128)S(1)} %get-tuple-element.33.g0_ref.refs_7_), channel_id=1, source_target_pairs={{1,0},{2,1},{3,2},{4,3},{5,4},{6,5},{7,6},{8,7},{9,8},{10,9},{11,1... | collective-permute-start | bytes 393224 | tf_op jit(solution)/shard_map/ppermute | solution.py:632
  35.4 35.5 %copy-start = (s32[32]{0:T(128)S(1)}, s32[32]{0:T(128)}, u32[]{:S(2)}) copy-start(s32[32]{0:T(128)} %refs_0_.1) | copy-start | bytes 388

commit v3 on v2

--- a/solution.py
+++ b/solution.py
@@ -257,7 +257,7 @@
 GROUP = 16
 
 
-def apply_row(own_ref, terms, consts_ref, out_ref, out_spread_ref):
+def apply_row(own_ref, terms, consts_ref, out_ref, out_spread_ref, beside_ref=None):
     noise = constant(consts_ref, NOISE)
     spread_ends(out_spread_ref)
 
@@ -266,6 +266,8 @@
             tile = g * GROUP + j
             here = lanes(tile)
             both = banded(*terms[0], tile)
+            if beside_ref is not None:
+                beside_ref[:, here] = joined(both)
             for term in terms[1:]:
                 both = both + banded(*term, tile)
             total = noise * own_ref[:, here] + joined(both)
@@ -329,10 +331,14 @@
         return Pair(jnp.where(keep, self.high, other.high), jnp.where(keep, self.low, other.low))
 
 
+SUMS = 9
+STRIDE = TILE // SUMS
+
+
 def grid_mask(k):
     lane = lax.broadcasted_iota(jnp.int32, (ROWS, TILE), 1)
     row = lax.broadcasted_iota(jnp.int32, (ROWS, TILE), 0)
-    return lane == row + ROWS * k
+    return (lane == row + STRIDE * k) & (row < RHS)
 
 
 def accumulate(sums, term):
@@ -377,6 +383,7 @@
     weights_ref,
     out_ref,
     out_spread_ref,
+    beside_ref,
     feats_ref,
     spread_ref,
 ):
@@ -385,7 +392,7 @@
     fill_weights(own_ref, 2 * slot - 1, feats_ref, weights_ref, 0, consts_ref, rows)
     spread_sides(other_ref, spread_ref)
     terms = ((spread_ref, weights_ref, 0), (spread0_ref, left_ref, slot), (spread1_ref, right_ref, slot))
-    apply_row(own_ref, terms, consts_ref, out_ref, out_spread_ref)
+    apply_row(own_ref, terms, consts_ref, out_ref, out_spread_ref, beside_ref)
 
 
 def product_kernel(
@@ -413,6 +420,7 @@
     f0_ref,
     f1_ref,
     g0_ref,
+    b_beside_ref,
     consts_ref,
     left_ref,
     right_ref,
@@ -424,16 +432,17 @@
     sums_ref,
     spread_ref,
     g1_spread_ref,
+    f_beside_ref,
 ):
     spread(below_ref, spread_ref)
     terms = ((spread_ref, under_ref, 0), (f0_spread_ref, left_ref, 1), (f1_spread_ref, right_ref, 1))
-    apply_row(f1_ref, terms, consts_ref, g1_ref, g1_spread_ref)
+    apply_row(f1_ref, terms, consts_ref, g1_ref, g1_spread_ref, f_beside_ref)
     zero = jnp.zeros((ROWS, TILE), F32)
     noise = constant(consts_ref, NOISE)
 
     def group(g, sums):
         sums = list(sums)
-        terms = [zero] * 7
+        terms = [zero] * SUMS
         for j in range(8):
             tile = g * 8 + j
             here = lanes(tile)
@@ -441,32 +450,36 @@
                 v = [ref[:, here] for ref in refs]
                 for k, (i, m) in enumerate(((0, 0), (0, 1), (0, 2), (1, 1), (1, 2), (2, 2))):
                     terms[k] = terms[k] + v[i] * v[m]
-                if half == 0:
-                    both = banded(g0_spread_ref, left_ref, 0, tile)
-                    both = both + 2.0 * banded(g1_spread_ref, right_ref, 0, tile)
-                else:
-                    both = banded(g1_spread_ref, right_ref, 1, tile)
-                terms[6] = terms[6] + v[2] * (noise * v[2] + joined(both))
+                both = banded(g0_spread_ref, left_ref, half, tile)
+                both = both + banded(g1_spread_ref, right_ref, half, tile)
+                image = noise * v[2] + joined(both)
+                for k in range(3):
+                    terms[6 + k] = terms[6 + k] + v[k] * image
+                if half == 1:
+                    terms[6] = terms[6] + v[2] * b_beside_ref[:, here]
+                    terms[7] = terms[7] + v[2] * f_beside_ref[:, here]
             if j % 2 == 1:
                 sums = [accumulate(s, t) for s, t in zip(sums, terms)]
-                terms = [zero] * 7
+                terms = [zero] * SUMS
         return tuple(sums)
 
-    high, low = lines(lax.fori_loop(0, GX // 8, group, ((zero, zero),) * 7), 0)
+    high, low = lines(lax.fori_loop(0, GX // 8, group, ((zero, zero),) * SUMS), 0)
     sums_ref[0:1, :] = high
     sums_ref[1:2, :] = low
 
 
-def moment_kernel(sums_ref, below_ref, own_ref, weights_ref, out_ref, spread_ref):
+def moment_kernel(sums_ref, below_ref, b_ref, f_ref, g_ref, weights_ref, out_ref, spread_ref):
     spread(below_ref, spread_ref)
     zero = jnp.zeros((ROWS, TILE), F32)
-    sums, term = (zero, zero), zero
+    sums, terms = [(zero, zero)] * 3, [zero] * 3
     for tile in range(GX):
+        here = slice(tile * TILE, (tile + 1) * TILE)
         image = joined(banded(spread_ref, weights_ref, 0, tile))
-        term = term + own_ref[:, tile * TILE : (tile + 1) * TILE] * (2.0 * image)
+        factors = (b_ref[:, here], f_ref[:, here], 2.0 * g_ref[:, here])
+        terms = [t + v * image for t, v in zip(terms, factors)]
         if tile % 4 == 3:
-            sums, term = accumulate(sums, term), zero
-    high, low = lines((sums,), 6)
+            sums, terms = [accumulate(s, t) for s, t in zip(sums, terms)], [zero] * 3
+    high, low = lines(sums, 6)
     total, left = two_sum(sums_ref[0:1, :], high)
     both = jnp.concatenate([total, left + (low + sums_ref[1:2, :])], axis=1)
     out_ref[...] = jnp.broadcast_to(both[None], out_ref.shape)
@@ -500,11 +513,11 @@
         high, left = two_sum(high, pltpu.roll(high, shift, 0))
         low = (low + pltpu.roll(low, shift, 0)) + left
     high, low = quick_sum(high, low)
-    bb, bf, bg, ff, fg, gg, gag = (
+    bb, bf, bg, ff, fg, gg, bag, fag, gag = (
         Pair(high, low)
         if k == 0
-        else Pair(pltpu.roll(high, TILE - ROWS * k, 1), pltpu.roll(low, TILE - ROWS * k, 1))
-        for k in range(7)
+        else Pair(pltpu.roll(high, TILE - STRIDE * k, 1), pltpu.roll(low, TILE - STRIDE * k, 1))
+        for k in range(SUMS)
     )
     zero = jnp.zeros_like(high)
     none = Pair(zero, zero)
@@ -533,9 +546,7 @@
     q0, q1, q2 = one + beta1 * p0, r1 + beta1 * p1, r2
     alpha2, good2 = step(
         rr2,
-        q0 * (q0 * bf + q1 * (bg + ff) + q2 * fg * 2.0)
-        + q1 * (q1 * fg + q2 * gg * 2.0)
-        + q2 * q2 * gag,
+        q0 * (q0 * bf + q1 * (bg + ff) + q2 * (fg + bag)) + q1 * (q1 * fg + q2 * (gg + fag)) + q2 * q2 * gag,
     )
     alpha2 = alpha2.where(good1, none)
     on_b = alpha0 + alpha1 * p0 + alpha2 * q0
@@ -601,7 +612,7 @@
         return call(
             lambda *refs: outer_kernel(slot, *refs),
             f"outer{slot}",
-            (weight_rows(1), grid_row(), spread_row()),
+            (weight_rows(1), grid_row(), spread_row(), grid_row()),
             [VMEM] * 7,
             [feature_tiles(), spread_row(ROWS)],
             flops=1 << 30,
@@ -617,9 +628,9 @@
         [feature_tiles()],
         flops=1 << 30,
     )(first, second, consts)
-    over, f0, f0_spread = outer(0, above, first)
+    over, f0, f0_spread, _ = outer(0, above, first)
     f_below = lax.ppermute(f0, "rows", up)
-    under, f1, f1_spread = outer(1, below, second)
+    under, f1, f1_spread, b_beside = outer(1, below, second)
     f_above = lax.ppermute(f1, "rows", down)
     g0, g0_spread = call(
         product_kernel,
@@ -634,18 +645,18 @@
         gram_kernel,
         "gram",
         (grid_row(), jax.ShapeDtypeStruct((2, TILE), F32)),
-        [VMEM] * 13,
-        [spread_row(), spread_row()],
+        [VMEM] * 14,
+        [spread_row(), spread_row(), pltpu.VMEM((ROWS, WIDE), F32)],
         flops=1 << 29,
-    )(f_below, first, second, f0, f1, g0, consts, left, right, under, f0_spread, f1_spread, g0_spread)
+    )(f_below, first, second, f0, f1, g0, b_beside, consts, left, right, under, f0_spread, f1_spread, g0_spread)
     parts = call(
         moment_kernel,
         "moment",
         jax.ShapeDtypeStruct((size, 1, 2 * TILE), F32),
-        [VMEM] * 4,
+        [VMEM] * 6,
         [spread_row()],
         flops=1 << 29,
-    )(sums, g_below, g1, under)
+    )(sums, g_below, second, f1, g1, under)
     parts = lax.all_to_all(parts, "rows", split_axis=0, concat_axis=0, tiled=True)
 
     solutions, quad = call(

time: 72.8 us -> 73.4 us (level)
  Pallas kernels: 24.4 us -> 25.5 us
  transfers between devices with their start and end apart: 5 -> 5, of which waited for: 1 -> 1; matrix products, arithmetic and copies ran while one was open for 0% -> 0% of each run, Pallas kernels for 28% -> 30%
where the time goes in v3:
time: 73.4 us; the launch traced here: 73.1 us
  blocking collectives  30.2 us (41%)
  Pallas kernels  25.5 us (35%)
  starting transfers between devices  12.1 us (16%)
  between operations  2.85 us (4%)
  waiting for transfers between devices  2.5 us (3%)
    all_to_all x1, blocking collectives, shards(): lax.all_to_all(parts, 'rows', split_axis=0, concat_axis=0, tiled=True)  30.2 us
    pallas_call x1, Pallas kernels, shards(): call(inner_kernel, 'inner', (weight_rows(2), weight_rows(2), spread_row(R...  7.99 us
    pallas_call x2, Pallas kernels, outer(): call(lambda *refs: outer_kernel(slot, *refs), f'outer{slot}', (weight_row...  7.79 us
    ppermute x1, starting transfers between devices, shards(): above = lax.ppermute(second, 'rows', down)  4.55 us
    pallas_call x1, Pallas kernels, shards(): call(gram_kernel, 'gram', (grid_row(), jax.ShapeDtypeStruct((2, TILE), F3...  4.23 us
    ppermute x1, starting transfers between devices, shards(): f_above = lax.ppermute(f1, 'rows', down)  3.49 us
    ppermute x1, waiting for transfers between devices, shards(): f_below = lax.ppermute(f0, 'rows', up)  2.49 us
    pallas_call x1, Pallas kernels, shards(): call(product_kernel, 'product', (grid_row(), spread_row()), [VMEM] * 8, [...  1.57 us
  transfers between devices with their start and end apart: 5, of which 1 were waited for; matrix products, arithmetic and copies ran while one was open for 0% of the time, Pallas kernels for 30%

profile of v3, /device:TPU:2, one launch (start us, length us, event | category | flops | bytes accessed | tf_op | source)
XLA Modules:
  0.0 73.1 jit_solution(3601374896135187960)
XLA Ops:
  2.6 1.4 %pack.1 = (f32[16,2048]{1,0:T(8,128)S(1)}, f32[16,2048]{1,0:T(8,128)S(1)}, f32[8,128]{1,0:T(8,128)S(1)}) custom-call(s32[32]{0:T(128)} %refs_0_.1, f32[2,4096]{1,0:T(2,128)} %offsets_hbm.1, s32[8,4096]{1,0:T(8,128)} %probes_hbm.1, f32[1,4096]{1,0:T(1,128)} %bitcast.2, f32[1]{0:T(128)S(6)} %copy.9.scale_ref, f32[1]{0:T(128)S(6)} %copy.10.amp_ref, ...), custom_call_target="tpu_custom_call" | custom-call | flops 1048576 | bytes 1048576 | tf_op jit(solution)/shard_map/pack/pallas_call | solution.py:587
  4.0 1.3 %collective-permute-start.2 = (f32[16,2048]{1,0:T(8,128)S(1)}, f32[16,2048]{1,0:T(8,128)S(1)}, u32[]{:S(2)}, u32[]{:S(2)}) collective-permute-start(f32[16,2048]{1,0:T(8,128)S(1)} %get-tuple-element.24.first_ref.refs_1_.b0_ref.refs_3_), channel_id=1, source_target_pairs={{1,0},{2,1},{3,2},{4,3},{5,4},{6,5},{7,6},{8,7},{9,8},{10,9},{11,1... | collective-permute-start | bytes 393224 | tf_op jit(solution)/shard_map/ppermute | solution.py:622
  5.3 4.6 %collective-permute-start = (f32[16,2048]{1,0:T(8,128)S(1)}, f32[16,2048]{1,0:T(8,128)S(1)}, u32[]{:S(2)}, u32[]{:S(2)}) collective-permute-start(f32[16,2048]{1,0:T(8,128)S(1)} %get-tuple-element.23.second_ref.refs_1_.b1_ref.b_ref.refs_4_), channel_id=1, source_target_pairs={{0,1},{1,2},{2,3},{3,4},{4,5},{5,6},{6,7},{7,8},{8,9},{9,10},{10,1... | collective-permute-start | bytes 393224 | tf_op jit(solution)/shard_map/ppermute | solution.py:621
  9.8 8.0 %inner.1 = (bf16[2,16,768,128]{3,2,1,0:T(8,128)(2,1)S(1)}, bf16[2,16,768,128]{3,2,1,0:T(8,128)(2,1)S(1)}, bf16[16,4608]{1,0:T(8,128)(2,1)S(1)}, bf16[16,4608]{1,0:T(8,128)(2,1)S(1)}) custom-call(f32[16,2048]{1,0:T(8,128)S(1)} %get-tuple-element.24.first_ref.refs_1_.b0_ref.refs_3_, f32[16,2048]{1,0:T(8,128)S(1)} %get-tuple-element.23.second_ref.refs_1_.b1_ref.b_ref.refs_4_, ...), custom_call_target="tpu_custom_call" | custom-call | flops 1073741824 | bytes 1048576 | tf_op jit(solution)/shard_map/inner/pallas_call | solution.py:623
  17.8 0.0 collective-permute-done.2.refs_0_
  17.8 3.6 %outer1.1 = (bf16[1,16,768,128]{3,2,1,0:T(8,128)(2,1)S(1)}, f32[16,2048]{1,0:T(8,128)S(1)}, bf16[32,4608]{1,0:T(8,128)(2,1)S(1)}, f32[16,2048]{1,0:T(8,128)S(1)}) custom-call(f32[16,2048]{1,0:T(8,128)S(1)} %collective-permute-done.2.refs_0_, f32[16,2048]{1,0:T(8,128)S(1)} %get-tuple-element.23.second_ref.refs_1_.b1_ref.b_ref.refs_4_, ...), custom_call_target="tpu_custom_call" | custom-call | flops 1073741824 | bytes 1048576 | tf_op jit(solution)/shard_map/outer1/pallas_call | solution.py:612
  21.4 3.5 %collective-permute-start.3 = (f32[16,2048]{1,0:T(8,128)S(1)}, f32[16,2048]{1,0:T(8,128)S(1)}, u32[]{:S(2)}, u32[]{:S(2)}) collective-permute-start(f32[16,2048]{1,0:T(8,128)S(1)} %get-tuple-element.30.f1_ref.f_ref.refs_6_), channel_id=1, source_target_pairs={{0,1},{1,2},{2,3},{3,4},{4,5},{5,6},{6,7},{7,8},{8,9},{9,10},{10,1... | collective-permute-start | bytes 393224 | tf_op jit(solution)/shard_map/ppermute | solution.py:634
  24.9 0.0 collective-permute-done.refs_0_
  24.9 4.2 %outer0.1 = (bf16[1,16,768,128]{3,2,1,0:T(8,128)(2,1)S(1)}, f32[16,2048]{1,0:T(8,128)S(1)}, bf16[32,4608]{1,0:T(8,128)(2,1)S(1)}, f32[16,2048]{1,0:T(8,128)}) custom-call(f32[16,2048]{1,0:T(8,128)S(1)} %collective-permute-done.refs_0_, f32[16,2048]{1,0:T(8,128)S(1)} %get-tuple-element.24.first_ref.refs_1_.b0_ref.refs_3_, ...), custom_call_target="tpu_custom_call" | custom-call | flops 1073741824 | bytes 1048576 | tf_op jit(solution)/shard_map/outer0/pallas_call | solution.py:612
  29.1 1.3 %collective-permute-start.1 = (f32[16,2048]{1,0:T(8,128)S(1)}, f32[16,2048]{1,0:T(8,128)S(1)}, u32[]{:S(2)}, u32[]{:S(2)}) collective-permute-start(f32[16,2048]{1,0:T(8,128)S(1)} %get-tuple-element.29.own_ref.f0_ref.refs_5_), channel_id=1, source_target_pairs={{1,0},{2,1},{3,2},{4,3},{5,4},{6,5},{7,6},{8,7},{9,8},{10,9},{11,1... | collective-permute-start | bytes 393224 | tf_op jit(solution)/shard_map/ppermute | solution.py:632
  30.4 0.0 collective-permute-done.3.other_ref
  30.4 1.6 %product.1 = (f32[16,2048]{1,0:T(8,128)S(1)}, bf16[32,4608]{1,0:T(8,128)(2,1)S(1)}) custom-call(f32[16,2048]{1,0:T(8,128)S(1)} %collective-permute-done.3.other_ref, f32[16,2048]{1,0:T(8,128)S(1)} %get-tuple-element.29.own_ref.f0_ref.refs_5_, f32[8,128]{1,0:T(8,128)S(1)} %get-tuple-element.22.consts_ref.refs_2_.refs_1_, ...), custom_call_target="tpu_custom_call" | custom-call | flops 536870912 | bytes 1048576 | tf_op jit(solution)/shard_map/product/pallas_call | solution.py:635
  32.0 1.5 %collective-permute-start.4 = (f32[16,2048]{1,0:T(8,128)S(1)}, f32[16,2048]{1,0:T(8,128)S(1)}, u32[]{:S(2)}, u32[]{:S(2)}) collective-permute-start(f32[16,2048]{1,0:T(8,128)S(1)} %get-tuple-element.34.g0_ref.refs_7_), channel_id=1, source_target_pairs={{1,0},{2,1},{3,2},{4,3},{5,4},{6,5},{7,6},{8,7},{9,8},{10,9},{11,1... | collective-permute-start | bytes 393224 | tf_op jit(solution)/shard_map/ppermute | solution.py:643
  33.5 2.5 %collective-permute-done.1.below_ref = f32[16,2048]{1,0:T(8,128)S(1)} collective-permute-done((f32[16,2048]{1,0:T(8,128)S(1)}, f32[16,2048]{1,0:T(8,128)S(1)}, u32[]{:S(2)}, u32[]{:S(2)}) %collective-permute-start.1) | collective-permute-done | bytes 131104 | tf_op jit(solution)/shard_map/ppermute | solution.py:632
  36.0 0.0 copy-start
  36.0 4.2 %gram.1 = (f32[16,2048]{1,0:T(8,128)S(1)}, f32[2,128]{1,0:T(2,128)S(1)}) custom-call(f32[16,2048]{1,0:T(8,128)S(1)} %collective-permute-done.1.below_ref, f32[16,2048]{1,0:T(8,128)S(1)} %get-tuple-element.24.first_ref.refs_1_.b0_ref.refs_3_, f32[16,2048]{1,0:T(8,128)S(1)} %get-tuple-element.23.second_ref.refs_1_.b1_ref.b_ref.refs_4_, ...), custom_call_target="tpu_custom_call" | custom-call | flops 536870912 | bytes 1048576 | tf_op jit(solution)/shard_map/gram/pallas_call | solution.py:644
  40.2 0.0 collective-permute-done.4.below_ref
  40.2 1.1 %moment.1 = f32[64,1,256]{2,1,0:T(1,128)S(1)} custom-call(f32[2,128]{1,0:T(2,128)S(1)} %get-tuple-element.38.sums_ref, f32[16,2048]{1,0:T(8,128)S(1)} %collective-permute-done.4.below_ref, f32[16,2048]{1,0:T(8,128)S(1)} %get-tuple-element.23.second_ref.refs_1_.b1_ref.b_ref.refs_4_, f32[16,2048]{1,0:T(8,128)S(1)} %get-tuple-element.30.f1_ref.f_ref.refs_6_, ...), custom_call_target="tpu_custom_call" | custom-call | flops 536870912 | bytes 1048576 | tf_op jit(solution)/shard_map/moment/pallas_call | solution.py:652
  41.3 30.2 %all_to_all.5.refs_2_ = f32[64,1,256]{2,1,0:T(1,128)S(1)} all-to-all(f32[64,1,256]{2,1,0:T(1,128)S(1)} %moment.1), channel_id=1, replica_groups=mesh['hyp'=8,'rows'=64] {'rows'}, dimensions={0} | all-to-all | bytes 131072 | tf_op jit(solution)/shard_map/all_to_all | solution.py:660
  71.5 0.0 copy-done
  71.5 1.5 %finish.1 = (f32[9,4096]{1,0:T(8,128)}, f32[1,9]{1,0:T(1,128)}) custom-call(s32[32]{0:T(128)S(1)} %copy-done, f32[8,128]{1,0:T(8,128)S(1)} %get-tuple-element.22.consts_ref.refs_2_.refs_1_, f32[64,1,256]{2,1,0:T(1,128)S(1)} %all_to_all.5.refs_2_, f32[16,2048]{1,0:T(8,128)S(1)} %get-tuple-element.24.first_ref.refs_1_.b0_ref.refs_3_, ...), custom_call_target="tpu_custom_call" | custom-call | flops 1048576 | bytes 1048576 | tf_op jit(solution)/shard_map/finish/pallas_call | solution.py:662
Async XLA Ops:
  4.0 13.9 %collective-permute-start.2 = (f32[16,2048]{1,0:T(8,128)S(1)}, f32[16,2048]{1,0:T(8,128)S(1)}, u32[]{:S(2)}, u32[]{:S(2)}) collective-permute-start(f32[16,2048]{1,0:T(8,128)S(1)} %get-tuple-element.24.first_ref.refs_1_.b0_ref.refs_3_), channel_id=1, source_target_pairs={{1,0},{2,1},{3,2},{4,3},{5,4},{6,5},{7,6},{8,7},{9,8},{10,9},{11,1... | collective-permute-start | bytes 393224 | tf_op jit(solution)/shard_map/ppermute | solution.py:622
  5.3 19.7 %collective-permute-start = (f32[16,2048]{1,0:T(8,128)S(1)}, f32[16,2048]{1,0:T(8,128)S(1)}, u32[]{:S(2)}, u32[]{:S(2)}) collective-permute-start(f32[16,2048]{1,0:T(8,128)S(1)} %get-tuple-element.23.second_ref.refs_1_.b1_ref.b_ref.refs_4_), channel_id=1, source_target_pairs={{0,1},{1,2},{2,3},{3,4},{4,5},{5,6},{6,7},{7,8},{8,9},{9,10},{10,1... | collective-permute-start | bytes 393224 | tf_op jit(solution)/shard_map/ppermute | solution.py:621
  21.4 9.0 %collective-permute-start.3 = (f32[16,2048]{1,0:T(8,128)S(1)}, f32[16,2048]{1,0:T(8,128)S(1)}, u32[]{:S(2)}, u32[]{:S(2)}) collective-permute-start(f32[16,2048]{1,0:T(8,128)S(1)} %get-tuple-element.30.f1_ref.f_ref.refs_6_), channel_id=1, source_target_pairs={{0,1},{1,2},{2,3},{3,4},{4,5},{5,6},{6,7},{7,8},{8,9},{9,10},{10,1... | collective-permute-start | bytes 393224 | tf_op jit(solution)/shard_map/ppermute | solution.py:634
  29.1 6.8 %collective-permute-start.1 = (f32[16,2048]{1,0:T(8,128)S(1)}, f32[16,2048]{1,0:T(8,128)S(1)}, u32[]{:S(2)}, u32[]{:S(2)}) collective-permute-start(f32[16,2048]{1,0:T(8,128)S(1)} %get-tuple-element.29.own_ref.f0_ref.refs_5_), channel_id=1, source_target_pairs={{1,0},{2,1},{3,2},{4,3},{5,4},{6,5},{7,6},{8,7},{9,8},{10,9},{11,1... | collective-permute-start | bytes 393224 | tf_op jit(solution)/shard_map/ppermute | solution.py:632
  32.0 8.2 %collective-permute-start.4 = (f32[16,2048]{1,0:T(8,128)S(1)}, f32[16,2048]{1,0:T(8,128)S(1)}, u32[]{:S(2)}, u32[]{:S(2)}) collective-permute-start(f32[16,2048]{1,0:T(8,128)S(1)} %get-tuple-element.34.g0_ref.refs_7_), channel_id=1, source_target_pairs={{1,0},{2,1},{3,2},{4,3},{5,4},{6,5},{7,6},{8,7},{9,8},{10,9},{11,1... | collective-permute-start | bytes 393224 | tf_op jit(solution)/shard_map/ppermute | solution.py:643
  36.0 35.5 %copy-start = (s32[32]{0:T(128)S(1)}, s32[32]{0:T(128)}, u32[]{:S(2)}) copy-start(s32[32]{0:T(128)} %refs_0_.1) | copy-start | bytes 388

commit v4 on v3

--- a/solution.py
+++ b/solution.py
@@ -68,6 +68,7 @@
     second_ref,
     consts_ref,
     cell_ref,
+    from_ref,
     offsets_ref,
     probes_ref,
     target_ref,
@@ -88,25 +89,17 @@
         copy.start()
     for copy in copies:
         copy.wait()
+    for s in range(cell_ref.shape[0]):
+        from_ref[cell_ref[s]] = s
     filler = jnp.zeros((ROWS - RHS - 2, TILE), F32)
-    for s in range(cell_ref.shape[0]):
-        here = slice(s * TILE, (s + 1) * TILE)
-        signs = 2.0 * probes_ref[:, here].astype(F32) - 1.0
-        rest = jnp.concatenate([target_ref[:, here], offsets_ref[:, here], filler], axis=0)
-        cell = cell_ref[s]
-
-        def put(ref, column, signs=signs, rest=rest):
-            ref[0:8, lanes(column)] = signs
-            ref[8:16, lanes(column)] = rest
-
-        @pl.when(cell < GX)
-        def _():
-            put(first_ref, cell)
-
-        @pl.when(cell >= GX)
-        def _():
-            put(second_ref, cell - GX)
-
+    for cell in range(cell_ref.shape[0]):
+        stored = lanes(from_ref[cell])
+        here = slice(cell % GX * TILE, (cell % GX + 1) * TILE)
+        ref = (first_ref, second_ref)[cell // GX]
+        ref[0:8, here] = 2.0 * probes_ref[:, stored].astype(F32) - 1.0
+        ref[8:16, here] = jnp.concatenate(
+            [target_ref[:, stored], offsets_ref[:, stored], filler], axis=0
+        )
     amp = jnp.full((1, TILE), amp_ref[0], F32)
     reach = jnp.exp(0.2 * jnp.log(4.0 * amp))
     square = reach * reach
@@ -174,33 +167,36 @@
     return split_rows(values, target).astype(BF16)
 
 
-def fill_weights(target_ref, row_shift, feats_ref, weights_ref, combo, consts_ref, rows):
+def fill_weights(targets, feats_ref, consts_ref, rows):
     factor = constant(consts_ref, FACTOR)
-    reach = jnp.broadcast_to(constant(consts_ref, REACH), (16, TILE))
-    top = jnp.broadcast_to(constant(consts_ref, TOP), (16, TILE))
+    reach = jnp.broadcast_to(constant(consts_ref, REACH), (TILE, TILE))
+    top = jnp.broadcast_to(constant(consts_ref, TOP), (TILE, TILE))
 
     def one(tile, carry):
         for k in range(3):
-            wanted = target_features(target_ref, tile, float(row_shift), float(k - 1), factor, rows)
-            square = lax.dot_general(
+            wanted = [
+                target_features(ref, tile, float(row_shift), float(k - 1), factor, rows)
+                for ref, row_shift, _, _ in targets
+            ]
+            squares = lax.dot_general(
                 feats_ref[tile + k],
-                wanted,
+                wanted[0] if len(wanted) == 1 else jnp.concatenate(wanted, axis=1),
                 (((1,), (0,)), ((), ())),
                 preferred_element_type=F32,
             )
-            for part in range(TILE // 16):
-                here = jnp.maximum(square[part * 16 : (part + 1) * 16, :], 1e-12)
+            for i, (_, _, weights_ref, combo) in enumerate(targets):
+                here = jnp.maximum(squares[:, i * TILE : (i + 1) * TILE], 1e-12)
                 close = jnp.maximum(reach - here * lax.rsqrt(here), 0.0)
                 second = close * close
                 weight = (second * second) * (top - close)
                 high = weight.astype(BF16)
                 low = (weight - high.astype(F32)).astype(BF16)
-                base = k * 2 * TILE + part * 16
-                weights_ref[combo, tile, base : base + 16, :] = high
-                weights_ref[combo, tile, base + TILE : base + TILE + 16, :] = low
+                base = k * 2 * TILE
+                weights_ref[combo, tile, base : base + TILE, :] = high
+                weights_ref[combo, tile, base + TILE : base + 2 * TILE, :] = low
         return carry
 
-    lax.fori_loop(0, GX, one, 0, unroll=8)
+    lax.fori_loop(0, GX, one, 0, unroll=8 // len(targets))
 
 
 def spread_ends(out_ref):
@@ -347,13 +343,22 @@
 
 
 def lines(sums, first):
-    placed = [jnp.zeros((ROWS, TILE), F32), jnp.zeros((ROWS, TILE), F32)]
-    for k, (high, low) in enumerate(sums):
+    row = lax.broadcasted_iota(jnp.int32, (8, TILE), 0)
+    lane = lax.broadcasted_iota(jnp.int32, (8, TILE), 1)
+    blocks = [[(high[0:8], low[0:8]), lane == row + STRIDE * (first + k)] for k, (high, low) in enumerate(sums)]
+    for start in range(0, len(sums), 8):
+        last = [jnp.zeros((8, TILE), F32), jnp.zeros((8, TILE), F32)]
+        group = sums[start : start + 8]
+        for k, pair in enumerate(group):
+            last = [jnp.where(row == k, jnp.broadcast_to(v[8:9], (8, TILE)), t) for v, t in zip(pair, last)]
+        mask = (lane == 8 + STRIDE * (first + start + row)) & (row < len(group))
+        blocks.append([tuple(last), mask])
+    placed = [jnp.zeros((8, TILE), F32), jnp.zeros((8, TILE), F32)]
+    for (high, low), mask in blocks:
         for shift in (64, 32, 16, 8, 4, 2, 1):
             high, left = two_sum(high, pltpu.roll(high, shift, 1))
             low = (low + pltpu.roll(low, shift, 1)) + left
         high, low = quick_sum(high, low)
-        mask = grid_mask(first + k)
         placed = [jnp.where(mask, high, placed[0]), jnp.where(mask, low, placed[1])]
     return [jnp.sum(p, axis=0, keepdims=True) for p in placed]
 
@@ -366,8 +371,8 @@
         ((first_ref, left_ref, spread0_ref), (second_ref, right_ref, spread1_ref))
     ):
         source_features(own_ref, constant(consts_ref, FACTOR), rows, feats_ref)
-        fill_weights(first_ref, slot, feats_ref, weights_ref, 0, consts_ref, rows)
-        fill_weights(second_ref, slot - 1, feats_ref, weights_ref, 1, consts_ref, rows)
+        targets = ((first_ref, slot, weights_ref, 0), (second_ref, slot - 1, weights_ref, 1))
+        fill_weights(targets, feats_ref, consts_ref, rows)
         spread_sides(own_ref, spread_ref)
 
 
@@ -389,7 +394,7 @@
 ):
     rows = feature_rows()
     source_features(other_ref, constant(consts_ref, FACTOR), rows, feats_ref)
-    fill_weights(own_ref, 2 * slot - 1, feats_ref, weights_ref, 0, consts_ref, rows)
+    fill_weights(((own_ref, 2 * slot - 1, weights_ref, 0),), feats_ref, consts_ref, rows)
     spread_sides(other_ref, spread_ref)
     terms = ((spread_ref, weights_ref, 0), (spread0_ref, left_ref, slot), (spread1_ref, right_ref, slot))
     apply_row(own_ref, terms, consts_ref, out_ref, out_spread_ref, beside_ref)
@@ -591,6 +596,7 @@
         [HBM] * 4 + [SMEM] * 3,
         [
             pltpu.SMEM((tiles,), jnp.int32),
+            pltpu.SMEM((tiles,), jnp.int32),
             pltpu.VMEM((2, tiles * TILE), F32),
             pltpu.VMEM((8, tiles * TILE), jnp.int32),
             pltpu.VMEM((1, tiles * TILE), F32),

time: 73.4 us -> 72.8 us (level)
  the two profiles are of different devices: /device:TPU:2 before, /device:TPU:4 now
where the time goes in v4:
time: 72.8 us; the launch traced here: 72.4 us
  blocking collectives  30.2 us (41%)
  Pallas kernels  25 us (34%)
  starting transfers between devices  11.9 us (16%)
  between operations  2.69 us (4%)
  waiting for transfers between devices  2.68 us (4%)
    all_to_all x1, blocking collectives, shards(): lax.all_to_all(parts, 'rows', split_axis=0, concat_axis=0, tiled=True)  30.2 us
    pallas_call x1, Pallas kernels, shards(): call(inner_kernel, 'inner', (weight_rows(2), weight_rows(2), spread_row(R...  7.81 us
    pallas_call x2, Pallas kernels, outer(): call(lambda *refs: outer_kernel(slot, *refs), f'outer{slot}', (weight_row...  7.78 us
    ppermute x1, starting transfers between devices, shards(): above = lax.ppermute(second, 'rows', down)  4.55 us
    pallas_call x1, Pallas kernels, shards(): call(gram_kernel, 'gram', (grid_row(), jax.ShapeDtypeStruct((2, TILE), F3...  4.22 us
    ppermute x1, starting transfers between devices, shards(): f_above = lax.ppermute(f1, 'rows', down)  3.48 us
    ppermute x1, waiting for transfers between devices, shards(): f_below = lax.ppermute(f0, 'rows', up)  2.67 us
    pallas_call x1, Pallas kernels, shards(): call(product_kernel, 'product', (grid_row(), spread_row()), [VMEM] * 8, [...  1.57 us
  transfers between devices with their start and end apart: 5, of which 1 were waited for; matrix products, arithmetic and copies ran while one was open for 0% of the time, Pallas kernels for 30%

profile of v4, /device:TPU:4, one launch (start us, length us, event | category | flops | bytes accessed | tf_op | source)
XLA Modules:
  0.0 72.4 jit_solution(7029323383507078942)
XLA Ops:
  2.6 1.1 %pack.1 = (f32[16,2048]{1,0:T(8,128)S(1)}, f32[16,2048]{1,0:T(8,128)S(1)}, f32[8,128]{1,0:T(8,128)S(1)}) custom-call(s32[32]{0:T(128)} %refs_0_.1, f32[2,4096]{1,0:T(2,128)} %offsets_hbm.1, s32[8,4096]{1,0:T(8,128)} %probes_hbm.1, f32[1,4096]{1,0:T(1,128)} %bitcast.2, f32[1]{0:T(128)S(6)} %copy.9.scale_ref, f32[1]{0:T(128)S(6)} %copy.10.amp_ref, ...), custom_call_target="tpu_custom_call" | custom-call | flops 1048576 | bytes 1048576 | tf_op jit(solution)/shard_map/pack/pallas_call | solution.py:592
  3.6 1.3 %collective-permute-start.2 = (f32[16,2048]{1,0:T(8,128)S(1)}, f32[16,2048]{1,0:T(8,128)S(1)}, u32[]{:S(2)}, u32[]{:S(2)}) collective-permute-start(f32[16,2048]{1,0:T(8,128)S(1)} %get-tuple-element.24.first_ref.refs_1_.b0_ref.refs_3_), channel_id=1, source_target_pairs={{1,0},{2,1},{3,2},{4,3},{5,4},{6,5},{7,6},{8,7},{9,8},{10,9},{11,1... | collective-permute-start | bytes 393224 | tf_op jit(solution)/shard_map/ppermute | solution.py:628
  4.9 4.6 %collective-permute-start = (f32[16,2048]{1,0:T(8,128)S(1)}, f32[16,2048]{1,0:T(8,128)S(1)}, u32[]{:S(2)}, u32[]{:S(2)}) collective-permute-start(f32[16,2048]{1,0:T(8,128)S(1)} %get-tuple-element.23.second_ref.refs_1_.b1_ref.b_ref.refs_4_), channel_id=1, source_target_pairs={{0,1},{1,2},{2,3},{3,4},{4,5},{5,6},{6,7},{7,8},{8,9},{9,10},{10,1... | collective-permute-start | bytes 393224 | tf_op jit(solution)/shard_map/ppermute | solution.py:627
  9.5 7.8 %inner.1 = (bf16[2,16,768,128]{3,2,1,0:T(8,128)(2,1)S(1)}, bf16[2,16,768,128]{3,2,1,0:T(8,128)(2,1)S(1)}, bf16[16,4608]{1,0:T(8,128)(2,1)S(1)}, bf16[16,4608]{1,0:T(8,128)(2,1)S(1)}) custom-call(f32[16,2048]{1,0:T(8,128)S(1)} %get-tuple-element.24.first_ref.refs_1_.b0_ref.refs_3_, f32[16,2048]{1,0:T(8,128)S(1)} %get-tuple-element.23.second_ref.refs_1_.b1_ref.b_ref.refs_4_, ...), custom_call_target="tpu_custom_call" | custom-call | flops 1073741824 | bytes 1048576 | tf_op jit(solution)/shard_map/inner/pallas_call | solution.py:629
  17.3 0.0 collective-permute-done.2.refs_0_
  17.3 3.6 %outer1.1 = (bf16[1,16,768,128]{3,2,1,0:T(8,128)(2,1)S(1)}, f32[16,2048]{1,0:T(8,128)S(1)}, bf16[32,4608]{1,0:T(8,128)(2,1)S(1)}, f32[16,2048]{1,0:T(8,128)S(1)}) custom-call(f32[16,2048]{1,0:T(8,128)S(1)} %collective-permute-done.2.refs_0_, f32[16,2048]{1,0:T(8,128)S(1)} %get-tuple-element.23.second_ref.refs_1_.b1_ref.b_ref.refs_4_, ...), custom_call_target="tpu_custom_call" | custom-call | flops 1073741824 | bytes 1048576 | tf_op jit(solution)/shard_map/outer1/pallas_call | solution.py:618
  20.9 3.5 %collective-permute-start.3 = (f32[16,2048]{1,0:T(8,128)S(1)}, f32[16,2048]{1,0:T(8,128)S(1)}, u32[]{:S(2)}, u32[]{:S(2)}) collective-permute-start(f32[16,2048]{1,0:T(8,128)S(1)} %get-tuple-element.30.f1_ref.f_ref.refs_6_), channel_id=1, source_target_pairs={{0,1},{1,2},{2,3},{3,4},{4,5},{5,6},{6,7},{7,8},{8,9},{9,10},{10,1... | collective-permute-start | bytes 393224 | tf_op jit(solution)/shard_map/ppermute | solution.py:640
  24.4 0.0 collective-permute-done.refs_0_
  24.4 4.2 %outer0.1 = (bf16[1,16,768,128]{3,2,1,0:T(8,128)(2,1)S(1)}, f32[16,2048]{1,0:T(8,128)S(1)}, bf16[32,4608]{1,0:T(8,128)(2,1)S(1)}, f32[16,2048]{1,0:T(8,128)}) custom-call(f32[16,2048]{1,0:T(8,128)S(1)} %collective-permute-done.refs_0_, f32[16,2048]{1,0:T(8,128)S(1)} %get-tuple-element.24.first_ref.refs_1_.b0_ref.refs_3_, ...), custom_call_target="tpu_custom_call" | custom-call | flops 1073741824 | bytes 1048576 | tf_op jit(solution)/shard_map/outer0/pallas_call | solution.py:618
  28.6 1.3 %collective-permute-start.1 = (f32[16,2048]{1,0:T(8,128)S(1)}, f32[16,2048]{1,0:T(8,128)S(1)}, u32[]{:S(2)}, u32[]{:S(2)}) collective-permute-start(f32[16,2048]{1,0:T(8,128)S(1)} %get-tuple-element.29.own_ref.f0_ref.refs_5_), channel_id=1, source_target_pairs={{1,0},{2,1},{3,2},{4,3},{5,4},{6,5},{7,6},{8,7},{9,8},{10,9},{11,1... | collective-permute-start | bytes 393224 | tf_op jit(solution)/shard_map/ppermute | solution.py:638
  29.9 0.0 collective-permute-done.3.other_ref
  29.9 1.6 %product.1 = (f32[16,2048]{1,0:T(8,128)S(1)}, bf16[32,4608]{1,0:T(8,128)(2,1)S(1)}) custom-call(f32[16,2048]{1,0:T(8,128)S(1)} %collective-permute-done.3.other_ref, f32[16,2048]{1,0:T(8,128)S(1)} %get-tuple-element.29.own_ref.f0_ref.refs_5_, f32[8,128]{1,0:T(8,128)S(1)} %get-tuple-element.22.consts_ref.refs_2_.refs_1_, ...), custom_call_target="tpu_custom_call" | custom-call | flops 536870912 | bytes 1048576 | tf_op jit(solution)/shard_map/product/pallas_call | solution.py:641
  31.5 1.3 %collective-permute-start.4 = (f32[16,2048]{1,0:T(8,128)S(1)}, f32[16,2048]{1,0:T(8,128)S(1)}, u32[]{:S(2)}, u32[]{:S(2)}) collective-permute-start(f32[16,2048]{1,0:T(8,128)S(1)} %get-tuple-element.34.g0_ref.refs_7_), channel_id=1, source_target_pairs={{1,0},{2,1},{3,2},{4,3},{5,4},{6,5},{7,6},{8,7},{9,8},{10,9},{11,1... | collective-permute-start | bytes 393224 | tf_op jit(solution)/shard_map/ppermute | solution.py:649
  32.8 2.7 %collective-permute-done.1.below_ref = f32[16,2048]{1,0:T(8,128)S(1)} collective-permute-done((f32[16,2048]{1,0:T(8,128)S(1)}, f32[16,2048]{1,0:T(8,128)S(1)}, u32[]{:S(2)}, u32[]{:S(2)}) %collective-permute-start.1) | collective-permute-done | bytes 131104 | tf_op jit(solution)/shard_map/ppermute | solution.py:638
  35.5 0.0 copy-start
  35.5 4.2 %gram.1 = (f32[16,2048]{1,0:T(8,128)S(1)}, f32[2,128]{1,0:T(2,128)S(1)}) custom-call(f32[16,2048]{1,0:T(8,128)S(1)} %collective-permute-done.1.below_ref, f32[16,2048]{1,0:T(8,128)S(1)} %get-tuple-element.24.first_ref.refs_1_.b0_ref.refs_3_, f32[16,2048]{1,0:T(8,128)S(1)} %get-tuple-element.23.second_ref.refs_1_.b1_ref.b_ref.refs_4_, ...), custom_call_target="tpu_custom_call" | custom-call | flops 536870912 | bytes 1048576 | tf_op jit(solution)/shard_map/gram/pallas_call | solution.py:650
  39.7 0.0 collective-permute-done.4.below_ref
  39.7 1.1 %moment.1 = f32[64,1,256]{2,1,0:T(1,128)S(1)} custom-call(f32[2,128]{1,0:T(2,128)S(1)} %get-tuple-element.38.sums_ref, f32[16,2048]{1,0:T(8,128)S(1)} %collective-permute-done.4.below_ref, f32[16,2048]{1,0:T(8,128)S(1)} %get-tuple-element.23.second_ref.refs_1_.b1_ref.b_ref.refs_4_, f32[16,2048]{1,0:T(8,128)S(1)} %get-tuple-element.30.f1_ref.f_ref.refs_6_, ...), custom_call_target="tpu_custom_call" | custom-call | flops 536870912 | bytes 1048576 | tf_op jit(solution)/shard_map/moment/pallas_call | solution.py:658
  40.8 30.2 %all_to_all.5.refs_2_ = f32[64,1,256]{2,1,0:T(1,128)S(1)} all-to-all(f32[64,1,256]{2,1,0:T(1,128)S(1)} %moment.1), channel_id=1, replica_groups=mesh['hyp'=8,'rows'=64] {'rows'}, dimensions={0} | all-to-all | bytes 131072 | tf_op jit(solution)/shard_map/all_to_all | solution.py:666
  71.0 0.0 copy-done
  71.0 1.5 %finish.1 = (f32[9,4096]{1,0:T(8,128)}, f32[1,9]{1,0:T(1,128)}) custom-call(s32[32]{0:T(128)S(1)} %copy-done, f32[8,128]{1,0:T(8,128)S(1)} %get-tuple-element.22.consts_ref.refs_2_.refs_1_, f32[64,1,256]{2,1,0:T(1,128)S(1)} %all_to_all.5.refs_2_, f32[16,2048]{1,0:T(8,128)S(1)} %get-tuple-element.24.first_ref.refs_1_.b0_ref.refs_3_, ...), custom_call_target="tpu_custom_call" | custom-call | flops 1048576 | bytes 1048576 | tf_op jit(solution)/shard_map/finish/pallas_call | solution.py:668
Async XLA Ops:
  3.6 13.7 %collective-permute-start.2 = (f32[16,2048]{1,0:T(8,128)S(1)}, f32[16,2048]{1,0:T(8,128)S(1)}, u32[]{:S(2)}, u32[]{:S(2)}) collective-permute-start(f32[16,2048]{1,0:T(8,128)S(1)} %get-tuple-element.24.first_ref.refs_1_.b0_ref.refs_3_), channel_id=1, source_target_pairs={{1,0},{2,1},{3,2},{4,3},{5,4},{6,5},{7,6},{8,7},{9,8},{10,9},{11,1... | collective-permute-start | bytes 393224 | tf_op jit(solution)/shard_map/ppermute | solution.py:628
  4.9 19.5 %collective-permute-start = (f32[16,2048]{1,0:T(8,128)S(1)}, f32[16,2048]{1,0:T(8,128)S(1)}, u32[]{:S(2)}, u32[]{:S(2)}) collective-permute-start(f32[16,2048]{1,0:T(8,128)S(1)} %get-tuple-element.23.second_ref.refs_1_.b1_ref.b_ref.refs_4_), channel_id=1, source_target_pairs={{0,1},{1,2},{2,3},{3,4},{4,5},{5,6},{6,7},{7,8},{8,9},{9,10},{10,1... | collective-permute-start | bytes 393224 | tf_op jit(solution)/shard_map/ppermute | solution.py:627
  20.9 9.0 %collective-permute-start.3 = (f32[16,2048]{1,0:T(8,128)S(1)}, f32[16,2048]{1,0:T(8,128)S(1)}, u32[]{:S(2)}, u32[]{:S(2)}) collective-permute-start(f32[16,2048]{1,0:T(8,128)S(1)} %get-tuple-element.30.f1_ref.f_ref.refs_6_), channel_id=1, source_target_pairs={{0,1},{1,2},{2,3},{3,4},{4,5},{5,6},{6,7},{7,8},{8,9},{9,10},{10,1... | collective-permute-start | bytes 393224 | tf_op jit(solution)/shard_map/ppermute | solution.py:640
  28.6 6.8 %collective-permute-start.1 = (f32[16,2048]{1,0:T(8,128)S(1)}, f32[16,2048]{1,0:T(8,128)S(1)}, u32[]{:S(2)}, u32[]{:S(2)}) collective-permute-start(f32[16,2048]{1,0:T(8,128)S(1)} %get-tuple-element.29.own_ref.f0_ref.refs_5_), channel_id=1, source_target_pairs={{1,0},{2,1},{3,2},{4,3},{5,4},{6,5},{7,6},{8,7},{9,8},{10,9},{11,1... | collective-permute-start | bytes 393224 | tf_op jit(solution)/shard_map/ppermute | solution.py:638
  31.5 8.2 %collective-permute-start.4 = (f32[16,2048]{1,0:T(8,128)S(1)}, f32[16,2048]{1,0:T(8,128)S(1)}, u32[]{:S(2)}, u32[]{:S(2)}) collective-permute-start(f32[16,2048]{1,0:T(8,128)S(1)} %get-tuple-element.34.g0_ref.refs_7_), channel_id=1, source_target_pairs={{1,0},{2,1},{3,2},{4,3},{5,4},{6,5},{7,6},{8,7},{9,8},{10,9},{11,1... | collective-permute-start | bytes 393224 | tf_op jit(solution)/shard_map/ppermute | solution.py:649
  35.5 35.5 %copy-start = (s32[32]{0:T(128)S(1)}, s32[32]{0:T(128)}, u32[]{:S(2)}) copy-start(s32[32]{0:T(128)} %refs_0_.1) | copy-start | bytes 388

commit v5 on v4

--- a/solution.py
+++ b/solution.py
@@ -388,10 +388,9 @@
     weights_ref,
     out_ref,
     out_spread_ref,
-    beside_ref,
-    feats_ref,
-    spread_ref,
+    *more,
 ):
+    beside_ref, feats_ref, spread_ref = more if slot else (None, *more)
     rows = feature_rows()
     source_features(other_ref, constant(consts_ref, FACTOR), rows, feats_ref)
     fill_weights(((own_ref, 2 * slot - 1, weights_ref, 0),), feats_ref, consts_ref, rows)
@@ -618,7 +617,7 @@
         return call(
             lambda *refs: outer_kernel(slot, *refs),
             f"outer{slot}",
-            (weight_rows(1), grid_row(), spread_row(), grid_row()),
+            (weight_rows(1), grid_row(), spread_row()) + (grid_row(),) * slot,
             [VMEM] * 7,
             [feature_tiles(), spread_row(ROWS)],
             flops=1 << 30,
@@ -634,7 +633,7 @@
         [feature_tiles()],
         flops=1 << 30,
     )(first, second, consts)
-    over, f0, f0_spread, _ = outer(0, above, first)
+    over, f0, f0_spread = outer(0, above, first)
     f_below = lax.ppermute(f0, "rows", up)
     under, f1, f1_spread, b_beside = outer(1, below, second)
     f_above = lax.ppermute(f1, "rows", down)

time: 72.8 us -> 72.1 us (level)
  the two profiles are of different devices: /device:TPU:4 before, /device:TPU:2 now
where the time goes in v5:
time: 72.1 us; the launch traced here: 71.8 us
  blocking collectives  30.2 us (42%)
  Pallas kernels  24.4 us (34%)
  starting transfers between devices  11.9 us (17%)
  waiting for transfers between devices  2.69 us (4%)
  between operations  2.69 us (4%)
    all_to_all x1, blocking collectives, shards(): lax.all_to_all(parts, 'rows', split_axis=0, concat_axis=0, tiled=True)  30.2 us
    pallas_call x1, Pallas kernels, shards(): call(inner_kernel, 'inner', (weight_rows(2), weight_rows(2), spread_row(R...  7.81 us
    pallas_call x2, Pallas kernels, outer(): call(lambda *refs: outer_kernel(slot, *refs), f'outer{slot}', (weight_row...  7.16 us
    ppermute x1, starting transfers between devices, shards(): above = lax.ppermute(second, 'rows', down)  4.55 us
    pallas_call x1, Pallas kernels, shards(): call(gram_kernel, 'gram', (grid_row(), jax.ShapeDtypeStruct((2, TILE), F3...  4.22 us
    ppermute x1, starting transfers between devices, shards(): f_above = lax.ppermute(f1, 'rows', down)  3.48 us
    ppermute x1, waiting for transfers between devices, shards(): f_below = lax.ppermute(f0, 'rows', up)  2.67 us
    pallas_call x1, Pallas kernels, shards(): call(product_kernel, 'product', (grid_row(), spread_row()), [VMEM] * 8, [...  1.57 us
  transfers between devices with their start and end apart: 5, of which 1 were waited for; matrix products, arithmetic and copies ran while one was open for 0% of the time, Pallas kernels for 29%

profile of v5, /device:TPU:2, one launch (start us, length us, event | category | flops | bytes accessed | tf_op | source)
XLA Modules:
  0.0 71.8 jit_solution(17811043678378718532)
XLA Ops:
  2.6 1.1 %pack.1 = (f32[16,2048]{1,0:T(8,128)S(1)}, f32[16,2048]{1,0:T(8,128)S(1)}, f32[8,128]{1,0:T(8,128)S(1)}) custom-call(s32[32]{0:T(128)} %refs_0_.1, f32[2,4096]{1,0:T(2,128)} %offsets_hbm.1, s32[8,4096]{1,0:T(8,128)} %probes_hbm.1, f32[1,4096]{1,0:T(1,128)} %bitcast.2, f32[1]{0:T(128)S(6)} %copy.9.scale_ref, f32[1]{0:T(128)S(6)} %copy.10.amp_ref, ...), custom_call_target="tpu_custom_call" | custom-call | flops 1048576 | bytes 1048576 | tf_op jit(solution)/shard_map/pack/pallas_call | solution.py:591
  3.6 1.3 %collective-permute-start.2 = (f32[16,2048]{1,0:T(8,128)S(1)}, f32[16,2048]{1,0:T(8,128)S(1)}, u32[]{:S(2)}, u32[]{:S(2)}) collective-permute-start(f32[16,2048]{1,0:T(8,128)S(1)} %get-tuple-element.24.first_ref.refs_1_.b0_ref.refs_3_), channel_id=1, source_target_pairs={{1,0},{2,1},{3,2},{4,3},{5,4},{6,5},{7,6},{8,7},{9,8},{10,9},{11,1... | collective-permute-start | bytes 393224 | tf_op jit(solution)/shard_map/ppermute | solution.py:627
  4.9 4.6 %collective-permute-start = (f32[16,2048]{1,0:T(8,128)S(1)}, f32[16,2048]{1,0:T(8,128)S(1)}, u32[]{:S(2)}, u32[]{:S(2)}) collective-permute-start(f32[16,2048]{1,0:T(8,128)S(1)} %get-tuple-element.23.second_ref.refs_1_.b1_ref.b_ref.refs_4_), channel_id=1, source_target_pairs={{0,1},{1,2},{2,3},{3,4},{4,5},{5,6},{6,7},{7,8},{8,9},{9,10},{10,1... | collective-permute-start | bytes 393224 | tf_op jit(solution)/shard_map/ppermute | solution.py:626
  9.5 7.8 %inner.1 = (bf16[2,16,768,128]{3,2,1,0:T(8,128)(2,1)S(1)}, bf16[2,16,768,128]{3,2,1,0:T(8,128)(2,1)S(1)}, bf16[16,4608]{1,0:T(8,128)(2,1)S(1)}, bf16[16,4608]{1,0:T(8,128)(2,1)S(1)}) custom-call(f32[16,2048]{1,0:T(8,128)S(1)} %get-tuple-element.24.first_ref.refs_1_.b0_ref.refs_3_, f32[16,2048]{1,0:T(8,128)S(1)} %get-tuple-element.23.second_ref.refs_1_.b1_ref.b_ref.refs_4_, ...), custom_call_target="tpu_custom_call" | custom-call | flops 1073741824 | bytes 1048576 | tf_op jit(solution)/shard_map/inner/pallas_call | solution.py:628
  17.3 0.0 collective-permute-done.2.refs_0_
  17.3 3.6 %outer1.1 = (bf16[1,16,768,128]{3,2,1,0:T(8,128)(2,1)S(1)}, f32[16,2048]{1,0:T(8,128)S(1)}, bf16[32,4608]{1,0:T(8,128)(2,1)S(1)}, f32[16,2048]{1,0:T(8,128)S(1)}) custom-call(f32[16,2048]{1,0:T(8,128)S(1)} %collective-permute-done.2.refs_0_, f32[16,2048]{1,0:T(8,128)S(1)} %get-tuple-element.23.second_ref.refs_1_.b1_ref.b_ref.refs_4_, ...), custom_call_target="tpu_custom_call" | custom-call | flops 1073741824 | bytes 1048576 | tf_op jit(solution)/shard_map/outer1/pallas_call | solution.py:617
  20.9 3.5 %collective-permute-start.3 = (f32[16,2048]{1,0:T(8,128)S(1)}, f32[16,2048]{1,0:T(8,128)S(1)}, u32[]{:S(2)}, u32[]{:S(2)}) collective-permute-start(f32[16,2048]{1,0:T(8,128)S(1)} %get-tuple-element.30.f1_ref.f_ref.refs_6_), channel_id=1, source_target_pairs={{0,1},{1,2},{2,3},{3,4},{4,5},{5,6},{6,7},{7,8},{8,9},{9,10},{10,1... | collective-permute-start | bytes 393224 | tf_op jit(solution)/shard_map/ppermute | solution.py:639
  24.4 0.0 collective-permute-done.refs_0_
  24.4 3.6 %outer0.1 = (bf16[1,16,768,128]{3,2,1,0:T(8,128)(2,1)S(1)}, f32[16,2048]{1,0:T(8,128)S(1)}, bf16[32,4608]{1,0:T(8,128)(2,1)S(1)}) custom-call(f32[16,2048]{1,0:T(8,128)S(1)} %collective-permute-done.refs_0_, f32[16,2048]{1,0:T(8,128)S(1)} %get-tuple-element.24.first_ref.refs_1_.b0_ref.refs_3_, f32[8,128]{1,0:T(8,128)S(1)} %get-tuple-element.22.consts_ref.refs_2_.refs_1_, ...), custom_call_target="tpu_custom_call" | custom-call | flops 1073741824 | bytes 1048576 | tf_op jit(solution)/shard_map/outer0/pallas_call | solution.py:617
  28.0 1.3 %collective-permute-start.1 = (f32[16,2048]{1,0:T(8,128)S(1)}, f32[16,2048]{1,0:T(8,128)S(1)}, u32[]{:S(2)}, u32[]{:S(2)}) collective-permute-start(f32[16,2048]{1,0:T(8,128)S(1)} %get-tuple-element.29.own_ref.f0_ref.refs_5_), channel_id=1, source_target_pairs={{1,0},{2,1},{3,2},{4,3},{5,4},{6,5},{7,6},{8,7},{9,8},{10,9},{11,1... | collective-permute-start | bytes 393224 | tf_op jit(solution)/shard_map/ppermute | solution.py:637
  29.3 0.0 collective-permute-done.3.other_ref
  29.3 1.6 %product.1 = (f32[16,2048]{1,0:T(8,128)S(1)}, bf16[32,4608]{1,0:T(8,128)(2,1)S(1)}) custom-call(f32[16,2048]{1,0:T(8,128)S(1)} %collective-permute-done.3.other_ref, f32[16,2048]{1,0:T(8,128)S(1)} %get-tuple-element.29.own_ref.f0_ref.refs_5_, f32[8,128]{1,0:T(8,128)S(1)} %get-tuple-element.22.consts_ref.refs_2_.refs_1_, ...), custom_call_target="tpu_custom_call" | custom-call | flops 536870912 | bytes 1048576 | tf_op jit(solution)/shard_map/product/pallas_call | solution.py:640
  30.9 1.3 %collective-permute-start.4 = (f32[16,2048]{1,0:T(8,128)S(1)}, f32[16,2048]{1,0:T(8,128)S(1)}, u32[]{:S(2)}, u32[]{:S(2)}) collective-permute-start(f32[16,2048]{1,0:T(8,128)S(1)} %get-tuple-element.34.g0_ref.refs_7_), channel_id=1, source_target_pairs={{1,0},{2,1},{3,2},{4,3},{5,4},{6,5},{7,6},{8,7},{9,8},{10,9},{11,1... | collective-permute-start | bytes 393224 | tf_op jit(solution)/shard_map/ppermute | solution.py:648
  32.2 2.7 %collective-permute-done.1.below_ref = f32[16,2048]{1,0:T(8,128)S(1)} collective-permute-done((f32[16,2048]{1,0:T(8,128)S(1)}, f32[16,2048]{1,0:T(8,128)S(1)}, u32[]{:S(2)}, u32[]{:S(2)}) %collective-permute-start.1) | collective-permute-done | bytes 131104 | tf_op jit(solution)/shard_map/ppermute | solution.py:637
  34.9 0.0 copy-start
  34.9 4.2 %gram.1 = (f32[16,2048]{1,0:T(8,128)S(1)}, f32[2,128]{1,0:T(2,128)S(1)}) custom-call(f32[16,2048]{1,0:T(8,128)S(1)} %collective-permute-done.1.below_ref, f32[16,2048]{1,0:T(8,128)S(1)} %get-tuple-element.24.first_ref.refs_1_.b0_ref.refs_3_, f32[16,2048]{1,0:T(8,128)S(1)} %get-tuple-element.23.second_ref.refs_1_.b1_ref.b_ref.refs_4_, ...), custom_call_target="tpu_custom_call" | custom-call | flops 536870912 | bytes 1048576 | tf_op jit(solution)/shard_map/gram/pallas_call | solution.py:649
  39.1 0.0 collective-permute-done.4.below_ref
  39.1 1.1 %moment.1 = f32[64,1,256]{2,1,0:T(1,128)S(1)} custom-call(f32[2,128]{1,0:T(2,128)S(1)} %get-tuple-element.38.sums_ref, f32[16,2048]{1,0:T(8,128)S(1)} %collective-permute-done.4.below_ref, f32[16,2048]{1,0:T(8,128)S(1)} %get-tuple-element.23.second_ref.refs_1_.b1_ref.b_ref.refs_4_, f32[16,2048]{1,0:T(8,128)S(1)} %get-tuple-element.30.f1_ref.f_ref.refs_6_, ...), custom_call_target="tpu_custom_call" | custom-call | flops 536870912 | bytes 1048576 | tf_op jit(solution)/shard_map/moment/pallas_call | solution.py:657
  40.2 30.2 %all_to_all.5.refs_2_ = f32[64,1,256]{2,1,0:T(1,128)S(1)} all-to-all(f32[64,1,256]{2,1,0:T(1,128)S(1)} %moment.1), channel_id=1, replica_groups=mesh['hyp'=8,'rows'=64] {'rows'}, dimensions={0} | all-to-all | bytes 131072 | tf_op jit(solution)/shard_map/all_to_all | solution.py:665
  70.4 0.0 copy-done
  70.4 1.5 %finish.1 = (f32[9,4096]{1,0:T(8,128)}, f32[1,9]{1,0:T(1,128)}) custom-call(s32[32]{0:T(128)S(1)} %copy-done, f32[8,128]{1,0:T(8,128)S(1)} %get-tuple-element.22.consts_ref.refs_2_.refs_1_, f32[64,1,256]{2,1,0:T(1,128)S(1)} %all_to_all.5.refs_2_, f32[16,2048]{1,0:T(8,128)S(1)} %get-tuple-element.24.first_ref.refs_1_.b0_ref.refs_3_, ...), custom_call_target="tpu_custom_call" | custom-call | flops 1048576 | bytes 1048576 | tf_op jit(solution)/shard_map/finish/pallas_call | solution.py:667
Async XLA Ops:
  3.6 13.7 %collective-permute-start.2 = (f32[16,2048]{1,0:T(8,128)S(1)}, f32[16,2048]{1,0:T(8,128)S(1)}, u32[]{:S(2)}, u32[]{:S(2)}) collective-permute-start(f32[16,2048]{1,0:T(8,128)S(1)} %get-tuple-element.24.first_ref.refs_1_.b0_ref.refs_3_), channel_id=1, source_target_pairs={{1,0},{2,1},{3,2},{4,3},{5,4},{6,5},{7,6},{8,7},{9,8},{10,9},{11,1... | collective-permute-start | bytes 393224 | tf_op jit(solution)/shard_map/ppermute | solution.py:627
  4.9 19.5 %collective-permute-start = (f32[16,2048]{1,0:T(8,128)S(1)}, f32[16,2048]{1,0:T(8,128)S(1)}, u32[]{:S(2)}, u32[]{:S(2)}) collective-permute-start(f32[16,2048]{1,0:T(8,128)S(1)} %get-tuple-element.23.second_ref.refs_1_.b1_ref.b_ref.refs_4_), channel_id=1, source_target_pairs={{0,1},{1,2},{2,3},{3,4},{4,5},{5,6},{6,7},{7,8},{8,9},{9,10},{10,1... | collective-permute-start | bytes 393224 | tf_op jit(solution)/shard_map/ppermute | solution.py:626
  20.9 8.4 %collective-permute-start.3 = (f32[16,2048]{1,0:T(8,128)S(1)}, f32[16,2048]{1,0:T(8,128)S(1)}, u32[]{:S(2)}, u32[]{:S(2)}) collective-permute-start(f32[16,2048]{1,0:T(8,128)S(1)} %get-tuple-element.30.f1_ref.f_ref.refs_6_), channel_id=1, source_target_pairs={{0,1},{1,2},{2,3},{3,4},{4,5},{5,6},{6,7},{7,8},{8,9},{9,10},{10,1... | collective-permute-start | bytes 393224 | tf_op jit(solution)/shard_map/ppermute | solution.py:639
  28.0 6.9 %collective-permute-start.1 = (f32[16,2048]{1,0:T(8,128)S(1)}, f32[16,2048]{1,0:T(8,128)S(1)}, u32[]{:S(2)}, u32[]{:S(2)}) collective-permute-start(f32[16,2048]{1,0:T(8,128)S(1)} %get-tuple-element.29.own_ref.f0_ref.refs_5_), channel_id=1, source_target_pairs={{1,0},{2,1},{3,2},{4,3},{5,4},{6,5},{7,6},{8,7},{9,8},{10,9},{11,1... | collective-permute-start | bytes 393224 | tf_op jit(solution)/shard_map/ppermute | solution.py:637
  30.9 8.2 %collective-permute-start.4 = (f32[16,2048]{1,0:T(8,128)S(1)}, f32[16,2048]{1,0:T(8,128)S(1)}, u32[]{:S(2)}, u32[]{:S(2)}) collective-permute-start(f32[16,2048]{1,0:T(8,128)S(1)} %get-tuple-element.34.g0_ref.refs_7_), channel_id=1, source_target_pairs={{1,0},{2,1},{3,2},{4,3},{5,4},{6,5},{7,6},{8,7},{9,8},{10,9},{11,1... | collective-permute-start | bytes 393224 | tf_op jit(solution)/shard_map/ppermute | solution.py:648
  34.9 35.5 %copy-start = (s32[32]{0:T(128)S(1)}, s32[32]{0:T(128)}, u32[]{:S(2)}) copy-start(s32[32]{0:T(128)} %refs_0_.1) | copy-start | bytes 388

commit v6 on v5

--- a/solution.py
+++ b/solution.py
@@ -342,16 +342,16 @@
     return total, sums[1] + left
 
 
-def lines(sums, first):
+def lines(sums):
     row = lax.broadcasted_iota(jnp.int32, (8, TILE), 0)
     lane = lax.broadcasted_iota(jnp.int32, (8, TILE), 1)
-    blocks = [[(high[0:8], low[0:8]), lane == row + STRIDE * (first + k)] for k, (high, low) in enumerate(sums)]
+    blocks = [[(high[0:8], low[0:8]), lane == row + STRIDE * k] for k, (high, low) in enumerate(sums)]
     for start in range(0, len(sums), 8):
         last = [jnp.zeros((8, TILE), F32), jnp.zeros((8, TILE), F32)]
         group = sums[start : start + 8]
         for k, pair in enumerate(group):
             last = [jnp.where(row == k, jnp.broadcast_to(v[8:9], (8, TILE)), t) for v, t in zip(pair, last)]
-        mask = (lane == 8 + STRIDE * (first + start + row)) & (row < len(group))
+        mask = (lane == 8 + STRIDE * (start + row)) & (row < len(group))
         blocks.append([tuple(last), mask])
     placed = [jnp.zeros((8, TILE), F32), jnp.zeros((8, TILE), F32)]
     for (high, low), mask in blocks:
@@ -467,25 +467,26 @@
                 terms = [zero] * SUMS
         return tuple(sums)
 
-    high, low = lines(lax.fori_loop(0, GX // 8, group, ((zero, zero),) * SUMS), 0)
-    sums_ref[0:1, :] = high
-    sums_ref[1:2, :] = low
+    sums = lax.fori_loop(0, GX // 8, group, ((zero, zero),) * SUMS)
+    for k, (high, low) in enumerate(sums):
+        sums_ref[k, 0] = high
+        sums_ref[k, 1] = low
 
 
 def moment_kernel(sums_ref, below_ref, b_ref, f_ref, g_ref, weights_ref, out_ref, spread_ref):
     spread(below_ref, spread_ref)
     zero = jnp.zeros((ROWS, TILE), F32)
-    sums, terms = [(zero, zero)] * 3, [zero] * 3
+    sums = [(sums_ref[k, 0], sums_ref[k, 1]) for k in range(SUMS)]
+    terms = [zero] * 3
     for tile in range(GX):
         here = slice(tile * TILE, (tile + 1) * TILE)
         image = joined(banded(spread_ref, weights_ref, 0, tile))
         factors = (b_ref[:, here], f_ref[:, here], 2.0 * g_ref[:, here])
         terms = [t + v * image for t, v in zip(terms, factors)]
         if tile % 4 == 3:
-            sums, terms = [accumulate(s, t) for s, t in zip(sums, terms)], [zero] * 3
-    high, low = lines(sums, 6)
-    total, left = two_sum(sums_ref[0:1, :], high)
-    both = jnp.concatenate([total, left + (low + sums_ref[1:2, :])], axis=1)
+            sums[6:] = [accumulate(s, t) for s, t in zip(sums[6:], terms)]
+            terms = [zero] * 3
+    both = jnp.concatenate(lines(sums), axis=1)
     out_ref[...] = jnp.broadcast_to(both[None], out_ref.shape)
 
 
@@ -633,10 +634,11 @@
         [feature_tiles()],
         flops=1 << 30,
     )(first, second, consts)
+    under, f1, f1_spread, b_beside = outer(1, below, second)
     over, f0, f0_spread = outer(0, above, first)
+    sent, f0 = lax.optimization_barrier((f1, f0))
+    f_above = lax.ppermute(sent, "rows", down)
     f_below = lax.ppermute(f0, "rows", up)
-    under, f1, f1_spread, b_beside = outer(1, below, second)
-    f_above = lax.ppermute(f1, "rows", down)
     g0, g0_spread = call(
         product_kernel,
         "product",
@@ -649,7 +651,7 @@
     g1, sums = call(
         gram_kernel,
         "gram",
-        (grid_row(), jax.ShapeDtypeStruct((2, TILE), F32)),
+        (grid_row(), jax.ShapeDtypeStruct((SUMS, 2, ROWS, TILE), F32)),
         [VMEM] * 14,
         [spread_row(), spread_row(), pltpu.VMEM((ROWS, WIDE), F32)],
         flops=1 << 29,

time: 72.1 us -> 73.6 us (1.021)
  the two profiles are of different devices: /device:TPU:2 before, /device:TPU:4 now
where the time goes in v6:
time: 73.6 us; the launch traced here: 73.3 us
  blocking collectives  31.5 us (43%)
  Pallas kernels  23.7 us (32%)
  starting transfers between devices  11.9 us (16%)
  waiting for transfers between devices  3.53 us (5%)
  between operations  2.68 us (4%)
    all_to_all x1, blocking collectives, shards(): lax.all_to_all(parts, 'rows', split_axis=0, concat_axis=0, tiled=True)  31.5 us
    pallas_call x1, Pallas kernels, shards(): call(inner_kernel, 'inner', (weight_rows(2), weight_rows(2), spread_row(R...  7.78 us
    pallas_call x2, Pallas kernels, outer(): call(lambda *refs: outer_kernel(slot, *refs), f'outer{slot}', (weight_row...  7.12 us
    ppermute x1, starting transfers between devices, shards(): f_above = lax.ppermute(sent, 'rows', down)  4.55 us
    pallas_call x1, Pallas kernels, shards(): call(gram_kernel, 'gram', (grid_row(), jax.ShapeDtypeStruct((SUMS, 2, ROW...  3.65 us
    ppermute x1, starting transfers between devices, shards(): above = lax.ppermute(second, 'rows', down)  3.49 us
    ppermute x1, waiting for transfers between devices, shards(): f_below = lax.ppermute(f0, 'rows', up)  1.55 us
    pallas_call x1, Pallas kernels, shards(): call(product_kernel, 'product', (grid_row(), spread_row()), [VMEM] * 8, [...  1.5 us
  transfers between devices with their start and end apart: 5, of which 3 were waited for; matrix products, arithmetic and copies ran while one was open for 0% of the time, Pallas kernels for 22%

profile of v6, /device:TPU:4, one launch (start us, length us, event | category | flops | bytes accessed | tf_op | source)
XLA Modules:
  0.0 73.3 jit_solution(16603090307463819881)
XLA Ops:
  2.6 1.1 %pack.1 = (f32[16,2048]{1,0:T(8,128)S(1)}, f32[16,2048]{1,0:T(8,128)S(1)}, f32[8,128]{1,0:T(8,128)S(1)}) custom-call(s32[32]{0:T(128)} %refs_0_.1, f32[2,4096]{1,0:T(2,128)} %offsets_hbm.1, s32[8,4096]{1,0:T(8,128)} %probes_hbm.1, f32[1,4096]{1,0:T(1,128)} %bitcast.2, f32[1]{0:T(128)S(6)} %copy.9.scale_ref, f32[1]{0:T(128)S(6)} %copy.10.amp_ref, ...), custom_call_target="tpu_custom_call" | custom-call | flops 1048576 | bytes 1048576 | tf_op jit(solution)/shard_map/pack/pallas_call | solution.py:592
  3.6 3.5 %collective-permute-start.1 = (f32[16,2048]{1,0:T(8,128)S(1)}, f32[16,2048]{1,0:T(8,128)S(1)}, u32[]{:S(2)}, u32[]{:S(2)}) collective-permute-start(f32[16,2048]{1,0:T(8,128)S(1)} %get-tuple-element.26.second_ref.refs_1_.b1_ref.b_ref.refs_4_), channel_id=1, source_target_pairs={{0,1},{1,2},{2,3},{3,4},{4,5},{5,6},{6,7},{7,8},{8,9},{9,10},{10,1... | collective-permute-start | bytes 393224 | tf_op jit(solution)/shard_map/ppermute | solution.py:627
  7.1 1.3 %collective-permute-start = (f32[16,2048]{1,0:T(8,128)S(1)}, f32[16,2048]{1,0:T(8,128)S(1)}, u32[]{:S(2)}, u32[]{:S(2)}) collective-permute-start(f32[16,2048]{1,0:T(8,128)S(1)} %get-tuple-element.25.first_ref.refs_1_.b0_ref.refs_3_), channel_id=1, source_target_pairs={{1,0},{2,1},{3,2},{4,3},{5,4},{6,5},{7,6},{8,7},{9,8},{10,9},{11,1... | collective-permute-start | bytes 393224 | tf_op jit(solution)/shard_map/ppermute | solution.py:628
  8.4 7.8 %inner.1 = (bf16[2,16,768,128]{3,2,1,0:T(8,128)(2,1)S(1)}, bf16[2,16,768,128]{3,2,1,0:T(8,128)(2,1)S(1)}, bf16[16,4608]{1,0:T(8,128)(2,1)S(1)}, bf16[16,4608]{1,0:T(8,128)(2,1)S(1)}) custom-call(f32[16,2048]{1,0:T(8,128)S(1)} %get-tuple-element.25.first_ref.refs_1_.b0_ref.refs_3_, f32[16,2048]{1,0:T(8,128)S(1)} %get-tuple-element.26.second_ref.refs_1_.b1_ref.b_ref.refs_4_, ...), custom_call_target="tpu_custom_call" | custom-call | flops 1073741824 | bytes 1048576 | tf_op jit(solution)/shard_map/inner/pallas_call | solution.py:629
  16.2 0.0 collective-permute-done.1.refs_0_
  16.2 3.5 %outer0.1 = (bf16[1,16,768,128]{3,2,1,0:T(8,128)(2,1)S(1)}, f32[16,2048]{1,0:T(8,128)S(1)}, bf16[32,4608]{1,0:T(8,128)(2,1)S(1)}) custom-call(f32[16,2048]{1,0:T(8,128)S(1)} %collective-permute-done.1.refs_0_, f32[16,2048]{1,0:T(8,128)S(1)} %get-tuple-element.25.first_ref.refs_1_.b0_ref.refs_3_, f32[8,128]{1,0:T(8,128)S(1)} %get-tuple-element.24.consts_ref.refs_2_.refs_1_, ...), custom_call_target="tpu_custom_call" | custom-call | flops 1073741824 | bytes 1048576 | tf_op jit(solution)/shard_map/outer0/pallas_call | solution.py:618
  19.8 0.0 collective-permute-done.refs_0_
  19.8 3.6 %outer1.1 = (bf16[1,16,768,128]{3,2,1,0:T(8,128)(2,1)S(1)}, f32[16,2048]{1,0:T(8,128)S(1)}, bf16[32,4608]{1,0:T(8,128)(2,1)S(1)}, f32[16,2048]{1,0:T(8,128)S(1)}) custom-call(f32[16,2048]{1,0:T(8,128)S(1)} %collective-permute-done.refs_0_, f32[16,2048]{1,0:T(8,128)S(1)} %get-tuple-element.26.second_ref.refs_1_.b1_ref.b_ref.refs_4_, ...), custom_call_target="tpu_custom_call" | custom-call | flops 1073741824 | bytes 1048576 | tf_op jit(solution)/shard_map/outer1/pallas_call | solution.py:618
  23.4 4.5 %collective-permute-start.3 = (f32[16,2048]{1,0:T(8,128)S(1)}, f32[16,2048]{1,0:T(8,128)S(1)}, u32[]{:S(2)}, u32[]{:S(2)}) collective-permute-start(f32[16,2048]{1,0:T(8,128)S(1)} %get-tuple-element.34.f1_ref.f_ref.refs_6_), channel_id=1, source_target_pairs={{0,1},{1,2},{2,3},{3,4},{4,5},{5,6},{6,7},{7,8},{8,9},{9,10},{10,1... | collective-permute-start | bytes 393224 | tf_op jit(solution)/shard_map/ppermute | solution.py:640
  27.9 1.3 %collective-permute-start.2 = (f32[16,2048]{1,0:T(8,128)S(1)}, f32[16,2048]{1,0:T(8,128)S(1)}, u32[]{:S(2)}, u32[]{:S(2)}) collective-permute-start(f32[16,2048]{1,0:T(8,128)S(1)} %get-tuple-element.33.own_ref.f0_ref.refs_5_), channel_id=1, source_target_pairs={{1,0},{2,1},{3,2},{4,3},{5,4},{6,5},{7,6},{8,7},{9,8},{10,9},{11,1... | collective-permute-start | bytes 393224 | tf_op jit(solution)/shard_map/ppermute | solution.py:641
  29.2 1.2 %collective-permute-done.3.other_ref = f32[16,2048]{1,0:T(8,128)S(1)} collective-permute-done((f32[16,2048]{1,0:T(8,128)S(1)}, f32[16,2048]{1,0:T(8,128)S(1)}, u32[]{:S(2)}, u32[]{:S(2)}) %collective-permute-start.3) | collective-permute-done | bytes 131104 | tf_op jit(solution)/shard_map/ppermute | solution.py:640
  30.4 1.5 %product.1 = (f32[16,2048]{1,0:T(8,128)S(1)}, bf16[32,4608]{1,0:T(8,128)(2,1)S(1)}) custom-call(f32[16,2048]{1,0:T(8,128)S(1)} %collective-permute-done.3.other_ref, f32[16,2048]{1,0:T(8,128)S(1)} %get-tuple-element.33.own_ref.f0_ref.refs_5_, f32[8,128]{1,0:T(8,128)S(1)} %get-tuple-element.24.consts_ref.refs_2_.refs_1_, ...), custom_call_target="tpu_custom_call" | custom-call | flops 536870912 | bytes 1048576 | tf_op jit(solution)/shard_map/product/pallas_call | solution.py:642
  32.0 1.3 %collective-permute-start.4 = (f32[16,2048]{1,0:T(8,128)S(1)}, f32[16,2048]{1,0:T(8,128)S(1)}, u32[]{:S(2)}, u32[]{:S(2)}) collective-permute-start(f32[16,2048]{1,0:T(8,128)S(1)} %get-tuple-element.38.g0_ref.refs_7_), channel_id=1, source_target_pairs={{1,0},{2,1},{3,2},{4,3},{5,4},{6,5},{7,6},{8,7},{9,8},{10,9},{11,1... | collective-permute-start | bytes 393224 | tf_op jit(solution)/shard_map/ppermute | solution.py:650
  33.3 1.6 %collective-permute-done.2.below_ref = f32[16,2048]{1,0:T(8,128)S(1)} collective-permute-done((f32[16,2048]{1,0:T(8,128)S(1)}, f32[16,2048]{1,0:T(8,128)S(1)}, u32[]{:S(2)}, u32[]{:S(2)}) %collective-permute-start.2) | collective-permute-done | bytes 131104 | tf_op jit(solution)/shard_map/ppermute | solution.py:641
  34.8 0.0 copy-start
  34.8 3.7 %gram.1 = (f32[16,2048]{1,0:T(8,128)S(1)}, f32[9,2,16,128]{3,2,1,0:T(8,128)S(1)}) custom-call(f32[16,2048]{1,0:T(8,128)S(1)} %collective-permute-done.2.below_ref, f32[16,2048]{1,0:T(8,128)S(1)} %get-tuple-element.25.first_ref.refs_1_.b0_ref.refs_3_, f32[16,2048]{1,0:T(8,128)S(1)} %get-tuple-element.26.second_ref.refs_1_.b1_ref.b_ref.refs_4_, ...), custom_call_target="tpu_custom_call" | custom-call | flops 536870912 | bytes 1048576 | tf_op jit(solution)/shard_map/gram/pallas_call | solution.py:651
  38.5 0.8 %collective-permute-done.4.below_ref = f32[16,2048]{1,0:T(8,128)S(1)} collective-permute-done((f32[16,2048]{1,0:T(8,128)S(1)}, f32[16,2048]{1,0:T(8,128)S(1)}, u32[]{:S(2)}, u32[]{:S(2)}) %collective-permute-start.4) | collective-permute-done | bytes 131104 | tf_op jit(solution)/shard_map/ppermute | solution.py:650
  39.2 1.1 %moment.1 = f32[64,1,256]{2,1,0:T(1,128)S(1)} custom-call(f32[9,2,16,128]{3,2,1,0:T(8,128)S(1)} %get-tuple-element.42.sums_ref, f32[16,2048]{1,0:T(8,128)S(1)} %collective-permute-done.4.below_ref, f32[16,2048]{1,0:T(8,128)S(1)} %get-tuple-element.26.second_ref.refs_1_.b1_ref.b_ref.refs_4_, f32[16,2048]{1,0:T(8,128)S(1)} %get-tuple-element.34.f1_ref.f_ref.refs_6_, ...), custom_call_target="tpu_custom_call" | custom-call | flops 536870912 | bytes 1048576 | tf_op jit(solution)/shard_map/moment/pallas_call | solution.py:659
  40.3 31.5 %all_to_all.5.refs_2_ = f32[64,1,256]{2,1,0:T(1,128)S(1)} all-to-all(f32[64,1,256]{2,1,0:T(1,128)S(1)} %moment.1), channel_id=1, replica_groups=mesh['hyp'=8,'rows'=64] {'rows'}, dimensions={0} | all-to-all | bytes 131072 | tf_op jit(solution)/shard_map/all_to_all | solution.py:667
  71.8 0.0 copy-done
  71.8 1.5 %finish.1 = (f32[9,4096]{1,0:T(8,128)}, f32[1,9]{1,0:T(1,128)}) custom-call(s32[32]{0:T(128)S(1)} %copy-done, f32[8,128]{1,0:T(8,128)S(1)} %get-tuple-element.24.consts_ref.refs_2_.refs_1_, f32[64,1,256]{2,1,0:T(1,128)S(1)} %all_to_all.5.refs_2_, f32[16,2048]{1,0:T(8,128)S(1)} %get-tuple-element.25.first_ref.refs_1_.b0_ref.refs_3_, ...), custom_call_target="tpu_custom_call" | custom-call | flops 1048576 | bytes 1048576 | tf_op jit(solution)/shard_map/finish/pallas_call | solution.py:669
Async XLA Ops:
  3.6 12.6 %collective-permute-start.1 = (f32[16,2048]{1,0:T(8,128)S(1)}, f32[16,2048]{1,0:T(8,128)S(1)}, u32[]{:S(2)}, u32[]{:S(2)}) collective-permute-start(f32[16,2048]{1,0:T(8,128)S(1)} %get-tuple-element.26.second_ref.refs_1_.b1_ref.b_ref.refs_4_), channel_id=1, source_target_pairs={{0,1},{1,2},{2,3},{3,4},{4,5},{5,6},{6,7},{7,8},{8,9},{9,10},{10,1... | collective-permute-start | bytes 393224 | tf_op jit(solution)/shard_map/ppermute | solution.py:627
  7.1 12.7 %collective-permute-start = (f32[16,2048]{1,0:T(8,128)S(1)}, f32[16,2048]{1,0:T(8,128)S(1)}, u32[]{:S(2)}, u32[]{:S(2)}) collective-permute-start(f32[16,2048]{1,0:T(8,128)S(1)} %get-tuple-element.25.first_ref.refs_1_.b0_ref.refs_3_), channel_id=1, source_target_pairs={{1,0},{2,1},{3,2},{4,3},{5,4},{6,5},{7,6},{8,7},{9,8},{10,9},{11,1... | collective-permute-start | bytes 393224 | tf_op jit(solution)/shard_map/ppermute | solution.py:628
  23.4 7.1 %collective-permute-start.3 = (f32[16,2048]{1,0:T(8,128)S(1)}, f32[16,2048]{1,0:T(8,128)S(1)}, u32[]{:S(2)}, u32[]{:S(2)}) collective-permute-start(f32[16,2048]{1,0:T(8,128)S(1)} %get-tuple-element.34.f1_ref.f_ref.refs_6_), channel_id=1, source_target_pairs={{0,1},{1,2},{2,3},{3,4},{4,5},{5,6},{6,7},{7,8},{8,9},{9,10},{10,1... | collective-permute-start | bytes 393224 | tf_op jit(solution)/shard_map/ppermute | solution.py:640
  27.9 6.9 %collective-permute-start.2 = (f32[16,2048]{1,0:T(8,128)S(1)}, f32[16,2048]{1,0:T(8,128)S(1)}, u32[]{:S(2)}, u32[]{:S(2)}) collective-permute-start(f32[16,2048]{1,0:T(8,128)S(1)} %get-tuple-element.33.own_ref.f0_ref.refs_5_), channel_id=1, source_target_pairs={{1,0},{2,1},{3,2},{4,3},{5,4},{6,5},{7,6},{8,7},{9,8},{10,9},{11,1... | collective-permute-start | bytes 393224 | tf_op jit(solution)/shard_map/ppermute | solution.py:641
  32.0 7.3 %collective-permute-start.4 = (f32[16,2048]{1,0:T(8,128)S(1)}, f32[16,2048]{1,0:T(8,128)S(1)}, u32[]{:S(2)}, u32[]{:S(2)}) collective-permute-start(f32[16,2048]{1,0:T(8,128)S(1)} %get-tuple-element.38.g0_ref.refs_7_), channel_id=1, source_target_pairs={{1,0},{2,1},{3,2},{4,3},{5,4},{6,5},{7,6},{8,7},{9,8},{10,9},{11,1... | collective-permute-start | bytes 393224 | tf_op jit(solution)/shard_map/ppermute | solution.py:650
  34.8 37.0 %copy-start = (s32[32]{0:T(128)S(1)}, s32[32]{0:T(128)}, u32[]{:S(2)}) copy-start(s32[32]{0:T(128)} %refs_0_.1) | copy-start | bytes 388

commit v7 on v6

--- a/solution.py
+++ b/solution.py
@@ -634,11 +634,10 @@
         [feature_tiles()],
         flops=1 << 30,
     )(first, second, consts)
+    over, f0, f0_spread = outer(0, above, first)
+    f_below = lax.ppermute(f0, "rows", up)
     under, f1, f1_spread, b_beside = outer(1, below, second)
-    over, f0, f0_spread = outer(0, above, first)
-    sent, f0 = lax.optimization_barrier((f1, f0))
-    f_above = lax.ppermute(sent, "rows", down)
-    f_below = lax.ppermute(f0, "rows", up)
+    f_above = lax.ppermute(f1, "rows", down)
     g0, g0_spread = call(
         product_kernel,
         "product",

time: 73.6 us -> 72 us (0.978)
  the two profiles are of different devices: /device:TPU:4 before, /device:TPU:2 now
where the time goes in v7:
time: 72 us; the launch traced here: 71.7 us
  blocking collectives  30.7 us (43%)
  Pallas kernels  23.7 us (33%)
  starting transfers between devices  11.9 us (17%)
  waiting for transfers between devices  2.75 us (4%)
  between operations  2.69 us (4%)
    all_to_all x1, blocking collectives, shards(): lax.all_to_all(parts, 'rows', split_axis=0, concat_axis=0, tiled=True)  30.7 us
    pallas_call x1, Pallas kernels, shards(): call(inner_kernel, 'inner', (weight_rows(2), weight_rows(2), spread_row(R...  7.78 us
    pallas_call x2, Pallas kernels, outer(): call(lambda *refs: outer_kernel(slot, *refs), f'outer{slot}', (weight_row...  7.12 us
    ppermute x1, starting transfers between devices, shards(): above = lax.ppermute(second, 'rows', down)  4.55 us
    pallas_call x1, Pallas kernels, shards(): call(gram_kernel, 'gram', (grid_row(), jax.ShapeDtypeStruct((SUMS, 2, ROW...  3.66 us
    ppermute x1, starting transfers between devices, shards(): f_above = lax.ppermute(f1, 'rows', down)  3.5 us
    ppermute x1, waiting for transfers between devices, shards(): f_below = lax.ppermute(f0, 'rows', up)  2.74 us
    pallas_call x1, Pallas kernels, shards(): call(product_kernel, 'product', (grid_row(), spread_row()), [VMEM] * 8, [...  1.51 us
  transfers between devices with their start and end apart: 5, of which 1 were waited for; matrix products, arithmetic and copies ran while one was open for 0% of the time, Pallas kernels for 28%

profile of v7, /device:TPU:2, one launch (start us, length us, event | category | flops | bytes accessed | tf_op | source)
XLA Modules:
  0.0 71.7 jit_solution(5354833821666334729)
XLA Ops:
  2.6 1.1 %pack.1 = (f32[16,2048]{1,0:T(8,128)S(1)}, f32[16,2048]{1,0:T(8,128)S(1)}, f32[8,128]{1,0:T(8,128)S(1)}) custom-call(s32[32]{0:T(128)} %refs_0_.1, f32[2,4096]{1,0:T(2,128)} %offsets_hbm.1, s32[8,4096]{1,0:T(8,128)} %probes_hbm.1, f32[1,4096]{1,0:T(1,128)} %bitcast.2, f32[1]{0:T(128)S(6)} %copy.9.scale_ref, f32[1]{0:T(128)S(6)} %copy.10.amp_ref, ...), custom_call_target="tpu_custom_call" | custom-call | flops 1048576 | bytes 1048576 | tf_op jit(solution)/shard_map/pack/pallas_call | solution.py:592
  3.6 1.3 %collective-permute-start.2 = (f32[16,2048]{1,0:T(8,128)S(1)}, f32[16,2048]{1,0:T(8,128)S(1)}, u32[]{:S(2)}, u32[]{:S(2)}) collective-permute-start(f32[16,2048]{1,0:T(8,128)S(1)} %get-tuple-element.24.first_ref.refs_1_.b0_ref.refs_3_), channel_id=1, source_target_pairs={{1,0},{2,1},{3,2},{4,3},{5,4},{6,5},{7,6},{8,7},{9,8},{10,9},{11,1... | collective-permute-start | bytes 393224 | tf_op jit(solution)/shard_map/ppermute | solution.py:628
  4.9 4.6 %collective-permute-start = (f32[16,2048]{1,0:T(8,128)S(1)}, f32[16,2048]{1,0:T(8,128)S(1)}, u32[]{:S(2)}, u32[]{:S(2)}) collective-permute-start(f32[16,2048]{1,0:T(8,128)S(1)} %get-tuple-element.23.second_ref.refs_1_.b1_ref.b_ref.refs_4_), channel_id=1, source_target_pairs={{0,1},{1,2},{2,3},{3,4},{4,5},{5,6},{6,7},{7,8},{8,9},{9,10},{10,1... | collective-permute-start | bytes 393224 | tf_op jit(solution)/shard_map/ppermute | solution.py:627
  9.5 7.8 %inner.1 = (bf16[2,16,768,128]{3,2,1,0:T(8,128)(2,1)S(1)}, bf16[2,16,768,128]{3,2,1,0:T(8,128)(2,1)S(1)}, bf16[16,4608]{1,0:T(8,128)(2,1)S(1)}, bf16[16,4608]{1,0:T(8,128)(2,1)S(1)}) custom-call(f32[16,2048]{1,0:T(8,128)S(1)} %get-tuple-element.24.first_ref.refs_1_.b0_ref.refs_3_, f32[16,2048]{1,0:T(8,128)S(1)} %get-tuple-element.23.second_ref.refs_1_.b1_ref.b_ref.refs_4_, ...), custom_call_target="tpu_custom_call" | custom-call | flops 1073741824 | bytes 1048576 | tf_op jit(solution)/shard_map/inner/pallas_call | solution.py:629
  17.3 0.0 collective-permute-done.2.refs_0_
  17.3 3.6 %outer1.1 = (bf16[1,16,768,128]{3,2,1,0:T(8,128)(2,1)S(1)}, f32[16,2048]{1,0:T(8,128)S(1)}, bf16[32,4608]{1,0:T(8,128)(2,1)S(1)}, f32[16,2048]{1,0:T(8,128)S(1)}) custom-call(f32[16,2048]{1,0:T(8,128)S(1)} %collective-permute-done.2.refs_0_, f32[16,2048]{1,0:T(8,128)S(1)} %get-tuple-element.23.second_ref.refs_1_.b1_ref.b_ref.refs_4_, ...), custom_call_target="tpu_custom_call" | custom-call | flops 1073741824 | bytes 1048576 | tf_op jit(solution)/shard_map/outer1/pallas_call | solution.py:618
  20.9 3.5 %collective-permute-start.3 = (f32[16,2048]{1,0:T(8,128)S(1)}, f32[16,2048]{1,0:T(8,128)S(1)}, u32[]{:S(2)}, u32[]{:S(2)}) collective-permute-start(f32[16,2048]{1,0:T(8,128)S(1)} %get-tuple-element.30.f1_ref.f_ref.refs_6_), channel_id=1, source_target_pairs={{0,1},{1,2},{2,3},{3,4},{4,5},{5,6},{6,7},{7,8},{8,9},{9,10},{10,1... | collective-permute-start | bytes 393224 | tf_op jit(solution)/shard_map/ppermute | solution.py:640
  24.4 0.0 collective-permute-done.refs_0_
  24.4 3.5 %outer0.1 = (bf16[1,16,768,128]{3,2,1,0:T(8,128)(2,1)S(1)}, f32[16,2048]{1,0:T(8,128)S(1)}, bf16[32,4608]{1,0:T(8,128)(2,1)S(1)}) custom-call(f32[16,2048]{1,0:T(8,128)S(1)} %collective-permute-done.refs_0_, f32[16,2048]{1,0:T(8,128)S(1)} %get-tuple-element.24.first_ref.refs_1_.b0_ref.refs_3_, f32[8,128]{1,0:T(8,128)S(1)} %get-tuple-element.22.consts_ref.refs_2_.refs_1_, ...), custom_call_target="tpu_custom_call" | custom-call | flops 1073741824 | bytes 1048576 | tf_op jit(solution)/shard_map/outer0/pallas_call | solution.py:618
  28.0 1.3 %collective-permute-start.1 = (f32[16,2048]{1,0:T(8,128)S(1)}, f32[16,2048]{1,0:T(8,128)S(1)}, u32[]{:S(2)}, u32[]{:S(2)}) collective-permute-start(f32[16,2048]{1,0:T(8,128)S(1)} %get-tuple-element.29.own_ref.f0_ref.refs_5_), channel_id=1, source_target_pairs={{1,0},{2,1},{3,2},{4,3},{5,4},{6,5},{7,6},{8,7},{9,8},{10,9},{11,1... | collective-permute-start | bytes 393224 | tf_op jit(solution)/shard_map/ppermute | solution.py:638
  29.3 0.0 collective-permute-done.3.other_ref
  29.3 1.5 %product.1 = (f32[16,2048]{1,0:T(8,128)S(1)}, bf16[32,4608]{1,0:T(8,128)(2,1)S(1)}) custom-call(f32[16,2048]{1,0:T(8,128)S(1)} %collective-permute-done.3.other_ref, f32[16,2048]{1,0:T(8,128)S(1)} %get-tuple-element.29.own_ref.f0_ref.refs_5_, f32[8,128]{1,0:T(8,128)S(1)} %get-tuple-element.22.consts_ref.refs_2_.refs_1_, ...), custom_call_target="tpu_custom_call" | custom-call | flops 536870912 | bytes 1048576 | tf_op jit(solution)/shard_map/product/pallas_call | solution.py:641
  30.8 1.3 %collective-permute-start.4 = (f32[16,2048]{1,0:T(8,128)S(1)}, f32[16,2048]{1,0:T(8,128)S(1)}, u32[]{:S(2)}, u32[]{:S(2)}) collective-permute-start(f32[16,2048]{1,0:T(8,128)S(1)} %get-tuple-element.34.g0_ref.refs_7_), channel_id=1, source_target_pairs={{1,0},{2,1},{3,2},{4,3},{5,4},{6,5},{7,6},{8,7},{9,8},{10,9},{11,1... | collective-permute-start | bytes 393224 | tf_op jit(solution)/shard_map/ppermute | solution.py:649
  32.1 2.7 %collective-permute-done.1.below_ref = f32[16,2048]{1,0:T(8,128)S(1)} collective-permute-done((f32[16,2048]{1,0:T(8,128)S(1)}, f32[16,2048]{1,0:T(8,128)S(1)}, u32[]{:S(2)}, u32[]{:S(2)}) %collective-permute-start.1) | collective-permute-done | bytes 131104 | tf_op jit(solution)/shard_map/ppermute | solution.py:638
  34.8 0.0 copy-start
  34.8 3.7 %gram.1 = (f32[16,2048]{1,0:T(8,128)S(1)}, f32[9,2,16,128]{3,2,1,0:T(8,128)S(1)}) custom-call(f32[16,2048]{1,0:T(8,128)S(1)} %collective-permute-done.1.below_ref, f32[16,2048]{1,0:T(8,128)S(1)} %get-tuple-element.24.first_ref.refs_1_.b0_ref.refs_3_, f32[16,2048]{1,0:T(8,128)S(1)} %get-tuple-element.23.second_ref.refs_1_.b1_ref.b_ref.refs_4_, ...), custom_call_target="tpu_custom_call" | custom-call | flops 536870912 | bytes 1048576 | tf_op jit(solution)/shard_map/gram/pallas_call | solution.py:650
  38.5 0.0 collective-permute-done.4.below_ref
  38.5 1.1 %moment.1 = f32[64,1,256]{2,1,0:T(1,128)S(1)} custom-call(f32[9,2,16,128]{3,2,1,0:T(8,128)S(1)} %get-tuple-element.38.sums_ref, f32[16,2048]{1,0:T(8,128)S(1)} %collective-permute-done.4.below_ref, f32[16,2048]{1,0:T(8,128)S(1)} %get-tuple-element.23.second_ref.refs_1_.b1_ref.b_ref.refs_4_, f32[16,2048]{1,0:T(8,128)S(1)} %get-tuple-element.30.f1_ref.f_ref.refs_6_, ...), custom_call_target="tpu_custom_call" | custom-call | flops 536870912 | bytes 1048576 | tf_op jit(solution)/shard_map/moment/pallas_call | solution.py:658
  39.6 30.7 %all_to_all.5.refs_2_ = f32[64,1,256]{2,1,0:T(1,128)S(1)} all-to-all(f32[64,1,256]{2,1,0:T(1,128)S(1)} %moment.1), channel_id=1, replica_groups=mesh['hyp'=8,'rows'=64] {'rows'}, dimensions={0} | all-to-all | bytes 131072 | tf_op jit(solution)/shard_map/all_to_all | solution.py:666
  70.3 0.0 copy-done
  70.3 1.5 %finish.1 = (f32[9,4096]{1,0:T(8,128)}, f32[1,9]{1,0:T(1,128)}) custom-call(s32[32]{0:T(128)S(1)} %copy-done, f32[8,128]{1,0:T(8,128)S(1)} %get-tuple-element.22.consts_ref.refs_2_.refs_1_, f32[64,1,256]{2,1,0:T(1,128)S(1)} %all_to_all.5.refs_2_, f32[16,2048]{1,0:T(8,128)S(1)} %get-tuple-element.24.first_ref.refs_1_.b0_ref.refs_3_, ...), custom_call_target="tpu_custom_call" | custom-call | flops 1048576 | bytes 1048576 | tf_op jit(solution)/shard_map/finish/pallas_call | solution.py:668
Async XLA Ops:
  3.6 13.7 %collective-permute-start.2 = (f32[16,2048]{1,0:T(8,128)S(1)}, f32[16,2048]{1,0:T(8,128)S(1)}, u32[]{:S(2)}, u32[]{:S(2)}) collective-permute-start(f32[16,2048]{1,0:T(8,128)S(1)} %get-tuple-element.24.first_ref.refs_1_.b0_ref.refs_3_), channel_id=1, source_target_pairs={{1,0},{2,1},{3,2},{4,3},{5,4},{6,5},{7,6},{8,7},{9,8},{10,9},{11,1... | collective-permute-start | bytes 393224 | tf_op jit(solution)/shard_map/ppermute | solution.py:628
  4.9 19.5 %collective-permute-start = (f32[16,2048]{1,0:T(8,128)S(1)}, f32[16,2048]{1,0:T(8,128)S(1)}, u32[]{:S(2)}, u32[]{:S(2)}) collective-permute-start(f32[16,2048]{1,0:T(8,128)S(1)} %get-tuple-element.23.second_ref.refs_1_.b1_ref.b_ref.refs_4_), channel_id=1, source_target_pairs={{0,1},{1,2},{2,3},{3,4},{4,5},{5,6},{6,7},{7,8},{8,9},{9,10},{10,1... | collective-permute-start | bytes 393224 | tf_op jit(solution)/shard_map/ppermute | solution.py:627
  20.9 8.4 %collective-permute-start.3 = (f32[16,2048]{1,0:T(8,128)S(1)}, f32[16,2048]{1,0:T(8,128)S(1)}, u32[]{:S(2)}, u32[]{:S(2)}) collective-permute-start(f32[16,2048]{1,0:T(8,128)S(1)} %get-tuple-element.30.f1_ref.f_ref.refs_6_), channel_id=1, source_target_pairs={{0,1},{1,2},{2,3},{3,4},{4,5},{5,6},{6,7},{7,8},{8,9},{9,10},{10,1... | collective-permute-start | bytes 393224 | tf_op jit(solution)/shard_map/ppermute | solution.py:640
  28.0 6.9 %collective-permute-start.1 = (f32[16,2048]{1,0:T(8,128)S(1)}, f32[16,2048]{1,0:T(8,128)S(1)}, u32[]{:S(2)}, u32[]{:S(2)}) collective-permute-start(f32[16,2048]{1,0:T(8,128)S(1)} %get-tuple-element.29.own_ref.f0_ref.refs_5_), channel_id=1, source_target_pairs={{1,0},{2,1},{3,2},{4,3},{5,4},{6,5},{7,6},{8,7},{9,8},{10,9},{11,1... | collective-permute-start | bytes 393224 | tf_op jit(solution)/shard_map/ppermute | solution.py:638
  30.8 7.7 %collective-permute-start.4 = (f32[16,2048]{1,0:T(8,128)S(1)}, f32[16,2048]{1,0:T(8,128)S(1)}, u32[]{:S(2)}, u32[]{:S(2)}) collective-permute-start(f32[16,2048]{1,0:T(8,128)S(1)} %get-tuple-element.34.g0_ref.refs_7_), channel_id=1, source_target_pairs={{1,0},{2,1},{3,2},{4,3},{5,4},{6,5},{7,6},{8,7},{9,8},{10,9},{11,1... | collective-permute-start | bytes 393224 | tf_op jit(solution)/shard_map/ppermute | solution.py:649
  34.8 35.5 %copy-start = (s32[32]{0:T(128)S(1)}, s32[32]{0:T(128)}, u32[]{:S(2)}) copy-start(s32[32]{0:T(128)} %refs_0_.1) | copy-start | bytes 388

commit v8 on v7

--- a/solution.py
+++ b/solution.py
@@ -167,7 +167,7 @@
     return split_rows(values, target).astype(BF16)
 
 
-def fill_weights(targets, feats_ref, consts_ref, rows):
+def fill_weights(targets, feats_ref, consts_ref, rows, also=None):
     factor = constant(consts_ref, FACTOR)
     reach = jnp.broadcast_to(constant(consts_ref, REACH), (TILE, TILE))
     top = jnp.broadcast_to(constant(consts_ref, TOP), (TILE, TILE))
@@ -194,6 +194,8 @@
                 base = k * 2 * TILE
                 weights_ref[combo, tile, base : base + TILE, :] = high
                 weights_ref[combo, tile, base + TILE : base + 2 * TILE, :] = low
+        if also is not None:
+            also(tile)
         return carry
 
     lax.fori_loop(0, GX, one, 0, unroll=8 // len(targets))
@@ -393,10 +395,25 @@
     beside_ref, feats_ref, spread_ref = more if slot else (None, *more)
     rows = feature_rows()
     source_features(other_ref, constant(consts_ref, FACTOR), rows, feats_ref)
-    fill_weights(((own_ref, 2 * slot - 1, weights_ref, 0),), feats_ref, consts_ref, rows)
+    noise = constant(consts_ref, NOISE)
+
+    def own_part(tile):
+        here = lanes(tile)
+        both = banded(spread0_ref, left_ref, slot, tile) + banded(spread1_ref, right_ref, slot, tile)
+        out_ref[:, here] = noise * own_ref[:, here] + joined(both)
+
+    targets = ((own_ref, 2 * slot - 1, weights_ref, 0),)
+    fill_weights(targets, feats_ref, consts_ref, rows, own_part)
     spread_sides(other_ref, spread_ref)
-    terms = ((spread_ref, weights_ref, 0), (spread0_ref, left_ref, slot), (spread1_ref, right_ref, slot))
-    apply_row(own_ref, terms, consts_ref, out_ref, out_spread_ref, beside_ref)
+    spread_ends(out_spread_ref)
+    for tile in range(GX):
+        here = slice(tile * TILE, (tile + 1) * TILE)
+        halo = joined(banded(spread_ref, weights_ref, 0, tile))
+        if beside_ref is not None:
+            beside_ref[:, here] = halo
+        total = out_ref[:, here] + halo
+        out_ref[:, here] = total
+        spread_tile(total, out_spread_ref, tile)
 
 
 def product_kernel(

time: 72 us -> 71 us (0.986)
  Pallas kernels: 23.7 us -> 22.6 us
    pallas_call x2, Pallas kernels: 7.12 us -> 6.03 us  [outer(): call(lambda *refs: outer_kernel(slot, *refs), f'outer{slot}', (weight_row...]
  transfers between devices with their start and end apart: 5 -> 5, of which waited for: 1 -> 1; matrix products, arithmetic and copies ran while one was open for 0% -> 0% of each run, Pallas kernels for 28% -> 27%
where the time goes in v8:
time: 71 us; the launch traced here: 70.6 us
  blocking collectives  30.7 us (43%)
  Pallas kernels  22.6 us (32%)
  starting transfers between devices  11.9 us (17%)
  waiting for transfers between devices  2.75 us (4%)
  between operations  2.69 us (4%)
    all_to_all x1, blocking collectives, shards(): lax.all_to_all(parts, 'rows', split_axis=0, concat_axis=0, tiled=True)  30.7 us
    pallas_call x1, Pallas kernels, shards(): call(inner_kernel, 'inner', (weight_rows(2), weight_rows(2), spread_row(R...  7.78 us
    pallas_call x2, Pallas kernels, outer(): call(lambda *refs: outer_kernel(slot, *refs), f'outer{slot}', (weight_row...  6.03 us
    ppermute x1, starting transfers between devices, shards(): above = lax.ppermute(second, 'rows', down)  4.55 us
    pallas_call x1, Pallas kernels, shards(): call(gram_kernel, 'gram', (grid_row(), jax.ShapeDtypeStruct((SUMS, 2, ROW...  3.65 us
    ppermute x1, starting transfers between devices, shards(): f_above = lax.ppermute(f1, 'rows', down)  3.5 us
    ppermute x1, waiting for transfers between devices, shards(): f_below = lax.ppermute(f0, 'rows', up)  2.74 us
    pallas_call x1, Pallas kernels, shards(): call(product_kernel, 'product', (grid_row(), spread_row()), [VMEM] * 8, [...  1.51 us
  transfers between devices with their start and end apart: 5, of which 1 were waited for; matrix products, arithmetic and copies ran while one was open for 0% of the time, Pallas kernels for 27%

profile of v8, /device:TPU:2, one launch (start us, length us, event | category | flops | bytes accessed | tf_op | source)
XLA Modules:
  0.0 70.6 jit_solution(15593720968703901512)
XLA Ops:
  2.6 1.1 %pack.1 = (f32[16,2048]{1,0:T(8,128)S(1)}, f32[16,2048]{1,0:T(8,128)S(1)}, f32[8,128]{1,0:T(8,128)S(1)}) custom-call(s32[32]{0:T(128)} %refs_0_.1, f32[2,4096]{1,0:T(2,128)} %offsets_hbm.1, s32[8,4096]{1,0:T(8,128)} %probes_hbm.1, f32[1,4096]{1,0:T(1,128)} %bitcast.2, f32[1]{0:T(128)S(6)} %copy.9.scale_ref, f32[1]{0:T(128)S(6)} %copy.10.amp_ref, ...), custom_call_target="tpu_custom_call" | custom-call | flops 1048576 | bytes 1048576 | tf_op jit(solution)/shard_map/pack/pallas_call | solution.py:609
  3.6 1.3 %collective-permute-start.2 = (f32[16,2048]{1,0:T(8,128)S(1)}, f32[16,2048]{1,0:T(8,128)S(1)}, u32[]{:S(2)}, u32[]{:S(2)}) collective-permute-start(f32[16,2048]{1,0:T(8,128)S(1)} %get-tuple-element.24.first_ref.refs_1_.b0_ref.refs_3_), channel_id=1, source_target_pairs={{1,0},{2,1},{3,2},{4,3},{5,4},{6,5},{7,6},{8,7},{9,8},{10,9},{11,1... | collective-permute-start | bytes 393224 | tf_op jit(solution)/shard_map/ppermute | solution.py:645
  4.9 4.6 %collective-permute-start = (f32[16,2048]{1,0:T(8,128)S(1)}, f32[16,2048]{1,0:T(8,128)S(1)}, u32[]{:S(2)}, u32[]{:S(2)}) collective-permute-start(f32[16,2048]{1,0:T(8,128)S(1)} %get-tuple-element.23.second_ref.refs_1_.b1_ref.b_ref.refs_4_), channel_id=1, source_target_pairs={{0,1},{1,2},{2,3},{3,4},{4,5},{5,6},{6,7},{7,8},{8,9},{9,10},{10,1... | collective-permute-start | bytes 393224 | tf_op jit(solution)/shard_map/ppermute | solution.py:644
  9.5 7.8 %inner.1 = (bf16[2,16,768,128]{3,2,1,0:T(8,128)(2,1)S(1)}, bf16[2,16,768,128]{3,2,1,0:T(8,128)(2,1)S(1)}, bf16[16,4608]{1,0:T(8,128)(2,1)S(1)}, bf16[16,4608]{1,0:T(8,128)(2,1)S(1)}) custom-call(f32[16,2048]{1,0:T(8,128)S(1)} %get-tuple-element.24.first_ref.refs_1_.b0_ref.refs_3_, f32[16,2048]{1,0:T(8,128)S(1)} %get-tuple-element.23.second_ref.refs_1_.b1_ref.b_ref.refs_4_, ...), custom_call_target="tpu_custom_call" | custom-call | flops 1073741824 | bytes 1048576 | tf_op jit(solution)/shard_map/inner/pallas_call | solution.py:646
  17.3 0.0 collective-permute-done.2.refs_0_
  17.3 3.0 %outer1.1 = (bf16[1,16,768,128]{3,2,1,0:T(8,128)(2,1)S(1)}, f32[16,2048]{1,0:T(8,128)S(1)}, bf16[32,4608]{1,0:T(8,128)(2,1)S(1)}, f32[16,2048]{1,0:T(8,128)S(1)}) custom-call(f32[16,2048]{1,0:T(8,128)S(1)} %collective-permute-done.2.refs_0_, f32[16,2048]{1,0:T(8,128)S(1)} %get-tuple-element.23.second_ref.refs_1_.b1_ref.b_ref.refs_4_, ...), custom_call_target="tpu_custom_call" | custom-call | flops 1073741824 | bytes 1048576 | tf_op jit(solution)/shard_map/outer1/pallas_call | solution.py:635
  20.3 3.5 %collective-permute-start.3 = (f32[16,2048]{1,0:T(8,128)S(1)}, f32[16,2048]{1,0:T(8,128)S(1)}, u32[]{:S(2)}, u32[]{:S(2)}) collective-permute-start(f32[16,2048]{1,0:T(8,128)S(1)} %get-tuple-element.30.f1_ref.f_ref.refs_6_), channel_id=1, source_target_pairs={{0,1},{1,2},{2,3},{3,4},{4,5},{5,6},{6,7},{7,8},{8,9},{9,10},{10,1... | collective-permute-start | bytes 393224 | tf_op jit(solution)/shard_map/ppermute | solution.py:657
  23.8 0.0 collective-permute-done.refs_0_
  23.8 3.0 %outer0.1 = (bf16[1,16,768,128]{3,2,1,0:T(8,128)(2,1)S(1)}, f32[16,2048]{1,0:T(8,128)S(1)}, bf16[32,4608]{1,0:T(8,128)(2,1)S(1)}) custom-call(f32[16,2048]{1,0:T(8,128)S(1)} %collective-permute-done.refs_0_, f32[16,2048]{1,0:T(8,128)S(1)} %get-tuple-element.24.first_ref.refs_1_.b0_ref.refs_3_, f32[8,128]{1,0:T(8,128)S(1)} %get-tuple-element.22.consts_ref.refs_2_.refs_1_, ...), custom_call_target="tpu_custom_call" | custom-call | flops 1073741824 | bytes 1048576 | tf_op jit(solution)/shard_map/outer0/pallas_call | solution.py:635
  26.9 1.3 %collective-permute-start.1 = (f32[16,2048]{1,0:T(8,128)S(1)}, f32[16,2048]{1,0:T(8,128)S(1)}, u32[]{:S(2)}, u32[]{:S(2)}) collective-permute-start(f32[16,2048]{1,0:T(8,128)S(1)} %get-tuple-element.29.own_ref.f0_ref.refs_5_), channel_id=1, source_target_pairs={{1,0},{2,1},{3,2},{4,3},{5,4},{6,5},{7,6},{8,7},{9,8},{10,9},{11,1... | collective-permute-start | bytes 393224 | tf_op jit(solution)/shard_map/ppermute | solution.py:655
  28.2 0.0 collective-permute-done.3.other_ref
  28.2 1.5 %product.1 = (f32[16,2048]{1,0:T(8,128)S(1)}, bf16[32,4608]{1,0:T(8,128)(2,1)S(1)}) custom-call(f32[16,2048]{1,0:T(8,128)S(1)} %collective-permute-done.3.other_ref, f32[16,2048]{1,0:T(8,128)S(1)} %get-tuple-element.29.own_ref.f0_ref.refs_5_, f32[8,128]{1,0:T(8,128)S(1)} %get-tuple-element.22.consts_ref.refs_2_.refs_1_, ...), custom_call_target="tpu_custom_call" | custom-call | flops 536870912 | bytes 1048576 | tf_op jit(solution)/shard_map/product/pallas_call | solution.py:658
  29.7 1.3 %collective-permute-start.4 = (f32[16,2048]{1,0:T(8,128)S(1)}, f32[16,2048]{1,0:T(8,128)S(1)}, u32[]{:S(2)}, u32[]{:S(2)}) collective-permute-start(f32[16,2048]{1,0:T(8,128)S(1)} %get-tuple-element.34.g0_ref.refs_7_), channel_id=1, source_target_pairs={{1,0},{2,1},{3,2},{4,3},{5,4},{6,5},{7,6},{8,7},{9,8},{10,9},{11,1... | collective-permute-start | bytes 393224 | tf_op jit(solution)/shard_map/ppermute | solution.py:666
  31.0 2.7 %collective-permute-done.1.below_ref = f32[16,2048]{1,0:T(8,128)S(1)} collective-permute-done((f32[16,2048]{1,0:T(8,128)S(1)}, f32[16,2048]{1,0:T(8,128)S(1)}, u32[]{:S(2)}, u32[]{:S(2)}) %collective-permute-start.1) | collective-permute-done | bytes 131104 | tf_op jit(solution)/shard_map/ppermute | solution.py:655
  33.7 0.0 copy-start
  33.7 3.7 %gram.1 = (f32[16,2048]{1,0:T(8,128)S(1)}, f32[9,2,16,128]{3,2,1,0:T(8,128)S(1)}) custom-call(f32[16,2048]{1,0:T(8,128)S(1)} %collective-permute-done.1.below_ref, f32[16,2048]{1,0:T(8,128)S(1)} %get-tuple-element.24.first_ref.refs_1_.b0_ref.refs_3_, f32[16,2048]{1,0:T(8,128)S(1)} %get-tuple-element.23.second_ref.refs_1_.b1_ref.b_ref.refs_4_, ...), custom_call_target="tpu_custom_call" | custom-call | flops 536870912 | bytes 1048576 | tf_op jit(solution)/shard_map/gram/pallas_call | solution.py:667
  37.4 0.0 collective-permute-done.4.below_ref
  37.4 1.1 %moment.1 = f32[64,1,256]{2,1,0:T(1,128)S(1)} custom-call(f32[9,2,16,128]{3,2,1,0:T(8,128)S(1)} %get-tuple-element.38.sums_ref, f32[16,2048]{1,0:T(8,128)S(1)} %collective-permute-done.4.below_ref, f32[16,2048]{1,0:T(8,128)S(1)} %get-tuple-element.23.second_ref.refs_1_.b1_ref.b_ref.refs_4_, f32[16,2048]{1,0:T(8,128)S(1)} %get-tuple-element.30.f1_ref.f_ref.refs_6_, ...), custom_call_target="tpu_custom_call" | custom-call | flops 536870912 | bytes 1048576 | tf_op jit(solution)/shard_map/moment/pallas_call | solution.py:675
  38.5 30.7 %all_to_all.5.refs_2_ = f32[64,1,256]{2,1,0:T(1,128)S(1)} all-to-all(f32[64,1,256]{2,1,0:T(1,128)S(1)} %moment.1), channel_id=1, replica_groups=mesh['hyp'=8,'rows'=64] {'rows'}, dimensions={0} | all-to-all | bytes 131072 | tf_op jit(solution)/shard_map/all_to_all | solution.py:683
  69.2 0.0 copy-done
  69.2 1.5 %finish.1 = (f32[9,4096]{1,0:T(8,128)}, f32[1,9]{1,0:T(1,128)}) custom-call(s32[32]{0:T(128)S(1)} %copy-done, f32[8,128]{1,0:T(8,128)S(1)} %get-tuple-element.22.consts_ref.refs_2_.refs_1_, f32[64,1,256]{2,1,0:T(1,128)S(1)} %all_to_all.5.refs_2_, f32[16,2048]{1,0:T(8,128)S(1)} %get-tuple-element.24.first_ref.refs_1_.b0_ref.refs_3_, ...), custom_call_target="tpu_custom_call" | custom-call | flops 1048576 | bytes 1048576 | tf_op jit(solution)/shard_map/finish/pallas_call | solution.py:685
Async XLA Ops:
  3.6 13.7 %collective-permute-start.2 = (f32[16,2048]{1,0:T(8,128)S(1)}, f32[16,2048]{1,0:T(8,128)S(1)}, u32[]{:S(2)}, u32[]{:S(2)}) collective-permute-start(f32[16,2048]{1,0:T(8,128)S(1)} %get-tuple-element.24.first_ref.refs_1_.b0_ref.refs_3_), channel_id=1, source_target_pairs={{1,0},{2,1},{3,2},{4,3},{5,4},{6,5},{7,6},{8,7},{9,8},{10,9},{11,1... | collective-permute-start | bytes 393224 | tf_op jit(solution)/shard_map/ppermute | solution.py:645
  4.9 18.9 %collective-permute-start = (f32[16,2048]{1,0:T(8,128)S(1)}, f32[16,2048]{1,0:T(8,128)S(1)}, u32[]{:S(2)}, u32[]{:S(2)}) collective-permute-start(f32[16,2048]{1,0:T(8,128)S(1)} %get-tuple-element.23.second_ref.refs_1_.b1_ref.b_ref.refs_4_), channel_id=1, source_target_pairs={{0,1},{1,2},{2,3},{3,4},{4,5},{5,6},{6,7},{7,8},{8,9},{9,10},{10,1... | collective-permute-start | bytes 393224 | tf_op jit(solution)/shard_map/ppermute | solution.py:644
  20.3 7.8 %collective-permute-start.3 = (f32[16,2048]{1,0:T(8,128)S(1)}, f32[16,2048]{1,0:T(8,128)S(1)}, u32[]{:S(2)}, u32[]{:S(2)}) collective-permute-start(f32[16,2048]{1,0:T(8,128)S(1)} %get-tuple-element.30.f1_ref.f_ref.refs_6_), channel_id=1, source_target_pairs={{0,1},{1,2},{2,3},{3,4},{4,5},{5,6},{6,7},{7,8},{8,9},{9,10},{10,1... | collective-permute-start | bytes 393224 | tf_op jit(solution)/shard_map/ppermute | solution.py:657
  26.9 6.9 %collective-permute-start.1 = (f32[16,2048]{1,0:T(8,128)S(1)}, f32[16,2048]{1,0:T(8,128)S(1)}, u32[]{:S(2)}, u32[]{:S(2)}) collective-permute-start(f32[16,2048]{1,0:T(8,128)S(1)} %get-tuple-element.29.own_ref.f0_ref.refs_5_), channel_id=1, source_target_pairs={{1,0},{2,1},{3,2},{4,3},{5,4},{6,5},{7,6},{8,7},{9,8},{10,9},{11,1... | collective-permute-start | bytes 393224 | tf_op jit(solution)/shard_map/ppermute | solution.py:655
  29.7 7.7 %collective-permute-start.4 = (f32[16,2048]{1,0:T(8,128)S(1)}, f32[16,2048]{1,0:T(8,128)S(1)}, u32[]{:S(2)}, u32[]{:S(2)}) collective-permute-start(f32[16,2048]{1,0:T(8,128)S(1)} %get-tuple-element.34.g0_ref.refs_7_), channel_id=1, source_target_pairs={{1,0},{2,1},{3,2},{4,3},{5,4},{6,5},{7,6},{8,7},{9,8},{10,9},{11,1... | collective-permute-start | bytes 393224 | tf_op jit(solution)/shard_map/ppermute | solution.py:666
  33.7 35.5 %copy-start = (s32[32]{0:T(128)S(1)}, s32[32]{0:T(128)}, u32[]{:S(2)}) copy-start(s32[32]{0:T(128)} %refs_0_.1) | copy-start | bytes 388

commit v9 on v8

--- a/solution.py
+++ b/solution.py
@@ -255,7 +255,7 @@
 GROUP = 16
 
 
-def apply_row(own_ref, terms, consts_ref, out_ref, out_spread_ref, beside_ref=None):
+def apply_row(own_ref, ahead_ref, terms, consts_ref, out_ref, out_spread_ref, beside_ref=None):
     noise = constant(consts_ref, NOISE)
     spread_ends(out_spread_ref)
 
@@ -268,7 +268,7 @@
                 beside_ref[:, here] = joined(both)
             for term in terms[1:]:
                 both = both + banded(*term, tile)
-            total = noise * own_ref[:, here] + joined(both)
+            total = noise * own_ref[:, here] + ahead_ref[:, here] + joined(both)
             out_ref[:, here] = total
             spread_tile(total, out_spread_ref, tile)
         return carry
@@ -366,41 +366,49 @@
 
 
 def inner_kernel(
-    first_ref, second_ref, consts_ref, left_ref, right_ref, spread0_ref, spread1_ref, feats_ref
+    first_ref,
+    second_ref,
+    consts_ref,
+    left_ref,
+    right_ref,
+    spread0_ref,
+    spread1_ref,
+    part0_ref,
+    part1_ref,
+    feats_ref,
 ):
     rows = feature_rows()
+
+    def first_part(tile):
+        for slot, part_ref in enumerate((part0_ref, part1_ref)):
+            part_ref[:, lanes(tile)] = joined(banded(spread0_ref, left_ref, slot, tile))
+
     for slot, (own_ref, weights_ref, spread_ref) in enumerate(
         ((first_ref, left_ref, spread0_ref), (second_ref, right_ref, spread1_ref))
     ):
         source_features(own_ref, constant(consts_ref, FACTOR), rows, feats_ref)
         targets = ((first_ref, slot, weights_ref, 0), (second_ref, slot - 1, weights_ref, 1))
-        fill_weights(targets, feats_ref, consts_ref, rows)
+        fill_weights(targets, feats_ref, consts_ref, rows, first_part if slot else None)
         spread_sides(own_ref, spread_ref)
 
 
-def outer_kernel(
-    slot,
-    other_ref,
-    own_ref,
-    consts_ref,
-    left_ref,
-    right_ref,
-    spread0_ref,
-    spread1_ref,
-    weights_ref,
-    out_ref,
-    out_spread_ref,
-    *more,
-):
-    beside_ref, feats_ref, spread_ref = more if slot else (None, *more)
+def outer_kernel(slot, other_ref, own_ref, consts_ref, part_ref, right_ref, spread1_ref, *more):
+    if slot:
+        weights_ref, out_ref, out_spread_ref, beside_ref, feats_ref, spread_ref = more
+        ahead, beside = (), beside_ref
+    else:
+        f1_ref, weights_ref, out_ref, out_spread_ref, ahead0_ref, ahead1_ref, feats_ref, spread_ref = more
+        ahead, beside = (ahead0_ref, ahead1_ref), None
     rows = feature_rows()
     source_features(other_ref, constant(consts_ref, FACTOR), rows, feats_ref)
     noise = constant(consts_ref, NOISE)
 
     def own_part(tile):
         here = lanes(tile)
-        both = banded(spread0_ref, left_ref, slot, tile) + banded(spread1_ref, right_ref, slot, tile)
-        out_ref[:, here] = noise * own_ref[:, here] + joined(both)
+        own = noise * own_ref[:, here] + part_ref[:, here]
+        out_ref[:, here] = own + joined(banded(spread1_ref, right_ref, slot, tile))
+        for i, ahead_ref in enumerate(ahead):
+            ahead_ref[:, here] = joined(banded(f1_ref, right_ref, i, tile))
 
     targets = ((own_ref, 2 * slot - 1, weights_ref, 0),)
     fill_weights(targets, feats_ref, consts_ref, rows, own_part)
@@ -409,8 +417,8 @@
     for tile in range(GX):
         here = slice(tile * TILE, (tile + 1) * TILE)
         halo = joined(banded(spread_ref, weights_ref, 0, tile))
-        if beside_ref is not None:
-            beside_ref[:, here] = halo
+        if beside is not None:
+            beside[:, here] = halo
         total = out_ref[:, here] + halo
         out_ref[:, here] = total
         spread_tile(total, out_spread_ref, tile)
@@ -419,19 +427,18 @@
 def product_kernel(
     other_ref,
     own_ref,
+    ahead_ref,
     consts_ref,
     left_ref,
-    right_ref,
     weights_ref,
     spread0_ref,
-    spread1_ref,
     out_ref,
     out_spread_ref,
     spread_ref,
 ):
     spread(other_ref, spread_ref)
-    terms = ((spread_ref, weights_ref, 0), (spread0_ref, left_ref, 0), (spread1_ref, right_ref, 0))
-    apply_row(own_ref, terms, consts_ref, out_ref, out_spread_ref)
+    terms = ((spread_ref, weights_ref, 0), (spread0_ref, left_ref, 0))
+    apply_row(own_ref, ahead_ref, terms, consts_ref, out_ref, out_spread_ref)
 
 
 def gram_kernel(
@@ -447,7 +454,7 @@
     right_ref,
     under_ref,
     f0_spread_ref,
-    f1_spread_ref,
+    ahead_ref,
     g0_spread_ref,
     g1_ref,
     sums_ref,
@@ -456,8 +463,8 @@
     f_beside_ref,
 ):
     spread(below_ref, spread_ref)
-    terms = ((spread_ref, under_ref, 0), (f0_spread_ref, left_ref, 1), (f1_spread_ref, right_ref, 1))
-    apply_row(f1_ref, terms, consts_ref, g1_ref, g1_spread_ref, f_beside_ref)
+    terms = ((spread_ref, under_ref, 0), (f0_spread_ref, left_ref, 1))
+    apply_row(f1_ref, ahead_ref, terms, consts_ref, g1_ref, g1_spread_ref, f_beside_ref)
     zero = jnp.zeros((ROWS, TILE), F32)
     noise = constant(consts_ref, NOISE)
 
@@ -631,38 +638,38 @@
         noise,
     )
 
-    def outer(slot, other, own):
+    def outer(slot, other, own, part, *ahead):
         return call(
             lambda *refs: outer_kernel(slot, *refs),
             f"outer{slot}",
-            (weight_rows(1), grid_row(), spread_row()) + (grid_row(),) * slot,
-            [VMEM] * 7,
+            (weight_rows(1), grid_row(), spread_row()) + (pltpu.VMEM((ROWS, WIDE), F32),) * (2 - slot),
+            [VMEM] * (7 - slot),
             [feature_tiles(), spread_row(ROWS)],
             flops=1 << 30,
-        )(other, own, consts, left, right, b0_spread, b1_spread)
+        )(other, own, consts, part, right, b1_spread, *ahead)
 
     above = lax.ppermute(second, "rows", down)
     below = lax.ppermute(first, "rows", up)
-    left, right, b0_spread, b1_spread = call(
+    left, right, _, b1_spread, part0, part1 = call(
         inner_kernel,
         "inner",
-        (weight_rows(2), weight_rows(2), spread_row(ROWS), spread_row(ROWS)),
+        (weight_rows(2), weight_rows(2), spread_row(ROWS), spread_row(ROWS), *(pltpu.VMEM((ROWS, WIDE), F32),) * 2),
         [VMEM] * 3,
         [feature_tiles()],
         flops=1 << 30,
     )(first, second, consts)
-    over, f0, f0_spread = outer(0, above, first)
+    under, f1, f1_spread, b_beside = outer(1, below, second, part1)
+    f_above = lax.ppermute(f1, "rows", down)
+    over, f0, f0_spread, ahead0, ahead1 = outer(0, above, first, part0, f1_spread)
     f_below = lax.ppermute(f0, "rows", up)
-    under, f1, f1_spread, b_beside = outer(1, below, second)
-    f_above = lax.ppermute(f1, "rows", down)
     g0, g0_spread = call(
         product_kernel,
         "product",
         (grid_row(), spread_row()),
-        [VMEM] * 8,
+        [VMEM] * 7,
         [spread_row()],
         flops=1 << 29,
-    )(f_above, f0, consts, left, right, over, f0_spread, f1_spread)
+    )(f_above, f0, ahead0, consts, left, over, f0_spread)
     g_below = lax.ppermute(g0, "rows", up)
     g1, sums = call(
         gram_kernel,
@@ -671,7 +678,7 @@
         [VMEM] * 14,
         [spread_row(), spread_row(), pltpu.VMEM((ROWS, WIDE), F32)],
         flops=1 << 29,
-    )(f_below, first, second, f0, f1, g0, b_beside, consts, left, right, under, f0_spread, f1_spread, g0_spread)
+    )(f_below, first, second, f0, f1, g0, b_beside, consts, left, right, under, f0_spread, ahead1, g0_spread)
     parts = call(
         moment_kernel,
         "moment",

time: 71 us -> 71.3 us (level)
  waiting for transfers between devices: 2.75 us -> 3.69 us
    ppermute x1, waiting for transfers between devices: 2.74 us -> 3.68 us  [shards(): f_below = lax.ppermute(f0, 'rows', up)]
    pallas_call x1, Pallas kernels: 7.78 us -> 8.66 us  [shards(): call(inner_kernel, 'inner', (weight_rows(2), weight_rows(2), spread_row(R...]
where the time goes in v9:
time: 71.3 us; the launch traced here: 71 us
  blocking collectives  30.3 us (42%)
  Pallas kernels  22.4 us (31%)
  starting transfers between devices  11.9 us (17%)
  waiting for transfers between devices  3.69 us (5%)
  between operations  2.68 us (4%)
    all_to_all x1, blocking collectives, shards(): lax.all_to_all(parts, 'rows', split_axis=0, concat_axis=0, tiled=True)  30.3 us
    pallas_call x1, Pallas kernels, shards(): call(inner_kernel, 'inner', (weight_rows(2), weight_rows(2), spread_row(R...  8.66 us
    pallas_call x2, Pallas kernels, outer(): call(lambda *refs: outer_kernel(slot, *refs), f'outer{slot}', (weight_row...  6.04 us
    ppermute x1, starting transfers between devices, shards(): above = lax.ppermute(second, 'rows', down)  4.55 us
    ppermute x1, waiting for transfers between devices, shards(): f_below = lax.ppermute(f0, 'rows', up)  3.68 us
    ppermute x1, starting transfers between devices, shards(): f_above = lax.ppermute(f1, 'rows', down)  3.48 us
    pallas_call x1, Pallas kernels, shards(): call(gram_kernel, 'gram', (grid_row(), jax.ShapeDtypeStruct((SUMS, 2, ROW...  3.14 us
    pallas_call x1, Pallas kernels, shards(): call(lambda *refs: finish_kernel(float(points), *refs), 'finish', (jax.Sh...  1.45 us
  transfers between devices with their start and end apart: 5, of which 1 were waited for; matrix products, arithmetic and copies ran while one was open for 0% of the time, Pallas kernels for 27%

profile of v9, /device:TPU:2, one launch (start us, length us, event | category | flops | bytes accessed | tf_op | source)
XLA Modules:
  0.0 71.0 jit_solution(12237645626284786377)
XLA Ops:
  2.6 1.1 %pack.1 = (f32[16,2048]{1,0:T(8,128)S(1)}, f32[16,2048]{1,0:T(8,128)S(1)}, f32[8,128]{1,0:T(8,128)S(1)}) custom-call(s32[32]{0:T(128)} %refs_0_.1, f32[2,4096]{1,0:T(2,128)} %offsets_hbm.1, s32[8,4096]{1,0:T(8,128)} %probes_hbm.1, f32[1,4096]{1,0:T(1,128)} %bitcast.2, f32[1]{0:T(128)S(6)} %copy.9.scale_ref, f32[1]{0:T(128)S(6)} %copy.10.amp_ref, ...), custom_call_target="tpu_custom_call" | custom-call | flops 1048576 | bytes 1048576 | tf_op jit(solution)/shard_map/pack/pallas_call | solution.py:616
  3.6 1.3 %collective-permute-start.1 = (f32[16,2048]{1,0:T(8,128)S(1)}, f32[16,2048]{1,0:T(8,128)S(1)}, u32[]{:S(2)}, u32[]{:S(2)}) collective-permute-start(f32[16,2048]{1,0:T(8,128)S(1)} %get-tuple-element.27.first_ref.refs_1_.b0_ref.refs_3_), channel_id=1, source_target_pairs={{1,0},{2,1},{3,2},{4,3},{5,4},{6,5},{7,6},{8,7},{9,8},{10,9},{11,1... | collective-permute-start | bytes 393224 | tf_op jit(solution)/shard_map/ppermute | solution.py:652
  4.9 4.6 %collective-permute-start = (f32[16,2048]{1,0:T(8,128)S(1)}, f32[16,2048]{1,0:T(8,128)S(1)}, u32[]{:S(2)}, u32[]{:S(2)}) collective-permute-start(f32[16,2048]{1,0:T(8,128)S(1)} %get-tuple-element.26.second_ref.refs_1_.b1_ref.b_ref.refs_4_), channel_id=1, source_target_pairs={{0,1},{1,2},{2,3},{3,4},{4,5},{5,6},{6,7},{7,8},{8,9},{9,10},{10,1... | collective-permute-start | bytes 393224 | tf_op jit(solution)/shard_map/ppermute | solution.py:651
  9.5 8.7 %inner.1 = (bf16[2,16,768,128]{3,2,1,0:T(8,128)(2,1)S(1)}, bf16[2,16,768,128]{3,2,1,0:T(8,128)(2,1)S(1)}, bf16[16,4608]{1,0:T(8,128)(2,1)}, bf16[16,4608]{1,0:T(...) custom-call(f32[16,2048]{1,0:T(8,128)S(1)} %get-tuple-element.27.first_ref.refs_1_.b0_ref.refs_3_, ...), custom_call_target="tpu_custom_call" | custom-call | flops 1073741824 | bytes 1048576 | tf_op jit(solution)/shard_map/inner/pallas_call | solution.py:653
  18.2 0.0 collective-permute-done.1.refs_0_
  18.2 2.9 %outer1.1 = (bf16[1,16,768,128]{3,2,1,0:T(8,128)(2,1)S(1)}, f32[16,2048]{1,0:T(8,128)S(1)}, bf16[32,4608]{1,0:T(8,128)(2,1)S(1)}, f32[16,2048]{1,0:T(8,128)S(1)}) custom-call(f32[16,2048]{1,0:T(8,128)S(1)} %collective-permute-done.1.refs_0_, f32[16,2048]{1,0:T(8,128)S(1)} %get-tuple-element.26.second_ref.refs_1_.b1_ref.b_ref.refs_4_, ...), custom_call_target="tpu_custom_call" | custom-call | flops 1073741824 | bytes 1048576 | tf_op jit(solution)/shard_map/outer1/pallas_call | solution.py:642
  21.0 3.5 %collective-permute-start.3 = (f32[16,2048]{1,0:T(8,128)S(1)}, f32[16,2048]{1,0:T(8,128)S(1)}, u32[]{:S(2)}, u32[]{:S(2)}) collective-permute-start(f32[16,2048]{1,0:T(8,128)S(1)} %get-tuple-element.34.f1_ref.f_ref.refs_6_), channel_id=1, source_target_pairs={{0,1},{1,2},{2,3},{3,4},{4,5},{5,6},{6,7},{7,8},{8,9},{9,10},{10,1... | collective-permute-start | bytes 393224 | tf_op jit(solution)/shard_map/ppermute | solution.py:662
  24.5 0.0 collective-permute-done.refs_0_
  24.5 3.2 %outer0.1 = (bf16[1,16,768,128]{3,2,1,0:T(8,128)(2,1)S(1)}, f32[16,2048]{1,0:T(8,128)S(1)}, bf16[32,4608]{1,0:T(8,128)(2,1)S(1)}, f32[16,2048]{1,0:T(8,128)S(1)}, f32[16,2048]{1,0:T(8,128)S(1)}) custom-call(f32[16,2048]{1,0:T(8,128)S(1)} %collective-permute-done.refs_0_, f32[16,2048]{1,0:T(8,128)S(1)} %get-tuple-element.27.first_ref.refs_1_.b0_ref.refs_3_, ...), custom_call_target="tpu_custom_call" | custom-call | flops 1073741824 | bytes 1048576 | tf_op jit(solution)/shard_map/outer0/pallas_call | solution.py:642
  27.7 1.3 %collective-permute-start.2 = (f32[16,2048]{1,0:T(8,128)S(1)}, f32[16,2048]{1,0:T(8,128)S(1)}, u32[]{:S(2)}, u32[]{:S(2)}) collective-permute-start(f32[16,2048]{1,0:T(8,128)S(1)} %get-tuple-element.33.own_ref.f0_ref.refs_5_), channel_id=1, source_target_pairs={{1,0},{2,1},{3,2},{4,3},{5,4},{6,5},{7,6},{8,7},{9,8},{10,9},{11,1... | collective-permute-start | bytes 393224 | tf_op jit(solution)/shard_map/ppermute | solution.py:664
  29.0 0.0 collective-permute-done.3.other_ref
  29.0 1.0 %product.1 = (f32[16,2048]{1,0:T(8,128)S(1)}, bf16[32,4608]{1,0:T(8,128)(2,1)S(1)}) custom-call(f32[16,2048]{1,0:T(8,128)S(1)} %collective-permute-done.3.other_ref, f32[16,2048]{1,0:T(8,128)S(1)} %get-tuple-element.33.own_ref.f0_ref.refs_5_, f32[16,2048]{1,0:T(8,128)S(1)} %get-tuple-element.35.ahead_ref, ...), custom_call_target="tpu_custom_call" | custom-call | flops 536870912 | bytes 1048576 | tf_op jit(solution)/shard_map/product/pallas_call | solution.py:665
  30.0 1.3 %collective-permute-start.4 = (f32[16,2048]{1,0:T(8,128)S(1)}, f32[16,2048]{1,0:T(8,128)S(1)}, u32[]{:S(2)}, u32[]{:S(2)}) collective-permute-start(f32[16,2048]{1,0:T(8,128)S(1)} %get-tuple-element.39.g0_ref.refs_7_), channel_id=1, source_target_pairs={{1,0},{2,1},{3,2},{4,3},{5,4},{6,5},{7,6},{8,7},{9,8},{10,9},{11,1... | collective-permute-start | bytes 393224 | tf_op jit(solution)/shard_map/ppermute | solution.py:673
  31.3 3.7 %collective-permute-done.2.below_ref = f32[16,2048]{1,0:T(8,128)S(1)} collective-permute-done((f32[16,2048]{1,0:T(8,128)S(1)}, f32[16,2048]{1,0:T(8,128)S(1)}, u32[]{:S(2)}, u32[]{:S(2)}) %collective-permute-start.2) | collective-permute-done | bytes 131104 | tf_op jit(solution)/shard_map/ppermute | solution.py:664
  35.0 0.0 copy-start
  35.0 3.1 %gram.1 = (f32[16,2048]{1,0:T(8,128)S(1)}, f32[9,2,16,128]{3,2,1,0:T(8,128)S(1)}) custom-call(f32[16,2048]{1,0:T(8,128)S(1)} %collective-permute-done.2.below_ref, f32[16,2048]{1,0:T(8,128)S(1)} %get-tuple-element.27.first_ref.refs_1_.b0_ref.refs_3_, f32[16,2048]{1,0:T(8,128)S(1)} %get-tuple-element.26.second_ref.refs_1_.b1_ref.b_ref.refs_4_, ...), custom_call_target="tpu_custom_call" | custom-call | flops 536870912 | bytes 1048576 | tf_op jit(solution)/shard_map/gram/pallas_call | solution.py:674
  38.2 0.0 collective-permute-done.4.below_ref
  38.2 1.1 %moment.1 = f32[64,1,256]{2,1,0:T(1,128)S(1)} custom-call(f32[9,2,16,128]{3,2,1,0:T(8,128)S(1)} %get-tuple-element.44.sums_ref, f32[16,2048]{1,0:T(8,128)S(1)} %collective-permute-done.4.below_ref, f32[16,2048]{1,0:T(8,128)S(1)} %get-tuple-element.26.second_ref.refs_1_.b1_ref.b_ref.refs_4_, f32[16,2048]{1,0:T(8,128)S(1)} %get-tuple-element.34.f1_ref.f_ref.refs_6_, ...), custom_call_target="tpu_custom_call" | custom-call | flops 536870912 | bytes 1048576 | tf_op jit(solution)/shard_map/moment/pallas_call | solution.py:682
  39.3 30.3 %all_to_all.5.refs_2_ = f32[64,1,256]{2,1,0:T(1,128)S(1)} all-to-all(f32[64,1,256]{2,1,0:T(1,128)S(1)} %moment.1), channel_id=1, replica_groups=mesh['hyp'=8,'rows'=64] {'rows'}, dimensions={0} | all-to-all | bytes 131072 | tf_op jit(solution)/shard_map/all_to_all | solution.py:690
  69.5 0.0 copy-done
  69.5 1.5 %finish.1 = (f32[9,4096]{1,0:T(8,128)}, f32[1,9]{1,0:T(1,128)}) custom-call(s32[32]{0:T(128)S(1)} %copy-done, f32[8,128]{1,0:T(8,128)S(1)} %get-tuple-element.25.consts_ref.refs_2_.refs_1_, f32[64,1,256]{2,1,0:T(1,128)S(1)} %all_to_all.5.refs_2_, f32[16,2048]{1,0:T(8,128)S(1)} %get-tuple-element.27.first_ref.refs_1_.b0_ref.refs_3_, ...), custom_call_target="tpu_custom_call" | custom-call | flops 1048576 | bytes 1048576 | tf_op jit(solution)/shard_map/finish/pallas_call | solution.py:692
Async XLA Ops:
  3.6 14.5 %collective-permute-start.1 = (f32[16,2048]{1,0:T(8,128)S(1)}, f32[16,2048]{1,0:T(8,128)S(1)}, u32[]{:S(2)}, u32[]{:S(2)}) collective-permute-start(f32[16,2048]{1,0:T(8,128)S(1)} %get-tuple-element.27.first_ref.refs_1_.b0_ref.refs_3_), channel_id=1, source_target_pairs={{1,0},{2,1},{3,2},{4,3},{5,4},{6,5},{7,6},{8,7},{9,8},{10,9},{11,1... | collective-permute-start | bytes 393224 | tf_op jit(solution)/shard_map/ppermute | solution.py:652
  4.9 19.6 %collective-permute-start = (f32[16,2048]{1,0:T(8,128)S(1)}, f32[16,2048]{1,0:T(8,128)S(1)}, u32[]{:S(2)}, u32[]{:S(2)}) collective-permute-start(f32[16,2048]{1,0:T(8,128)S(1)} %get-tuple-element.26.second_ref.refs_1_.b1_ref.b_ref.refs_4_), channel_id=1, source_target_pairs={{0,1},{1,2},{2,3},{3,4},{4,5},{5,6},{6,7},{7,8},{8,9},{9,10},{10,1... | collective-permute-start | bytes 393224 | tf_op jit(solution)/shard_map/ppermute | solution.py:651
  21.0 8.0 %collective-permute-start.3 = (f32[16,2048]{1,0:T(8,128)S(1)}, f32[16,2048]{1,0:T(8,128)S(1)}, u32[]{:S(2)}, u32[]{:S(2)}) collective-permute-start(f32[16,2048]{1,0:T(8,128)S(1)} %get-tuple-element.34.f1_ref.f_ref.refs_6_), channel_id=1, source_target_pairs={{0,1},{1,2},{2,3},{3,4},{4,5},{5,6},{6,7},{7,8},{8,9},{9,10},{10,1... | collective-permute-start | bytes 393224 | tf_op jit(solution)/shard_map/ppermute | solution.py:662
  27.7 7.3 %collective-permute-start.2 = (f32[16,2048]{1,0:T(8,128)S(1)}, f32[16,2048]{1,0:T(8,128)S(1)}, u32[]{:S(2)}, u32[]{:S(2)}) collective-permute-start(f32[16,2048]{1,0:T(8,128)S(1)} %get-tuple-element.33.own_ref.f0_ref.refs_5_), channel_id=1, source_target_pairs={{1,0},{2,1},{3,2},{4,3},{5,4},{6,5},{7,6},{8,7},{9,8},{10,9},{11,1... | collective-permute-start | bytes 393224 | tf_op jit(solution)/shard_map/ppermute | solution.py:664
  30.0 8.1 %collective-permute-start.4 = (f32[16,2048]{1,0:T(8,128)S(1)}, f32[16,2048]{1,0:T(8,128)S(1)}, u32[]{:S(2)}, u32[]{:S(2)}) collective-permute-start(f32[16,2048]{1,0:T(8,128)S(1)} %get-tuple-element.39.g0_ref.refs_7_), channel_id=1, source_target_pairs={{1,0},{2,1},{3,2},{4,3},{5,4},{6,5},{7,6},{8,7},{9,8},{10,9},{11,1... | collective-permute-start | bytes 393224 | tf_op jit(solution)/shard_map/ppermute | solution.py:673
  35.0 34.5 %copy-start = (s32[32]{0:T(128)S(1)}, s32[32]{0:T(128)}, u32[]{:S(2)}) copy-start(s32[32]{0:T(128)} %refs_0_.1) | copy-start | bytes 388

commit v10 on v9

--- a/solution.py
+++ b/solution.py
@@ -366,33 +366,21 @@
 
 
 def inner_kernel(
-    first_ref,
-    second_ref,
-    consts_ref,
-    left_ref,
-    right_ref,
-    spread0_ref,
-    spread1_ref,
-    part0_ref,
-    part1_ref,
-    feats_ref,
+    first_ref, second_ref, consts_ref, left_ref, right_ref, spread0_ref, spread1_ref, feats_ref
 ):
     rows = feature_rows()
-
-    def first_part(tile):
-        for slot, part_ref in enumerate((part0_ref, part1_ref)):
-            part_ref[:, lanes(tile)] = joined(banded(spread0_ref, left_ref, slot, tile))
-
     for slot, (own_ref, weights_ref, spread_ref) in enumerate(
         ((first_ref, left_ref, spread0_ref), (second_ref, right_ref, spread1_ref))
     ):
         source_features(own_ref, constant(consts_ref, FACTOR), rows, feats_ref)
         targets = ((first_ref, slot, weights_ref, 0), (second_ref, slot - 1, weights_ref, 1))
-        fill_weights(targets, feats_ref, consts_ref, rows, first_part if slot else None)
+        fill_weights(targets, feats_ref, consts_ref, rows)
         spread_sides(own_ref, spread_ref)
 
 
-def outer_kernel(slot, other_ref, own_ref, consts_ref, part_ref, right_ref, spread1_ref, *more):
+def outer_kernel(
+    slot, other_ref, own_ref, consts_ref, left_ref, right_ref, spread0_ref, spread1_ref, *more
+):
     if slot:
         weights_ref, out_ref, out_spread_ref, beside_ref, feats_ref, spread_ref = more
         ahead, beside = (), beside_ref
@@ -405,8 +393,8 @@
 
     def own_part(tile):
         here = lanes(tile)
-        own = noise * own_ref[:, here] + part_ref[:, here]
-        out_ref[:, here] = own + joined(banded(spread1_ref, right_ref, slot, tile))
+        both = banded(spread0_ref, left_ref, slot, tile) + banded(spread1_ref, right_ref, slot, tile)
+        out_ref[:, here] = noise * own_ref[:, here] + joined(both)
         for i, ahead_ref in enumerate(ahead):
             ahead_ref[:, here] = joined(banded(f1_ref, right_ref, i, tile))
 
@@ -638,29 +626,29 @@
         noise,
     )
 
-    def outer(slot, other, own, part, *ahead):
+    def outer(slot, other, own, *ahead):
         return call(
             lambda *refs: outer_kernel(slot, *refs),
             f"outer{slot}",
             (weight_rows(1), grid_row(), spread_row()) + (pltpu.VMEM((ROWS, WIDE), F32),) * (2 - slot),
-            [VMEM] * (7 - slot),
+            [VMEM] * (8 - slot),
             [feature_tiles(), spread_row(ROWS)],
             flops=1 << 30,
-        )(other, own, consts, part, right, b1_spread, *ahead)
+        )(other, own, consts, left, right, b0_spread, b1_spread, *ahead)
 
     above = lax.ppermute(second, "rows", down)
     below = lax.ppermute(first, "rows", up)
-    left, right, _, b1_spread, part0, part1 = call(
+    left, right, b0_spread, b1_spread = call(
         inner_kernel,
         "inner",
-        (weight_rows(2), weight_rows(2), spread_row(ROWS), spread_row(ROWS), *(pltpu.VMEM((ROWS, WIDE), F32),) * 2),
+        (weight_rows(2), weight_rows(2), spread_row(ROWS), spread_row(ROWS)),
         [VMEM] * 3,
         [feature_tiles()],
         flops=1 << 30,
     )(first, second, consts)
-    under, f1, f1_spread, b_beside = outer(1, below, second, part1)
+    under, f1, f1_spread, b_beside = outer(1, below, second)
     f_above = lax.ppermute(f1, "rows", down)
-    over, f0, f0_spread, ahead0, ahead1 = outer(0, above, first, part0, f1_spread)
+    over, f0, f0_spread, ahead0, ahead1 = outer(0, above, first, f1_spread)
     f_below = lax.ppermute(f0, "rows", up)
     g0, g0_spread = call(
         product_kernel,

time: 71.3 us -> 70.8 us (level)
    pallas_call x1, Pallas kernels: 8.66 us -> 7.78 us  [shards(): call(inner_kernel, 'inner', (weight_rows(2), weight_rows(2), spread_row(R...]
  transfers between devices with their start and end apart: 5 -> 5, of which waited for: 1 -> 1; matrix products, arithmetic and copies ran while one was open for 0% -> 0% of each run, Pallas kernels for 27% -> 26%
where the time goes in v10:
time: 70.8 us; the launch traced here: 70.4 us
  blocking collectives  30.2 us (43%)
  Pallas kernels  21.9 us (31%)
  starting transfers between devices  11.9 us (17%)
  waiting for transfers between devices  3.7 us (5%)
  between operations  2.69 us (4%)
    all_to_all x1, blocking collectives, shards(): lax.all_to_all(parts, 'rows', split_axis=0, concat_axis=0, tiled=True)  30.2 us
    pallas_call x1, Pallas kernels, shards(): call(inner_kernel, 'inner', (weight_rows(2), weight_rows(2), spread_row(R...  7.78 us
    pallas_call x2, Pallas kernels, outer(): call(lambda *refs: outer_kernel(slot, *refs), f'outer{slot}', (weight_row...  6.36 us
    ppermute x1, starting transfers between devices, shards(): above = lax.ppermute(second, 'rows', down)  4.55 us
    ppermute x1, waiting for transfers between devices, shards(): f_below = lax.ppermute(f0, 'rows', up)  3.69 us
    ppermute x1, starting transfers between devices, shards(): f_above = lax.ppermute(f1, 'rows', down)  3.5 us
    pallas_call x1, Pallas kernels, shards(): call(gram_kernel, 'gram', (grid_row(), jax.ShapeDtypeStruct((SUMS, 2, ROW...  3.13 us
    pallas_call x1, Pallas kernels, shards(): call(lambda *refs: finish_kernel(float(points), *refs), 'finish', (jax.Sh...  1.45 us
  transfers between devices with their start and end apart: 5, of which 1 were waited for; matrix products, arithmetic and copies ran while one was open for 0% of the time, Pallas kernels for 26%

profile of v10, /device:TPU:2, one launch (start us, length us, event | category | flops | bytes accessed | tf_op | source)
XLA Modules:
  0.0 70.4 jit_solution(7436635083080693041)
XLA Ops:
  2.6 1.1 %pack.1 = (f32[16,2048]{1,0:T(8,128)S(1)}, f32[16,2048]{1,0:T(8,128)S(1)}, f32[8,128]{1,0:T(8,128)S(1)}) custom-call(s32[32]{0:T(128)} %refs_0_.1, f32[2,4096]{1,0:T(2,128)} %offsets_hbm.1, s32[8,4096]{1,0:T(8,128)} %probes_hbm.1, f32[1,4096]{1,0:T(1,128)} %bitcast.2, f32[1]{0:T(128)S(6)} %copy.9.scale_ref, f32[1]{0:T(128)S(6)} %copy.10.amp_ref, ...), custom_call_target="tpu_custom_call" | custom-call | flops 1048576 | bytes 1048576 | tf_op jit(solution)/shard_map/pack/pallas_call | solution.py:604
  3.6 1.3 %collective-permute-start.1 = (f32[16,2048]{1,0:T(8,128)S(1)}, f32[16,2048]{1,0:T(8,128)S(1)}, u32[]{:S(2)}, u32[]{:S(2)}) collective-permute-start(f32[16,2048]{1,0:T(8,128)S(1)} %get-tuple-element.26.first_ref.refs_1_.b0_ref.refs_3_), channel_id=1, source_target_pairs={{1,0},{2,1},{3,2},{4,3},{5,4},{6,5},{7,6},{8,7},{9,8},{10,9},{11,1... | collective-permute-start | bytes 393224 | tf_op jit(solution)/shard_map/ppermute | solution.py:640
  4.9 4.6 %collective-permute-start = (f32[16,2048]{1,0:T(8,128)S(1)}, f32[16,2048]{1,0:T(8,128)S(1)}, u32[]{:S(2)}, u32[]{:S(2)}) collective-permute-start(f32[16,2048]{1,0:T(8,128)S(1)} %get-tuple-element.25.second_ref.refs_1_.b1_ref.b_ref.refs_4_), channel_id=1, source_target_pairs={{0,1},{1,2},{2,3},{3,4},{4,5},{5,6},{6,7},{7,8},{8,9},{9,10},{10,1... | collective-permute-start | bytes 393224 | tf_op jit(solution)/shard_map/ppermute | solution.py:639
  9.5 7.8 %inner.1 = (bf16[2,16,768,128]{3,2,1,0:T(8,128)(2,1)S(1)}, bf16[2,16,768,128]{3,2,1,0:T(8,128)(2,1)S(1)}, bf16[16,4608]{1,0:T(8,128)(2,1)S(1)}, bf16[16,4608]{1,0:T(8,128)(2,1)S(1)}) custom-call(f32[16,2048]{1,0:T(8,128)S(1)} %get-tuple-element.26.first_ref.refs_1_.b0_ref.refs_3_, f32[16,2048]{1,0:T(8,128)S(1)} %get-tuple-element.25.second_ref.refs_1_.b1_ref.b_ref.refs_4_, ...), custom_call_target="tpu_custom_call" | custom-call | flops 1073741824 | bytes 1048576 | tf_op jit(solution)/shard_map/inner/pallas_call | solution.py:641
  17.3 0.0 collective-permute-done.1.refs_0_
  17.3 3.0 %outer1.1 = (bf16[1,16,768,128]{3,2,1,0:T(8,128)(2,1)S(1)}, f32[16,2048]{1,0:T(8,128)S(1)}, bf16[32,4608]{1,0:T(8,128)(2,1)S(1)}, f32[16,2048]{1,0:T(8,128)S(1)}) custom-call(f32[16,2048]{1,0:T(8,128)S(1)} %collective-permute-done.1.refs_0_, f32[16,2048]{1,0:T(8,128)S(1)} %get-tuple-element.25.second_ref.refs_1_.b1_ref.b_ref.refs_4_, ...), custom_call_target="tpu_custom_call" | custom-call | flops 1073741824 | bytes 1048576 | tf_op jit(solution)/shard_map/outer1/pallas_call | solution.py:630
  20.3 3.5 %collective-permute-start.3 = (f32[16,2048]{1,0:T(8,128)S(1)}, f32[16,2048]{1,0:T(8,128)S(1)}, u32[]{:S(2)}, u32[]{:S(2)}) collective-permute-start(f32[16,2048]{1,0:T(8,128)S(1)} %get-tuple-element.33.f1_ref.f_ref.refs_6_), channel_id=1, source_target_pairs={{0,1},{1,2},{2,3},{3,4},{4,5},{5,6},{6,7},{7,8},{8,9},{9,10},{10,1... | collective-permute-start | bytes 393224 | tf_op jit(solution)/shard_map/ppermute | solution.py:650
  23.8 0.0 collective-permute-done.refs_0_
  23.8 3.3 %outer0.1 = (bf16[1,16,768,128]{3,2,1,0:T(8,128)(2,1)S(1)}, f32[16,2048]{1,0:T(8,128)S(1)}, bf16[32,4608]{1,0:T(8,128)(2,1)S(1)}, f32[16,2048]{1,0:T(8,128)S(1)}, f32[16,2048]{1,0:T(8,128)S(1)}) custom-call(f32[16,2048]{1,0:T(8,128)S(1)} %collective-permute-done.refs_0_, f32[16,2048]{1,0:T(8,128)S(1)} %get-tuple-element.26.first_ref.refs_1_.b0_ref.refs_3_, ...), custom_call_target="tpu_custom_call" | custom-call | flops 1073741824 | bytes 1048576 | tf_op jit(solution)/shard_map/outer0/pallas_call | solution.py:630
  27.2 1.3 %collective-permute-start.2 = (f32[16,2048]{1,0:T(8,128)S(1)}, f32[16,2048]{1,0:T(8,128)S(1)}, u32[]{:S(2)}, u32[]{:S(2)}) collective-permute-start(f32[16,2048]{1,0:T(8,128)S(1)} %get-tuple-element.32.own_ref.f0_ref.refs_5_), channel_id=1, source_target_pairs={{1,0},{2,1},{3,2},{4,3},{5,4},{6,5},{7,6},{8,7},{9,8},{10,9},{11,1... | collective-permute-start | bytes 393224 | tf_op jit(solution)/shard_map/ppermute | solution.py:652
  28.5 0.0 collective-permute-done.3.other_ref
  28.5 1.0 %product.1 = (f32[16,2048]{1,0:T(8,128)S(1)}, bf16[32,4608]{1,0:T(8,128)(2,1)S(1)}) custom-call(f32[16,2048]{1,0:T(8,128)S(1)} %collective-permute-done.3.other_ref, f32[16,2048]{1,0:T(8,128)S(1)} %get-tuple-element.32.own_ref.f0_ref.refs_5_, f32[16,2048]{1,0:T(8,128)S(1)} %get-tuple-element.34.ahead_ref, ...), custom_call_target="tpu_custom_call" | custom-call | flops 536870912 | bytes 1048576 | tf_op jit(solution)/shard_map/product/pallas_call | solution.py:653
  29.5 1.3 %collective-permute-start.4 = (f32[16,2048]{1,0:T(8,128)S(1)}, f32[16,2048]{1,0:T(8,128)S(1)}, u32[]{:S(2)}, u32[]{:S(2)}) collective-permute-start(f32[16,2048]{1,0:T(8,128)S(1)} %get-tuple-element.37.g0_ref.refs_7_), channel_id=1, source_target_pairs={{1,0},{2,1},{3,2},{4,3},{5,4},{6,5},{7,6},{8,7},{9,8},{10,9},{11,1... | collective-permute-start | bytes 393224 | tf_op jit(solution)/shard_map/ppermute | solution.py:661
  30.8 3.7 %collective-permute-done.2.below_ref = f32[16,2048]{1,0:T(8,128)S(1)} collective-permute-done((f32[16,2048]{1,0:T(8,128)S(1)}, f32[16,2048]{1,0:T(8,128)S(1)}, u32[]{:S(2)}, u32[]{:S(2)}) %collective-permute-start.2) | collective-permute-done | bytes 131104 | tf_op jit(solution)/shard_map/ppermute | solution.py:652
  34.5 0.0 copy-start
  34.5 3.1 %gram.1 = (f32[16,2048]{1,0:T(8,128)S(1)}, f32[9,2,16,128]{3,2,1,0:T(8,128)S(1)}) custom-call(f32[16,2048]{1,0:T(8,128)S(1)} %collective-permute-done.2.below_ref, f32[16,2048]{1,0:T(8,128)S(1)} %get-tuple-element.26.first_ref.refs_1_.b0_ref.refs_3_, f32[16,2048]{1,0:T(8,128)S(1)} %get-tuple-element.25.second_ref.refs_1_.b1_ref.b_ref.refs_4_, ...), custom_call_target="tpu_custom_call" | custom-call | flops 536870912 | bytes 1048576 | tf_op jit(solution)/shard_map/gram/pallas_call | solution.py:662
  37.6 0.0 collective-permute-done.4.below_ref
  37.6 1.1 %moment.1 = f32[64,1,256]{2,1,0:T(1,128)S(1)} custom-call(f32[9,2,16,128]{3,2,1,0:T(8,128)S(1)} %get-tuple-element.42.sums_ref, f32[16,2048]{1,0:T(8,128)S(1)} %collective-permute-done.4.below_ref, f32[16,2048]{1,0:T(8,128)S(1)} %get-tuple-element.25.second_ref.refs_1_.b1_ref.b_ref.refs_4_, f32[16,2048]{1,0:T(8,128)S(1)} %get-tuple-element.33.f1_ref.f_ref.refs_6_, ...), custom_call_target="tpu_custom_call" | custom-call | flops 536870912 | bytes 1048576 | tf_op jit(solution)/shard_map/moment/pallas_call | solution.py:670
  38.7 30.2 %all_to_all.5.refs_2_ = f32[64,1,256]{2,1,0:T(1,128)S(1)} all-to-all(f32[64,1,256]{2,1,0:T(1,128)S(1)} %moment.1), channel_id=1, replica_groups=mesh['hyp'=8,'rows'=64] {'rows'}, dimensions={0} | all-to-all | bytes 131072 | tf_op jit(solution)/shard_map/all_to_all | solution.py:678
  69.0 0.0 copy-done
  69.0 1.5 %finish.1 = (f32[9,4096]{1,0:T(8,128)}, f32[1,9]{1,0:T(1,128)}) custom-call(s32[32]{0:T(128)S(1)} %copy-done, f32[8,128]{1,0:T(8,128)S(1)} %get-tuple-element.24.consts_ref.refs_2_.refs_1_, f32[64,1,256]{2,1,0:T(1,128)S(1)} %all_to_all.5.refs_2_, f32[16,2048]{1,0:T(8,128)S(1)} %get-tuple-element.26.first_ref.refs_1_.b0_ref.refs_3_, ...), custom_call_target="tpu_custom_call" | custom-call | flops 1048576 | bytes 1048576 | tf_op jit(solution)/shard_map/finish/pallas_call | solution.py:680
Async XLA Ops:
  3.6 13.7 %collective-permute-start.1 = (f32[16,2048]{1,0:T(8,128)S(1)}, f32[16,2048]{1,0:T(8,128)S(1)}, u32[]{:S(2)}, u32[]{:S(2)}) collective-permute-start(f32[16,2048]{1,0:T(8,128)S(1)} %get-tuple-element.26.first_ref.refs_1_.b0_ref.refs_3_), channel_id=1, source_target_pairs={{1,0},{2,1},{3,2},{4,3},{5,4},{6,5},{7,6},{8,7},{9,8},{10,9},{11,1... | collective-permute-start | bytes 393224 | tf_op jit(solution)/shard_map/ppermute | solution.py:640
  4.9 18.9 %collective-permute-start = (f32[16,2048]{1,0:T(8,128)S(1)}, f32[16,2048]{1,0:T(8,128)S(1)}, u32[]{:S(2)}, u32[]{:S(2)}) collective-permute-start(f32[16,2048]{1,0:T(8,128)S(1)} %get-tuple-element.25.second_ref.refs_1_.b1_ref.b_ref.refs_4_), channel_id=1, source_target_pairs={{0,1},{1,2},{2,3},{3,4},{4,5},{5,6},{6,7},{7,8},{8,9},{9,10},{10,1... | collective-permute-start | bytes 393224 | tf_op jit(solution)/shard_map/ppermute | solution.py:639
  20.3 8.2 %collective-permute-start.3 = (f32[16,2048]{1,0:T(8,128)S(1)}, f32[16,2048]{1,0:T(8,128)S(1)}, u32[]{:S(2)}, u32[]{:S(2)}) collective-permute-start(f32[16,2048]{1,0:T(8,128)S(1)} %get-tuple-element.33.f1_ref.f_ref.refs_6_), channel_id=1, source_target_pairs={{0,1},{1,2},{2,3},{3,4},{4,5},{5,6},{6,7},{7,8},{8,9},{9,10},{10,1... | collective-permute-start | bytes 393224 | tf_op jit(solution)/shard_map/ppermute | solution.py:650
  27.2 7.3 %collective-permute-start.2 = (f32[16,2048]{1,0:T(8,128)S(1)}, f32[16,2048]{1,0:T(8,128)S(1)}, u32[]{:S(2)}, u32[]{:S(2)}) collective-permute-start(f32[16,2048]{1,0:T(8,128)S(1)} %get-tuple-element.32.own_ref.f0_ref.refs_5_), channel_id=1, source_target_pairs={{1,0},{2,1},{3,2},{4,3},{5,4},{6,5},{7,6},{8,7},{9,8},{10,9},{11,1... | collective-permute-start | bytes 393224 | tf_op jit(solution)/shard_map/ppermute | solution.py:652
  29.5 8.1 %collective-permute-start.4 = (f32[16,2048]{1,0:T(8,128)S(1)}, f32[16,2048]{1,0:T(8,128)S(1)}, u32[]{:S(2)}, u32[]{:S(2)}) collective-permute-start(f32[16,2048]{1,0:T(8,128)S(1)} %get-tuple-element.37.g0_ref.refs_7_), channel_id=1, source_target_pairs={{1,0},{2,1},{3,2},{4,3},{5,4},{6,5},{7,6},{8,7},{9,8},{10,9},{11,1... | collective-permute-start | bytes 393224 | tf_op jit(solution)/shard_map/ppermute | solution.py:661
  34.5 34.5 %copy-start = (s32[32]{0:T(128)S(1)}, s32[32]{0:T(128)}, u32[]{:S(2)}) copy-start(s32[32]{0:T(128)} %refs_0_.1) | copy-start | bytes 388

commit v11 on v10

--- a/solution.py
+++ b/solution.py
@@ -459,8 +459,8 @@
     def group(g, sums):
         sums = list(sums)
         terms = [zero] * SUMS
-        for j in range(8):
-            tile = g * 8 + j
+        for j in range(GROUP):
+            tile = g * GROUP + j
             here = lanes(tile)
             for half, refs in enumerate(((b0_ref, f0_ref, g0_ref), (b1_ref, f1_ref, g1_ref))):
                 v = [ref[:, here] for ref in refs]
@@ -474,12 +474,12 @@
                 if half == 1:
                     terms[6] = terms[6] + v[2] * b_beside_ref[:, here]
                     terms[7] = terms[7] + v[2] * f_beside_ref[:, here]
-            if j % 2 == 1:
+            if j % 4 == 3:
                 sums = [accumulate(s, t) for s, t in zip(sums, terms)]
                 terms = [zero] * SUMS
         return tuple(sums)
 
-    sums = lax.fori_loop(0, GX // 8, group, ((zero, zero),) * SUMS)
+    sums = lax.fori_loop(0, GX // GROUP, group, ((zero, zero),) * SUMS)
     for k, (high, low) in enumerate(sums):
         sums_ref[k, 0] = high
         sums_ref[k, 1] = low

time: 70.8 us -> 70.8 us (level)
  transfers between devices with their start and end apart: 5 -> 5, of which waited for: 1 -> 1; matrix products, arithmetic and copies ran while one was open for 0% -> 0% of each run, Pallas kernels for 26% -> 25%
where the time goes in v11:
time: 70.8 us; the launch traced here: 70.4 us
  blocking collectives  30.6 us (43%)
  Pallas kernels  21.6 us (31%)
  starting transfers between devices  11.9 us (17%)
  waiting for transfers between devices  3.7 us (5%)
  between operations  2.69 us (4%)
    all_to_all x1, blocking collectives, shards(): lax.all_to_all(parts, 'rows', split_axis=0, concat_axis=0, tiled=True)  30.6 us
    pallas_call x1, Pallas kernels, shards(): call(inner_kernel, 'inner', (weight_rows(2), weight_rows(2), spread_row(R...  7.78 us
    pallas_call x2, Pallas kernels, outer(): call(lambda *refs: outer_kernel(slot, *refs), f'outer{slot}', (weight_row...  6.36 us
    ppermute x1, starting transfers between devices, shards(): above = lax.ppermute(second, 'rows', down)  4.55 us
    ppermute x1, waiting for transfers between devices, shards(): f_below = lax.ppermute(f0, 'rows', up)  3.69 us
    ppermute x1, starting transfers between devices, shards(): f_above = lax.ppermute(f1, 'rows', down)  3.5 us
    pallas_call x1, Pallas kernels, shards(): call(gram_kernel, 'gram', (grid_row(), jax.ShapeDtypeStruct((SUMS, 2, ROW...  2.81 us
    pallas_call x1, Pallas kernels, shards(): call(lambda *refs: finish_kernel(float(points), *refs), 'finish', (jax.Sh...  1.45 us
  transfers between devices with their start and end apart: 5, of which 1 were waited for; matrix products, arithmetic and copies ran while one was open for 0% of the time, Pallas kernels for 25%

profile of v11, /device:TPU:2, one launch (start us, length us, event | category | flops | bytes accessed | tf_op | source)
XLA Modules:
  0.0 70.4 jit_solution(17684817621943515115)
XLA Ops:
  2.6 1.1 %pack.1 = (f32[16,2048]{1,0:T(8,128)S(1)}, f32[16,2048]{1,0:T(8,128)S(1)}, f32[8,128]{1,0:T(8,128)S(1)}) custom-call(s32[32]{0:T(128)} %refs_0_.1, f32[2,4096]{1,0:T(2,128)} %offsets_hbm.1, s32[8,4096]{1,0:T(8,128)} %probes_hbm.1, f32[1,4096]{1,0:T(1,128)} %bitcast.2, f32[1]{0:T(128)S(6)} %copy.9.scale_ref, f32[1]{0:T(128)S(6)} %copy.10.amp_ref, ...), custom_call_target="tpu_custom_call" | custom-call | flops 1048576 | bytes 1048576 | tf_op jit(solution)/shard_map/pack/pallas_call | solution.py:604
  3.6 1.3 %collective-permute-start.1 = (f32[16,2048]{1,0:T(8,128)S(1)}, f32[16,2048]{1,0:T(8,128)S(1)}, u32[]{:S(2)}, u32[]{:S(2)}) collective-permute-start(f32[16,2048]{1,0:T(8,128)S(1)} %get-tuple-element.26.first_ref.refs_1_.b0_ref.refs_3_), channel_id=1, source_target_pairs={{1,0},{2,1},{3,2},{4,3},{5,4},{6,5},{7,6},{8,7},{9,8},{10,9},{11,1... | collective-permute-start | bytes 393224 | tf_op jit(solution)/shard_map/ppermute | solution.py:640
  4.9 4.6 %collective-permute-start = (f32[16,2048]{1,0:T(8,128)S(1)}, f32[16,2048]{1,0:T(8,128)S(1)}, u32[]{:S(2)}, u32[]{:S(2)}) collective-permute-start(f32[16,2048]{1,0:T(8,128)S(1)} %get-tuple-element.25.second_ref.refs_1_.b1_ref.b_ref.refs_4_), channel_id=1, source_target_pairs={{0,1},{1,2},{2,3},{3,4},{4,5},{5,6},{6,7},{7,8},{8,9},{9,10},{10,1... | collective-permute-start | bytes 393224 | tf_op jit(solution)/shard_map/ppermute | solution.py:639
  9.5 7.8 %inner.1 = (bf16[2,16,768,128]{3,2,1,0:T(8,128)(2,1)S(1)}, bf16[2,16,768,128]{3,2,1,0:T(8,128)(2,1)S(1)}, bf16[16,4608]{1,0:T(8,128)(2,1)S(1)}, bf16[16,4608]{1,0:T(8,128)(2,1)S(1)}) custom-call(f32[16,2048]{1,0:T(8,128)S(1)} %get-tuple-element.26.first_ref.refs_1_.b0_ref.refs_3_, f32[16,2048]{1,0:T(8,128)S(1)} %get-tuple-element.25.second_ref.refs_1_.b1_ref.b_ref.refs_4_, ...), custom_call_target="tpu_custom_call" | custom-call | flops 1073741824 | bytes 1048576 | tf_op jit(solution)/shard_map/inner/pallas_call | solution.py:641
  17.3 0.0 collective-permute-done.1.refs_0_
  17.3 3.0 %outer1.1 = (bf16[1,16,768,128]{3,2,1,0:T(8,128)(2,1)S(1)}, f32[16,2048]{1,0:T(8,128)S(1)}, bf16[32,4608]{1,0:T(8,128)(2,1)S(1)}, f32[16,2048]{1,0:T(8,128)S(1)}) custom-call(f32[16,2048]{1,0:T(8,128)S(1)} %collective-permute-done.1.refs_0_, f32[16,2048]{1,0:T(8,128)S(1)} %get-tuple-element.25.second_ref.refs_1_.b1_ref.b_ref.refs_4_, ...), custom_call_target="tpu_custom_call" | custom-call | flops 1073741824 | bytes 1048576 | tf_op jit(solution)/shard_map/outer1/pallas_call | solution.py:630
  20.3 3.5 %collective-permute-start.3 = (f32[16,2048]{1,0:T(8,128)S(1)}, f32[16,2048]{1,0:T(8,128)S(1)}, u32[]{:S(2)}, u32[]{:S(2)}) collective-permute-start(f32[16,2048]{1,0:T(8,128)S(1)} %get-tuple-element.33.f1_ref.f_ref.refs_6_), channel_id=1, source_target_pairs={{0,1},{1,2},{2,3},{3,4},{4,5},{5,6},{6,7},{7,8},{8,9},{9,10},{10,1... | collective-permute-start | bytes 393224 | tf_op jit(solution)/shard_map/ppermute | solution.py:650
  23.8 0.0 collective-permute-done.refs_0_
  23.8 3.3 %outer0.1 = (bf16[1,16,768,128]{3,2,1,0:T(8,128)(2,1)S(1)}, f32[16,2048]{1,0:T(8,128)S(1)}, bf16[32,4608]{1,0:T(8,128)(2,1)S(1)}, f32[16,2048]{1,0:T(8,128)S(1)}, f32[16,2048]{1,0:T(8,128)S(1)}) custom-call(f32[16,2048]{1,0:T(8,128)S(1)} %collective-permute-done.refs_0_, f32[16,2048]{1,0:T(8,128)S(1)} %get-tuple-element.26.first_ref.refs_1_.b0_ref.refs_3_, ...), custom_call_target="tpu_custom_call" | custom-call | flops 1073741824 | bytes 1048576 | tf_op jit(solution)/shard_map/outer0/pallas_call | solution.py:630
  27.2 1.3 %collective-permute-start.2 = (f32[16,2048]{1,0:T(8,128)S(1)}, f32[16,2048]{1,0:T(8,128)S(1)}, u32[]{:S(2)}, u32[]{:S(2)}) collective-permute-start(f32[16,2048]{1,0:T(8,128)S(1)} %get-tuple-element.32.own_ref.f0_ref.refs_5_), channel_id=1, source_target_pairs={{1,0},{2,1},{3,2},{4,3},{5,4},{6,5},{7,6},{8,7},{9,8},{10,9},{11,1... | collective-permute-start | bytes 393224 | tf_op jit(solution)/shard_map/ppermute | solution.py:652
  28.5 0.0 collective-permute-done.3.other_ref
  28.5 1.0 %product.1 = (f32[16,2048]{1,0:T(8,128)S(1)}, bf16[32,4608]{1,0:T(8,128)(2,1)S(1)}) custom-call(f32[16,2048]{1,0:T(8,128)S(1)} %collective-permute-done.3.other_ref, f32[16,2048]{1,0:T(8,128)S(1)} %get-tuple-element.32.own_ref.f0_ref.refs_5_, f32[16,2048]{1,0:T(8,128)S(1)} %get-tuple-element.34.ahead_ref, ...), custom_call_target="tpu_custom_call" | custom-call | flops 536870912 | bytes 1048576 | tf_op jit(solution)/shard_map/product/pallas_call | solution.py:653
  29.5 1.3 %collective-permute-start.4 = (f32[16,2048]{1,0:T(8,128)S(1)}, f32[16,2048]{1,0:T(8,128)S(1)}, u32[]{:S(2)}, u32[]{:S(2)}) collective-permute-start(f32[16,2048]{1,0:T(8,128)S(1)} %get-tuple-element.37.g0_ref.refs_7_), channel_id=1, source_target_pairs={{1,0},{2,1},{3,2},{4,3},{5,4},{6,5},{7,6},{8,7},{9,8},{10,9},{11,1... | collective-permute-start | bytes 393224 | tf_op jit(solution)/shard_map/ppermute | solution.py:661
  30.8 3.7 %collective-permute-done.2.below_ref = f32[16,2048]{1,0:T(8,128)S(1)} collective-permute-done((f32[16,2048]{1,0:T(8,128)S(1)}, f32[16,2048]{1,0:T(8,128)S(1)}, u32[]{:S(2)}, u32[]{:S(2)}) %collective-permute-start.2) | collective-permute-done | bytes 131104 | tf_op jit(solution)/shard_map/ppermute | solution.py:652
  34.5 0.0 copy-start
  34.5 2.8 %gram.1 = (f32[16,2048]{1,0:T(8,128)S(1)}, f32[9,2,16,128]{3,2,1,0:T(8,128)S(1)}) custom-call(f32[16,2048]{1,0:T(8,128)S(1)} %collective-permute-done.2.below_ref, f32[16,2048]{1,0:T(8,128)S(1)} %get-tuple-element.26.first_ref.refs_1_.b0_ref.refs_3_, f32[16,2048]{1,0:T(8,128)S(1)} %get-tuple-element.25.second_ref.refs_1_.b1_ref.b_ref.refs_4_, ...), custom_call_target="tpu_custom_call" | custom-call | flops 536870912 | bytes 1048576 | tf_op jit(solution)/shard_map/gram/pallas_call | solution.py:662
  37.3 0.0 collective-permute-done.4.below_ref
  37.3 1.1 %moment.1 = f32[64,1,256]{2,1,0:T(1,128)S(1)} custom-call(f32[9,2,16,128]{3,2,1,0:T(8,128)S(1)} %get-tuple-element.42.sums_ref, f32[16,2048]{1,0:T(8,128)S(1)} %collective-permute-done.4.below_ref, f32[16,2048]{1,0:T(8,128)S(1)} %get-tuple-element.25.second_ref.refs_1_.b1_ref.b_ref.refs_4_, f32[16,2048]{1,0:T(8,128)S(1)} %get-tuple-element.33.f1_ref.f_ref.refs_6_, ...), custom_call_target="tpu_custom_call" | custom-call | flops 536870912 | bytes 1048576 | tf_op jit(solution)/shard_map/moment/pallas_call | solution.py:670
  38.4 30.6 %all_to_all.5.refs_2_ = f32[64,1,256]{2,1,0:T(1,128)S(1)} all-to-all(f32[64,1,256]{2,1,0:T(1,128)S(1)} %moment.1), channel_id=1, replica_groups=mesh['hyp'=8,'rows'=64] {'rows'}, dimensions={0} | all-to-all | bytes 131072 | tf_op jit(solution)/shard_map/all_to_all | solution.py:678
  69.0 0.0 copy-done
  69.0 1.5 %finish.1 = (f32[9,4096]{1,0:T(8,128)}, f32[1,9]{1,0:T(1,128)}) custom-call(s32[32]{0:T(128)S(1)} %copy-done, f32[8,128]{1,0:T(8,128)S(1)} %get-tuple-element.24.consts_ref.refs_2_.refs_1_, f32[64,1,256]{2,1,0:T(1,128)S(1)} %all_to_all.5.refs_2_, f32[16,2048]{1,0:T(8,128)S(1)} %get-tuple-element.26.first_ref.refs_1_.b0_ref.refs_3_, ...), custom_call_target="tpu_custom_call" | custom-call | flops 1048576 | bytes 1048576 | tf_op jit(solution)/shard_map/finish/pallas_call | solution.py:680
Async XLA Ops:
  3.6 13.7 %collective-permute-start.1 = (f32[16,2048]{1,0:T(8,128)S(1)}, f32[16,2048]{1,0:T(8,128)S(1)}, u32[]{:S(2)}, u32[]{:S(2)}) collective-permute-start(f32[16,2048]{1,0:T(8,128)S(1)} %get-tuple-element.26.first_ref.refs_1_.b0_ref.refs_3_), channel_id=1, source_target_pairs={{1,0},{2,1},{3,2},{4,3},{5,4},{6,5},{7,6},{8,7},{9,8},{10,9},{11,1... | collective-permute-start | bytes 393224 | tf_op jit(solution)/shard_map/ppermute | solution.py:640
  4.9 18.9 %collective-permute-start = (f32[16,2048]{1,0:T(8,128)S(1)}, f32[16,2048]{1,0:T(8,128)S(1)}, u32[]{:S(2)}, u32[]{:S(2)}) collective-permute-start(f32[16,2048]{1,0:T(8,128)S(1)} %get-tuple-element.25.second_ref.refs_1_.b1_ref.b_ref.refs_4_), channel_id=1, source_target_pairs={{0,1},{1,2},{2,3},{3,4},{4,5},{5,6},{6,7},{7,8},{8,9},{9,10},{10,1... | collective-permute-start | bytes 393224 | tf_op jit(solution)/shard_map/ppermute | solution.py:639
  20.3 8.2 %collective-permute-start.3 = (f32[16,2048]{1,0:T(8,128)S(1)}, f32[16,2048]{1,0:T(8,128)S(1)}, u32[]{:S(2)}, u32[]{:S(2)}) collective-permute-start(f32[16,2048]{1,0:T(8,128)S(1)} %get-tuple-element.33.f1_ref.f_ref.refs_6_), channel_id=1, source_target_pairs={{0,1},{1,2},{2,3},{3,4},{4,5},{5,6},{6,7},{7,8},{8,9},{9,10},{10,1... | collective-permute-start | bytes 393224 | tf_op jit(solution)/shard_map/ppermute | solution.py:650
  27.2 7.3 %collective-permute-start.2 = (f32[16,2048]{1,0:T(8,128)S(1)}, f32[16,2048]{1,0:T(8,128)S(1)}, u32[]{:S(2)}, u32[]{:S(2)}) collective-permute-start(f32[16,2048]{1,0:T(8,128)S(1)} %get-tuple-element.32.own_ref.f0_ref.refs_5_), channel_id=1, source_target_pairs={{1,0},{2,1},{3,2},{4,3},{5,4},{6,5},{7,6},{8,7},{9,8},{10,9},{11,1... | collective-permute-start | bytes 393224 | tf_op jit(solution)/shard_map/ppermute | solution.py:652
  29.5 7.8 %collective-permute-start.4 = (f32[16,2048]{1,0:T(8,128)S(1)}, f32[16,2048]{1,0:T(8,128)S(1)}, u32[]{:S(2)}, u32[]{:S(2)}) collective-permute-start(f32[16,2048]{1,0:T(8,128)S(1)} %get-tuple-element.37.g0_ref.refs_7_), channel_id=1, source_target_pairs={{1,0},{2,1},{3,2},{4,3},{5,4},{6,5},{7,6},{8,7},{9,8},{10,9},{11,1... | collective-permute-start | bytes 393224 | tf_op jit(solution)/shard_map/ppermute | solution.py:661
  34.5 34.5 %copy-start = (s32[32]{0:T(128)S(1)}, s32[32]{0:T(128)}, u32[]{:S(2)}) copy-start(s32[32]{0:T(128)} %refs_0_.1) | copy-start | bytes 388
